TPU v7x, 32 devices: a whole 2x2x4 slice. The times are simulated.
32 devices in a mesh: seq: 8 (over z, y), dp: 4 (over x, core).
Axes of the slice: x: 2, y: 2, z: 4, core: 2. Of those that a mesh axis runs over, the one named last changes fastest.
Arguments:
- tokens: bfloat16 [4, 2048, 2048], P('dp', 'seq'), may hold values from -6 to 6
- query_weight: bfloat16 [2048, 2048], P(None, 'seq'), may hold values from -0.125 to 0.125
- key_rows: bfloat16 [4, 2048, 2048], P('dp', 'seq'), may hold values from -6 to 6
- value_rows: bfloat16 [4, 2048, 2048], P('dp', 'seq'), may hold values from -6 to 6
- out_grad: bfloat16 [4, 2048, 2048], P('dp', 'seq'), may hold values from -6 to 6
Outputs:
- attended: bfloat16 [4, 2048, 2048], P('dp', 'seq')
- key_grad: bfloat16 [4, 2048, 2048], P('dp', 'seq')
- value_grad: bfloat16 [4, 2048, 2048], P('dp', 'seq')
- weight_grad: float32 [2048, 2048], P('seq')
All inputs are finite; a program needn't handle non-finite values.
Results may differ from a plain program's by a relative error of at most 0.0058.
Values may be sent and summed in bfloat16 or wider, within the bound.
No kernel may reach another device: no remote copies, remote signals or barrier semaphores. Data moves between devices by JAX's collectives and lax.ppermute only.
A program may use at most 320 MiB of HBM per device.

v0:
```python
import math

import jax
import jax.numpy as jnp
from jax import lax
from jax.sharding import PartitionSpec as P

DH = 128


def carried_in(value, axis, join, neutral, backward):
    count, mine = (lax.axis_size(axis), lax.axis_index(axis))
    pieces = lax.all_gather(value, axis)
    if backward:
        pieces = pieces[::-1]
        mine = count - 1 - mine
    total = jnp.full_like(value, 0) + jnp.asarray(neutral, value.dtype)

    def step(position, total):
        longer = join(total, pieces[position])
        return jnp.where(position < mine, longer, total)

    return lax.fori_loop(0, count - 1, step, total)


def pair_sum(earlier, later):
    return jax.tree.map(jnp.add, earlier, later)


def body(tokens, query_weight, key_rows, value_rows, out_grad):
    row_count = tokens.shape[1]
    hidden_width = key_rows.shape[2]
    head_count = hidden_width // DH
    seq_count = lax.axis_size("seq")
    factor = 1.0 / math.sqrt(DH * row_count * seq_count)
    local_tokens = tokens[0]
    query_rows = jnp.dot(
        local_tokens,
        lax.all_gather(query_weight, "seq", axis=1, tiled=True),
        preferred_element_type=jnp.float32,
    ).astype(jnp.bfloat16)
    query_heads = query_rows.reshape(row_count, head_count, DH)
    key_heads = key_rows[0].reshape(row_count, head_count, DH)
    value_heads = value_rows[0].reshape(row_count, head_count, DH)
    grad_heads = out_grad[0].reshape(row_count, head_count, DH)
    block_kv = jnp.einsum(
        "rhd,rhe->hde", key_heads, value_heads, preferred_element_type=jnp.float32
    )
    block_qg = jnp.einsum(
        "rhd,rhe->hde", query_heads, grad_heads, preferred_element_type=jnp.float32
    )
    zero_state = jnp.zeros_like(block_kv)
    prefix_state = carried_in(block_kv, "seq", pair_sum, zero_state, False)
    suffix_state = carried_in(block_qg, "seq", pair_sum, zero_state, True)
    prefix_half = prefix_state.astype(jnp.bfloat16)
    suffix_half = suffix_state.astype(jnp.bfloat16)
    lower_mask = (
        lax.broadcasted_iota(jnp.int32, (row_count, row_count), 0)
        >= lax.broadcasted_iota(jnp.int32, (row_count, row_count), 1)
    )[None]
    key_scores = jnp.where(
        lower_mask,
        factor
        * jnp.einsum("ihd,jhd->hij", query_heads, key_heads, preferred_element_type=jnp.float32),
        0.0,
    ).astype(jnp.bfloat16)
    grad_scores = jnp.where(
        lower_mask,
        factor
        * jnp.einsum("ihe,jhe->hij", grad_heads, value_heads, preferred_element_type=jnp.float32),
        0.0,
    ).astype(jnp.bfloat16)
    attended = jnp.einsum(
        "hij,jhe->ihe", key_scores, value_heads, preferred_element_type=jnp.float32
    ) + factor * jnp.einsum(
        "ihd,hde->ihe", query_heads, prefix_half, preferred_element_type=jnp.float32
    )
    query_grad = jnp.einsum(
        "hij,jhd->ihd", grad_scores, key_heads, preferred_element_type=jnp.float32
    ) + factor * jnp.einsum(
        "ihe,hde->ihd", grad_heads, prefix_half, preferred_element_type=jnp.float32
    )
    key_grad = jnp.einsum(
        "hij,ihd->jhd", grad_scores, query_heads, preferred_element_type=jnp.float32
    ) + factor * jnp.einsum(
        "jhe,hde->jhd", value_heads, suffix_half, preferred_element_type=jnp.float32
    )
    value_grad = jnp.einsum(
        "hij,ihe->jhe", key_scores, grad_heads, preferred_element_type=jnp.float32
    ) + factor * jnp.einsum(
        "jhd,hde->jhe", key_heads, suffix_half, preferred_element_type=jnp.float32
    )
    attended = attended.reshape(1, row_count, hidden_width).astype(jnp.bfloat16)
    query_grad = query_grad.reshape(row_count, hidden_width).astype(jnp.bfloat16)
    key_grad = key_grad.reshape(1, row_count, hidden_width).astype(jnp.bfloat16)
    value_grad = value_grad.reshape(1, row_count, hidden_width).astype(jnp.bfloat16)
    grad_shard = lax.psum_scatter(
        lax.dot_general(
            local_tokens, query_grad, (((0,), (0,)), ((), ())), preferred_element_type=jnp.float32
        ),
        "seq",
        scatter_dimension=0,
        tiled=True,
    )
    weight_grad = lax.psum(grad_shard, "dp")
    return (attended, key_grad, value_grad, weight_grad)


def solution(mesh):
    return jax.shard_map(
        body,
        mesh=mesh,
        in_specs=(
            P("dp", "seq", None),
            P(None, "seq"),
            P("dp", "seq", None),
            P("dp", "seq", None),
            P("dp", "seq", None),
        ),
        out_specs=(
            P("dp", "seq", None),
            P("dp", "seq", None),
            P("dp", "seq", None),
            P("seq", None),
        ),
        check_vma=False,
    )
```

profile of v0, /device:TPU:15, one launch (start us, length us, event | category | flops | bytes accessed | tf_op | source)
XLA Modules:
  0.0 729.7 jit_solution(10739160041827640124)
XLA Ops:
  10.7 1.6 copy.34
  13.8 2.5 copy.58
  16.3 116.3 %all-gather.6.cloned.1.call-done = bf16[2048,2048]{1,0:T(8,128)(2,1)} async-done(((bf16[2048,256]{1,0:T(8,128)(2,1)}), bf16[2048,2048]{1,0:T(8,128)(2,1)}) %all-gather.6.cloned.1.call-update) | async-done | bytes 8388624 | tf_op jit(solution)/shard_map/all_gather | solution.py:39
  132.6 6.7 convolution_convert_fusion
  140.8 3.1 fusion.11
  144.1 2.3 select_convert_fusion
  147.7 2.2 fusion.24
  149.9 108.1 %all-gather.8.cloned.1.call-done = f32[128,128,128]{2,1,0:T(8,128)} async-done(((f32[16,128,128]{2,1,0:T(8,128)}), f32[128,128,128]{2,1,0:T(8,128)}) %all-gather.8.cloned.1.call-update) | async-done | bytes 8388624 | tf_op jit(solution)/shard_map/all_gather | solution.py:13
  258.0 11.3 %while.28 = (s32[]{:T(128)}, f32[16,128,128]{2,1,0:T(8,128)S(1)}, s32[]{:T(128)}, f32[8,16,128,128]{3,2,1,0:T(8,128)}, s32[]{:T(128)}, /*index=5*/s32[]{:T(128)}) while((s32[]{:T(128)}, f32[16,128,128]{2,1,0:T(8,128)S(1)}, s32[]{:T(128)}, f32[8,16,128,128]{3,2,1,0:T(8,128)}, s32[]{:T(128)}, /*index=5*/s32[]{:T(128)}) %tuple.81), condition=%wide.region_1.2_spmd.clone, body=%wide.region_0.1_spmd.clone.sunk | while | flops 786436 | bytes 3145821 | solution.py:23
  259.6 1.6 add_select_fusion.4
  261.2 1.6 add_select_fusion.4
  262.8 1.6 add_select_fusion.4
  264.4 1.6 add_select_fusion.4
  266.1 1.6 add_select_fusion.4
  267.7 1.6 add_select_fusion.4
  269.3 2.8 fusion
  272.1 8.1 %convolution_bitcast_fusion = f32[2048,2048]{0,1:T(8,128)} fusion(bf16[256,2048]{0,1:T(8,128)(2,1)S(1)} %bitcast.79, bf16[1,256,2048]{2,1,0:T(8,128)(2,1)S(1)} %copy-done), kind=kOutput, calls=%fused_computation.2 | convolution fusion | flops 2147483648 | bytes 18874368 | tf_op jit(solution)/shard_map/dot_general | solution.py:98
  280.5 2.4 select_convert_fusion.1
  286.3 2.4 copy.49
  288.7 3.3 fusion.23
  292.0 90.8 %all-gather.10.cloned.1.call-done = f32[128,128,128]{2,1,0:T(8,128)} async-done(((f32[16,128,128]{2,1,0:T(8,128)}), f32[128,128,128]{2,1,0:T(8,128)}) %all-gather.10.cloned.1.call-update) | async-done | bytes 8388624 | tf_op jit(solution)/shard_map/all_gather | solution.py:13
  382.8 7.7 %rev.3 = f32[8,16,128,128]{3,2,1,0:T(8,128)} reverse(f32[8,16,128,128]{3,2,1,0:T(8,128)} %bitcast.78), dimensions={0} | reverse | bytes 16777216 | tf_op jit(solution)/shard_map/rev | solution.py:15
  390.6 11.6 %while.29 = (s32[]{:T(128)}, f32[16,128,128]{2,1,0:T(8,128)S(1)}, s32[]{:T(128)}, f32[8,16,128,128]{3,2,1,0:T(8,128)}, s32[]{:T(128)}, /*index=5*/s32[]{:T(128)}) while((s32[]{:T(128)}, f32[16,128,128]{2,1,0:T(8,128)S(1)}, s32[]{:T(128)}, f32[8,16,128,128]{3,2,1,0:T(8,128)}, s32[]{:T(128)}, /*index=5*/s32[]{:T(128)}) %tuple.68), condition=%wide.region_3.4_spmd.clone, body=%wide.region_2.3_spmd.clone.sunk | while | flops 786436 | bytes 3145821 | solution.py:23
  393.8 1.6 add_select_fusion.5
  395.4 1.9 add_select_fusion.5
  397.3 1.6 add_select_fusion.5
  400.5 1.6 add_select_fusion.5
  402.2 264.8 %reduce-scatter.2.cloned.1.call-done = f32[256,2048]{0,1:T(8,128)} async-done(((f32[2048,2048]{0,1:T(8,128)}), f32[256,2048]{0,1:T(8,128)}) %reduce-scatter.2.cloned.1.call-update) | async-done | bytes 2097168 | tf_op jit(solution)/shard_map/reduce_scatter | solution.py:97
  667.0 3.1 add_convert_fusion
  670.1 2.4 copy.50
  676.4 43.8 %all-reduce.2.cloned.1.call-done = f32[256,2048]{0,1:T(8,128)} async-done(((f32[256,2048]{0,1:T(8,128)}), f32[256,2048]{0,1:T(8,128)}) %all-reduce.2.cloned.1.call-update) | async-done | bytes 2097168 | tf_op jit(solution)/shard_map/psum | solution.py:105
  720.3 2.9 copy.52
  (52 shorter events, 21.8 us)
Async XLA Ops:
  7.2 125.4 %copy-start = (bf16[1,256,2048]{2,1,0:T(8,128)(2,1)S(1)}, bf16[1,256,2048]{2,1,0:T(8,128)(2,1)}, u32[]{:S(2)}) copy-start(bf16[1,256,2048]{2,1,0:T(8,128)(2,1)} %param.9) | copy-start | bytes 3145732
  7.2 2.3 copy-start.12
  7.2 125.4 %all-gather.6.cloned.1.call-start = ((), (), s32[]{:S(2)}) async-start(), calls=%async_computation.1 | async-start | bytes 9437184 | tf_op jit(solution)/shard_map/all_gather | solution.py:39
  7.9 250.1 %all-gather.8.cloned.1.call-start = ((), (), s32[]{:S(2)}) async-start(), calls=%async_computation.4 | async-start | bytes 9437184 | tf_op jit(solution)/shard_map/all_gather | solution.py:13
  12.3 1.5 copy-start.6
  13.8 369.0 %all-gather.10.cloned.1.call-start = ((), (), s32[]{:S(2)}) async-start(), calls=%async_computation.5 | async-start | bytes 9437184 | tf_op jit(solution)/shard_map/all_gather | solution.py:13
  140.8 3.2 copy-start.2
  144.0 523.1 %reduce-scatter.2.cloned.1.call-start = ((), (), s32[]{:S(2)}) async-start(), calls=%async_computation.2 | async-start | bytes 18874368 | tf_op jit(solution)/shard_map/reduce_scatter | solution.py:97
  144.1 3.6 copy-start.7
  146.3 1.3 copy-start.11
  280.2 440.0 %all-reduce.2.cloned.1.call-start = ((), (), s32[]{:S(2)}) async-start(), calls=%async_computation.3 | async-start | bytes 4194304 | tf_op jit(solution)/shard_map/psum | solution.py:105
  282.9 1.4 copy-start.9
  282.9 2.0 copy-start.3
  286.3 2.4 copy-start.4
  670.1 2.4 copy-start.8
  672.5 1.2 copy-start.5
  672.5 1.9 copy-start.10
  675.0 48.1 %copy-start.1 = (bf16[1,256,2048]{2,1,0:T(8,128)(2,1)S(1)}, bf16[1,256,2048]{2,1,0:T(8,128)(2,1)}, u32[]{:S(2)}) copy-start(bf16[1,256,2048]{2,1,0:T(8,128)(2,1)} %param.9) | copy-start | bytes 3145732
Sparse Core Ops, SparseCore 0:
  10.0 122.5 all-gather.5
  135.3 122.6 all-gather.7
  260.1 122.6 all-gather.9
  386.5 280.5 reduce-scatter.1
  669.2 50.9 all-reduce.1
where the time goes:
time: 733 us; the launch traced here: 730 us
  waiting for transfers between devices  625 us (85%)
  matrix products  38.9 us (5%)
  local copies, waits for them, and re-layouts  28.9 us (4%)
  other arithmetic  22.6 us (3%)
  between operations  14 us (2%)
    reduce_scatter x1, waiting for transfers between devices, body(): lax.psum_scatter(lax.dot_general(local_tokens, query_grad, (((0,), (0,)),...  265 us
    all_gather x2, waiting for transfers between devices, carried_in(): pieces = lax.all_gather(value, axis)  199 us
    all_gather x1, waiting for transfers between devices, body(): lax.all_gather(query_weight, 'seq', axis=1, tiled=True)  116 us
    psum x1, waiting for transfers between devices, body(): weight_grad = lax.psum(grad_shard, 'dp')  43.8 us
    select_n x14, other arithmetic, step(): return jnp.where(position < mine, longer, total)  22.6 us
    unnamed x33, local copies, waits for them, and re-layouts  18.1 us
  transfers between devices with their start and end apart: 5, of which 5 were waited for; matrix products, arithmetic and copies ran while one was open for 11% of the time, Pallas kernels for 0%

commit v1 on v0

v1 whole, which is shorter than its diff:
```python
import functools
import math

import jax
import jax.numpy as jnp
from jax import lax
from jax.experimental import pallas as pl
from jax.experimental.pallas import tpu as pltpu
from jax.sharding import PartitionSpec as P

DH = 128
F32 = jnp.float32
BF16 = jnp.bfloat16
MIB = 1 << 20


def dot(a, b, dims):
    return lax.dot_general(a, b, ((dims[:1], dims[1:]), ((), ())), preferred_element_type=F32)


def lanes(index, width=DH):
    return pl.ds(pl.multiple_of(index * width, DH), width)


def call(kernel, outs, *args, flops=0):
    moved = sum(math.prod(a.shape) * a.dtype.itemsize for a in (*args, *outs))
    return pl.pallas_call(
        kernel,
        out_shape=tuple(outs),
        in_specs=[pl.BlockSpec(memory_space=pltpu.VMEM)] * len(args),
        out_specs=tuple([pl.BlockSpec(memory_space=pltpu.VMEM)] * len(outs)),
        cost_estimate=pl.CostEstimate(flops=flops, bytes_accessed=moved, transcendentals=0),
        compiler_params=pltpu.CompilerParams(vmem_limit_bytes=min(60 * MIB, 2 * moved + 8 * MIB)),
    )(*args)


def out(shape, dtype):
    return jax.ShapeDtypeStruct(shape, dtype)


def causal(rows):
    return lax.broadcasted_iota(jnp.int32, (rows, rows), 0) >= lax.broadcasted_iota(
        jnp.int32, (rows, rows), 1
    )


def scores(a, b, mask, factor):
    return jnp.where(mask, factor * dot(a, b, (1, 1)), 0.0).astype(BF16)


def head_of(slot, shards, interleaved):
    if not interleaved:
        return slot
    s, d = lax.axis_index("seq"), lax.axis_index("dp")
    half, rest = divmod(slot, shards)
    step, side = divmod(rest, 2)
    source = lax.rem(s // 2 + (shards // 2 - step), shards // 2) * 2 + lax.rem(s + side, 2)
    return source * 2 + lax.rem(d // 2 + half, 2)


def kv_kernel(heads, k_ref, v_ref, o_ref):
    for h in range(heads):
        cols = pl.ds(h * DH, DH)
        o_ref[pl.ds(h * DH, DH), :] = dot(k_ref[:, cols], v_ref[:, cols], (0, 0)).astype(BF16)


def qg_kernel(heads, shards, inter, qa_ref, qb_ref, g_ref, o_ref):
    for slot in range(heads):
        ref = (qa_ref, qb_ref)[slot // (heads // 2)]
        h = head_of(slot, shards, inter)
        q = ref[:, pl.ds(slot % (heads // 2) * DH, DH)]
        o_ref[lanes(h), :] = dot(q, g_ref[:, lanes(h)], (0, 0)).astype(BF16)


def scan_kernel(count, backward, i_ref, o_ref):
    rows = i_ref.shape[0] // count
    total = jnp.zeros((rows, i_ref.shape[1]), F32)
    order = range(count)
    for c in reversed(order) if backward else order:
        block = pl.ds(c * rows, rows)
        o_ref[block, :] = total.astype(BF16)
        total = total + i_ref[block, :].astype(F32)


def query_grad_kernel(factor, heads, k_ref, v_ref, g_ref, p_ref, *o_refs):
    mask = causal(k_ref.shape[0])
    d = lax.axis_index("dp")
    per = heads // len(o_refs)
    for step, o_ref in enumerate(o_refs):
        base = jnp.bitwise_xor(d, step) * per
        for j in range(per):
            cols = lanes(base + j)
            g = g_ref[:, cols]
            grad_scores = scores(g, v_ref[:, cols], mask, factor)
            o_ref[:, pl.ds(j * DH, DH)] = (
                dot(grad_scores, k_ref[:, cols], (1, 0))
                + factor * dot(g, p_ref[cols, :], (1, 1))
            ).astype(BF16)


def attended_kernel(factor, heads, shards, inter, qa_ref, qb_ref, k_ref, v_ref, p_ref, o_ref):
    mask = causal(k_ref.shape[0])
    for slot in range(heads):
        ref = (qa_ref, qb_ref)[slot // (heads // 2)]
        cols = lanes(head_of(slot, shards, inter))
        q = ref[:, pl.ds(slot % (heads // 2) * DH, DH)]
        key_scores = scores(q, k_ref[:, cols], mask, factor)
        o_ref[:, cols] = (
            dot(key_scores, v_ref[:, cols], (1, 0)) + factor * dot(q, p_ref[cols, :], (1, 0))
        ).astype(BF16)


def pair_grad_kernel(
    factor, heads, shards, inter, qa_ref, qb_ref, k_ref, v_ref, g_ref, s_ref, dk_ref, dv_ref
):
    mask = causal(k_ref.shape[0])
    for slot in range(heads):
        ref = (qa_ref, qb_ref)[slot // (heads // 2)]
        cols = lanes(head_of(slot, shards, inter))
        q = ref[:, pl.ds(slot % (heads // 2) * DH, DH)]
        k, v, g, suffix = k_ref[:, cols], v_ref[:, cols], g_ref[:, cols], s_ref[cols, :]
        key_scores = scores(q, k, mask, factor)
        grad_scores = scores(g, v, mask, factor)
        dk_ref[:, cols] = (
            dot(grad_scores, q, (0, 0)) + factor * dot(v, suffix, (1, 1))
        ).astype(BF16)
        dv_ref[:, cols] = (
            dot(key_scores, g, (0, 0)) + factor * dot(k, suffix, (1, 0))
        ).astype(BF16)


def project_kernel(mine_ref, theirs_ref, near_ref, far_ref, qa_ref, qb_ref):
    depth = near_ref.shape[1]
    c = lax.rem(lax.axis_index("dp"), 2)
    width = near_ref.shape[2]
    for t_ref, o_ref in ((mine_ref, qa_ref), (theirs_ref, qb_ref)):
        near = t_ref[:, lanes(c, depth)]
        far = t_ref[:, lanes(1 - c, depth)]
        for step in range(near_ref.shape[0]):
            o_ref[:, pl.ds(step * width, width)] = (
                dot(near, near_ref[step], (1, 0)) + dot(far, far_ref[step], (1, 0))
            ).astype(BF16)


def weight_kernel(count, other, *refs):
    o_ref = refs[-1]
    pairs = len(refs) // 2
    rows = refs[0].shape[1] // count
    s = lax.axis_index("seq")
    for step in range(count // 2):
        target = lax.rem(s // 2 + step, count // 2) * 2 + lax.rem(s + other, 2)
        total = None
        for t_ref, g_ref in zip(refs[:pairs], refs[pairs:-1]):
            term = dot(t_ref[:, lanes(target, rows)], g_ref[...], (0, 0))
            total = term if total is None else total + term
        o_ref[pl.ds(step * rows, rows), :] = total.astype(o_ref.dtype)


def fold_kernel(keep_ref, got_ref, *o_refs):
    rows = o_refs[0].shape[0]
    for step, o_ref in enumerate(o_refs):
        block = pl.ds(step * rows, rows)
        o_ref[...] = (keep_ref[block, :] + got_ref[block, :].astype(F32)).astype(o_ref.dtype)


def sum_kernel(first_ref, *refs):
    total = first_ref[...]
    for ref in refs[:-1]:
        total = total + ref[...].astype(F32)
    refs[-1][...] = total.astype(refs[-1].dtype)


def join_kernel(*refs):
    d = lax.axis_index("dp")
    width = refs[0].shape[1]
    for step, ref in enumerate(refs[:-1]):
        refs[-1][:, lanes(jnp.bitwise_xor(d, step), width)] = ref[...].astype(F32)


def body(tokens, query_weight, key_rows, value_rows, out_grad):
    rows, width = key_rows.shape[1:]
    model = tokens.shape[2]
    heads = width // DH
    seqs, dps = lax.axis_size("seq"), lax.axis_size("dp")
    factor = 1.0 / math.sqrt(DH * rows * seqs)
    split = query_weight.shape[1] == 2 * DH and seqs == 8 and dps == 4
    toks, keys, values, grads = tokens[0], key_rows[0], value_rows[0], out_grad[0]
    state = out((heads * DH, DH), BF16)

    def xor_dp(value, step):
        return lax.ppermute(value, "dp", [(i, i ^ step) for i in range(dps)])

    def flip_seq(value):
        return lax.ppermute(value, "seq", [(i, i ^ 1) for i in range(seqs)])

    def turn_seq(value, step):
        return lax.ppermute(value, "seq", [(i, (i + 2 * step) % seqs) for i in range(seqs)])

    def swap(value):
        return lax.all_to_all(value, "seq", 0, 0, tiled=True)

    def carried(blocks, backward):
        scan = functools.partial(scan_kernel, seqs, backward)
        return swap(call(scan, [state], swap(blocks))[0])

    group = [toks] + [xor_dp(toks, step) for step in (1, 2) if step < dps]
    if split:
        group.append(xor_dp(group[2], 1))
    else:
        group += [xor_dp(toks, step) for step in range(3, dps)]

    if split:
        d = lax.axis_index("dp")
        half = model // 2
        piece = lax.dynamic_slice(query_weight, (d % 2 * half, d // 2 * DH), (half, DH))
        column = [piece] + [turn_seq(piece, step) for step in range(1, seqs // 2)]
        sides = [flip_seq(value) for value in column]
        near = jnp.stack([jnp.concatenate(two, axis=1) for two in zip(column, sides)])
        far = xor_dp(near, 1)
        qs = call(
            project_kernel,
            [out((rows, width // 2), BF16)] * 2,
            toks,
            group[2],
            near,
            far,
            flops=2 * rows * model * width,
        )
        pair = (qs[0], xor_dp(qs[1], 2))
    else:
        query_rows = jnp.dot(
            toks,
            lax.all_gather(query_weight, "seq", axis=1, tiled=True),
            preferred_element_type=F32,
        ).astype(BF16)
        pair = (query_rows[:, : width // 2], query_rows[:, width // 2 :])

    block_kv = call(functools.partial(kv_kernel, heads), [state], keys, values)[0]
    prefix = carried(block_kv, False)
    grad_parts = call(
        functools.partial(query_grad_kernel, factor, heads),
        [out((rows, width // dps), BF16)] * dps,
        keys,
        values,
        grads,
        prefix,
    )
    grad_group = [grad_parts[0]] + [xor_dp(grad_parts[step], step) for step in range(1, dps)]

    if split:
        block = model // seqs
        tall = (model // 2, width // dps)
        send = call(
            functools.partial(weight_kernel, seqs, 1),
            [out(tall, BF16)],
            *group,
            *grad_group,
        )[0]
        got = flip_seq(send)
        keep = call(
            functools.partial(weight_kernel, seqs, 0),
            [out(tall, F32)],
            *group,
            *grad_group,
        )[0]
        folded = call(
            fold_kernel,
            [out((block, tall[1]), F32 if step == 0 else BF16) for step in range(seqs // 2)],
            keep,
            got,
        )
        share = call(
            sum_kernel,
            [out((block, tall[1]), BF16)],
            folded[0],
            *[turn_seq(folded[step], step) for step in range(1, seqs // 2)],
        )[0]
    else:
        share = lax.psum_scatter(
            lax.dot_general(
                jnp.concatenate(group),
                jnp.concatenate(grad_group),
                (((0,), (0,)), ((), ())),
                preferred_element_type=F32,
            ),
            "seq",
            scatter_dimension=0,
            tiled=True,
        )
    weight_grad = call(
        join_kernel,
        [out((share.shape[0], width), F32)],
        share,
        *[xor_dp(share, step) for step in range(1, dps)],
    )[0]

    block_qg = call(
        functools.partial(qg_kernel, heads, seqs, split), [state], *pair, grads
    )[0]
    suffix = carried(block_qg, True)
    attended = call(
        functools.partial(attended_kernel, factor, heads, seqs, split),
        [out((rows, width), BF16)],
        *pair,
        keys,
        values,
        prefix,
    )[0]
    key_grad, value_grad = call(
        functools.partial(pair_grad_kernel, factor, heads, seqs, split),
        [out((rows, width), BF16)] * 2,
        *pair,
        keys,
        values,
        grads,
        suffix,
    )
    return (attended[None], key_grad[None], value_grad[None], weight_grad)


def solution(mesh):
    return jax.shard_map(
        body,
        mesh=mesh,
        in_specs=(
            P("dp", "seq", None),
            P(None, "seq"),
            P("dp", "seq", None),
            P("dp", "seq", None),
            P("dp", "seq", None),
        ),
        out_specs=(
            P("dp", "seq", None),
            P("dp", "seq", None),
            P("dp", "seq", None),
            P("seq", None),
        ),
        check_vma=False,
    )
```

time: 733 us -> 195 us (0.27)
  waiting for transfers between devices: 625 us -> 104 us
  starting transfers between devices: 0.38 us -> 45.3 us
  matrix products: 38.9 us -> 0 us
  Pallas kernels: 0 us -> 37.9 us
  local copies, waits for them, and re-layouts: 28.9 us -> 4.43 us
  other arithmetic: 22.6 us -> 1.81 us
  between operations: 14 us -> 0.81 us
    all_gather x3 -> x0, waiting for transfers between devices: 315 us -> none  [the longest x2 199 us: carried_in(): pieces = lax.all_gather(value, axis)]
    reduce_scatter x1 -> x0, waiting for transfers between devices: 265 us -> none  [body(): lax.psum_scatter(lax.dot_general(local_tokens, query_grad, (((0,), (0,)),...]
    ppermute x0 -> x22, waiting for transfers between devices: none -> 87.1 us  [the longest x6 43.7 us: turn_seq(): lax.ppermute(value, 'seq', [(i, (i + 2 * step) % seqs) for i in range(seq...]
    psum x1 -> x0, waiting for transfers between devices: 43.8 us -> none  [body(): weight_grad = lax.psum(grad_shard, 'dp')]
    dot_general x14 -> x0, matrix products: 38.9 us -> none  [the longest x1 8.08 us: body(): lax.dot_general(local_tokens, query_grad, (((0,), (0,)), ((), ())), prefe...]
    pallas_call x0 -> x13, Pallas kernels: none -> 37.9 us  [call(): pl.pallas_call(kernel, out_shape=tuple(outs), in_specs=[pl.BlockSpec(memo...]
    all_to_all x0 -> x4, starting transfers between devices: none -> 24.5 us  [swap(): return lax.all_to_all(value, 'seq', 0, 0, tiled=True)]
    select_n x14 -> x0, other arithmetic: 22.6 us -> none  [step(): return jnp.where(position < mine, longer, total)]
  transfers between devices with their start and end apart: 5 -> 26, of which waited for: 5 -> 16; matrix products, arithmetic and copies ran while one was open for 11% -> 0% of each run, Pallas kernels for 0% -> 16%
where the time goes in v1:
time: 195 us; the launch traced here: 194 us
  waiting for transfers between devices  104 us (53%)
  starting transfers between devices  45.3 us (23%)
  Pallas kernels  37.9 us (19%)
  local copies, waits for them, and re-layouts  4.43 us (2%)
    ppermute x6, waiting for transfers between devices, turn_seq(): lax.ppermute(value, 'seq', [(i, (i + 2 * step) % seqs) for i in range(seq...  43.7 us
    pallas_call x13, Pallas kernels, call(): pl.pallas_call(kernel, out_shape=tuple(outs), in_specs=[pl.BlockSpec(memo...  37.9 us
    all_to_all x4, starting transfers between devices, swap(): return lax.all_to_all(value, 'seq', 0, 0, tiled=True)  24.5 us
    ppermute x5, waiting for transfers between devices, flip_seq(): return lax.ppermute(value, 'seq', [(i, i ^ 1) for i in range(seqs)])  22.1 us
    ppermute x11, waiting for transfers between devices, xor_dp(): return lax.ppermute(value, 'dp', [(i, i ^ step) for i in range(dps)])  21.2 us
    all_to_all x4, waiting for transfers between devices, swap(): return lax.all_to_all(value, 'seq', 0, 0, tiled=True)  16.7 us
    ppermute x11, starting transfers between devices, xor_dp(): return lax.ppermute(value, 'dp', [(i, i ^ step) for i in range(dps)])  11.4 us
    ppermute x6, starting transfers between devices, turn_seq(): lax.ppermute(value, 'seq', [(i, (i + 2 * step) % seqs) for i in range(seq...  8.22 us
  transfers between devices with their start and end apart: 26, of which 16 were waited for; matrix products, arithmetic and copies ran while one was open for 0% of the time, Pallas kernels for 16%

profile of v1, /device:TPU:15, one launch (start us, length us, event | category | flops | bytes accessed | tf_op | source)
XLA Modules:
  0.0 193.9 jit_solution(2257513027110471690)
XLA Ops:
  5.7 3.2 %collective-permute-done.2 = bf16[1024,128]{1,0:T(8,128)(2,1)S(1)} collective-permute-done((bf16[1024,128]{1,0:T(8,128)(2,1)S(1)}, bf16[1024,128]{1,0:T(8,128)(2,1)S(1)}, u32[]{:S(2)}, u32[]{:S(2)}) %collective-permute-start.2) | collective-permute-done | bytes 262176 | tf_op jit(solution)/shard_map/ppermute | solution.py:197
  9.1 15.7 %collective-permute-done.4 = bf16[1024,128]{1,0:T(8,128)(2,1)S(1)} collective-permute-done((bf16[1024,128]{1,0:T(8,128)(2,1)S(1)}, bf16[1024,128]{1,0:T(8,128)(2,1)S(1)}, u32[]{:S(2)}, u32[]{:S(2)}) %collective-permute-start.4) | collective-permute-done | bytes 262176 | tf_op jit(solution)/shard_map/ppermute | solution.py:197
  25.1 2.6 %collective-permute-done.6 = bf16[1024,128]{1,0:T(8,128)(2,1)S(1)} collective-permute-done((bf16[1024,128]{1,0:T(8,128)(2,1)S(1)}, bf16[1024,128]{1,0:T(8,128)(2,1)S(1)}, u32[]{:S(2)}, u32[]{:S(2)}) %collective-permute-start.6) | collective-permute-done | bytes 262176 | tf_op jit(solution)/shard_map/ppermute | solution.py:197
  28.0 3.8 %collective-permute-done.5 = bf16[1024,128]{1,0:T(8,128)(2,1)S(1)} collective-permute-done((bf16[1024,128]{1,0:T(8,128)(2,1)S(1)}, bf16[1024,128]{1,0:T(8,128)(2,1)S(1)}, u32[]{:S(2)}, u32[]{:S(2)}) %collective-permute-start.5) | collective-permute-done | bytes 262176 | tf_op jit(solution)/shard_map/ppermute | solution.py:194
  31.8 5.6 %collective-permute-done.7 = bf16[1024,128]{1,0:T(8,128)(2,1)S(1)} collective-permute-done((bf16[1024,128]{1,0:T(8,128)(2,1)S(1)}, bf16[1024,128]{1,0:T(8,128)(2,1)S(1)}, u32[]{:S(2)}, u32[]{:S(2)}) %collective-permute-start.7) | collective-permute-done | bytes 262176 | tf_op jit(solution)/shard_map/ppermute | solution.py:194
  37.5 1.6 pad_maximum_fusion.near_ref
  39.1 2.1 %collective-permute-start.8 = (bf16[4,1024,256]{2,1,0:T(8,128)(2,1)}, bf16[4,1024,256]{2,1,0:T(8,128)(2,1)}, u32[]{:S(2)}, u32[]{:S(2)}) collective-permute-start(bf16[4,1024,256]{2,1,0:T(8,128)(2,1)} %pad_maximum_fusion.near_ref), channel_id=1, source_target_pairs={{0,1},{1,0},{2,3},{3,2},{4,5},{5,4},{6,7},{7,6},{8,9},{9,8},{10,11... | collective-permute-start | bytes 6291464 | tf_op jit(solution)/shard_map/ppermute | solution.py:191
  42.4 6.1 %all-to-all-start = ((bf16[8,256,128]{2,1,0:T(8,128)(2,1)}), bf16[8,256,128]{2,1,0:T(8,128)(2,1)S(1)}, u32[]{:S(2)}, u32[]{:S(2)}) async-start(bf16[8,256,128]{2,1,0:T(8,128)(2,1)} %bitcast.7), calls=%async_computation | async-start | bytes 1048576 | tf_op jit(solution)/shard_map/all_to_all | solution.py:200
  48.8 11.7 %all-to-all-done = bf16[8,256,128]{2,1,0:T(8,128)(2,1)S(1)} async-done(((bf16[8,256,128]{2,1,0:T(8,128)(2,1)}), bf16[8,256,128]{2,1,0:T(8,128)(2,1)S(1)}, u32[]{:S(2)}, u32[]{:S(2)}) %all-to-all-start) | async-done | bytes 524320 | tf_op jit(solution)/shard_map/all_to_all | solution.py:200
  61.4 6.3 %all-to-all-start.1 = ((bf16[8,256,128]{2,1,0:T(8,128)(2,1)}), bf16[8,256,128]{2,1,0:T(8,128)(2,1)}, u32[]{:S(2)}, u32[]{:S(2)}) async-start(bf16[8,256,128]{2,1,0:T(8,128)(2,1)} %bitcast.9), calls=%async_computation.1 | async-start | bytes 1048576 | tf_op jit(solution)/shard_map/all_to_all | solution.py:200
  69.2 3.1 %collective-permute-done.theirs_ref.refs_2_ = bf16[256,2048]{1,0:T(8,128)(2,1)} collective-permute-done((bf16[256,2048]{1,0:T(8,128)(2,1)}, bf16[256,2048]{1,0:T(8,128)(2,1)}, u32[]{:S(2)}, u32[]{:S(2)}) %collective-permute-start) | collective-permute-done | bytes 1048608 | tf_op jit(solution)/shard_map/ppermute | solution.py:191
  72.4 2.1 %collective-permute-start.11 = (bf16[256,2048]{1,0:T(8,128)(2,1)}, bf16[256,2048]{1,0:T(8,128)(2,1)}, u32[]{:S(2)}, u32[]{:S(2)}) collective-permute-start(bf16[256,2048]{1,0:T(8,128)(2,1)} %collective-permute-done.theirs_ref.refs_2_), channel_id=1, source_target_pairs={{0,1},{1,0},{2,3},{3,2},{4,5},{5,4},{6,7},{7,6},{8,9},{9,8},{10,11... | collective-permute-start | bytes 3145736 | tf_op jit(solution)/shard_map/ppermute | solution.py:191
  74.5 6.0 %shard_map.84 = (bf16[256,1024]{1,0:T(8,128)(2,1)S(1)}, bf16[256,1024]{1,0:T(8,128)(2,1)}) custom-call(bf16[256,2048]{1,0:T(8,128)(2,1)} %bitcast.mine_ref.refs_0_, bf16[256,2048]{1,0:T(8,128)(2,1)} %collective-permute-done.theirs_ref.refs_2_, bf16[4,1024,256]{2,1,0:T(8,128)(2,1)} %pad_maximum_fusion.near_ref, ...), custom_call_target="tpu_custom_call" | custom-call | flops 2147483648 | bytes 7340032 | tf_op jit(solution)/shard_map/pallas_call | solution.py:27
  81.5 3.8 %shard_map.91 = (bf16[256,512]{1,0:T(8,128)(2,1)S(1)}, bf16[256,512]{1,0:T(8,128)(2,1)}, bf16[256,512]{1,0:T(8,128)(2,1)}, bf16[256,512]{1,0:T(8,128)(2,1)}) custom-call(bf16[256,2048]{1,0:T(8,128)(2,1)S(1)} %bitcast.24, bf16[256,2048]{1,0:T(8,128)(2,1)S(1)} %bitcast.28, bf16[256,2048]{1,0:T(8,128)(2,1)S(1)} %bitcast.31, bf16[2048,128]{1,0:T(8,128)(2,1)} %bitcast.10.p_ref), custom_call_target="tpu_custom_call" | custom-call | bytes 4718592 | tf_op jit(solution)/shard_map/pallas_call | solution.py:27
  86.8 8.2 %collective-permute-done.9.qb_ref = bf16[256,1024]{1,0:T(8,128)(2,1)} collective-permute-done((bf16[256,1024]{1,0:T(8,128)(2,1)}, bf16[256,1024]{1,0:T(8,128)(2,1)}, u32[]{:S(2)}, u32[]{:S(2)}) %collective-permute-start.9) | collective-permute-done | bytes 524320 | tf_op jit(solution)/shard_map/ppermute | solution.py:191
  96.5 1.6 shard_map.88
  98.9 5.4 %all-to-all-start.2 = ((bf16[8,256,128]{2,1,0:T(8,128)(2,1)}), bf16[8,256,128]{2,1,0:T(8,128)(2,1)}, u32[]{:S(2)}, u32[]{:S(2)}) async-start(bf16[8,256,128]{2,1,0:T(8,128)(2,1)} %bitcast.34), calls=%async_computation.2 | async-start | bytes 1048576 | tf_op jit(solution)/shard_map/all_to_all | solution.py:200
  104.4 2.1 %collective-permute-done.14.refs_7_ = bf16[256,512]{1,0:T(8,128)(2,1)} collective-permute-done((bf16[256,512]{1,0:T(8,128)(2,1)}, bf16[256,512]{1,0:T(8,128)(2,1)}, u32[]{:S(2)}, u32[]{:S(2)}) %collective-permute-start.14) | collective-permute-done | bytes 262176 | tf_op jit(solution)/shard_map/ppermute | solution.py:191
  106.5 4.7 %shard_map.93 = bf16[1024,512]{1,0:T(8,128)(2,1)} custom-call(bf16[256,2048]{1,0:T(8,128)(2,1)} %bitcast.mine_ref.refs_0_, bf16[256,2048]{1,0:T(8,128)(2,1)} %collective-permute-done.10.refs_1_, bf16[256,2048]{1,0:T(8,128)(2,1)} %collective-permute-done.theirs_ref.refs_2_, bf16[256,2048]{1,0:T(8,128)(2,1)} %collective-permute-done.11.refs_3_, ...), custom_call_target="tpu_custom_call" | custom-call | bytes 6291456 | tf_op jit(solution)/shard_map/pallas_call | solution.py:27
  111.4 4.9 %all-to-all-done.2 = bf16[8,256,128]{2,1,0:T(8,128)(2,1)} async-done(((bf16[8,256,128]{2,1,0:T(8,128)(2,1)}), bf16[8,256,128]{2,1,0:T(8,128)(2,1)}, u32[]{:S(2)}, u32[]{:S(2)}) %all-to-all-start.2) | async-done | bytes 524320 | tf_op jit(solution)/shard_map/all_to_all | solution.py:200
  118.3 6.5 %all-to-all-start.3 = ((bf16[8,256,128]{2,1,0:T(8,128)(2,1)}), bf16[8,256,128]{2,1,0:T(8,128)(2,1)}, u32[]{:S(2)}, u32[]{:S(2)}) async-start(bf16[8,256,128]{2,1,0:T(8,128)(2,1)} %bitcast.35), calls=%async_computation.3 | async-start | bytes 1048576 | tf_op jit(solution)/shard_map/all_to_all | solution.py:200
  124.9 3.7 %shard_map.92.keep_ref = f32[1024,512]{1,0:T(8,128)S(1)} custom-call(bf16[256,2048]{1,0:T(8,128)(2,1)} %bitcast.mine_ref.refs_0_, bf16[256,2048]{1,0:T(8,128)(2,1)} %collective-permute-done.10.refs_1_, bf16[256,2048]{1,0:T(8,128)(2,1)} %collective-permute-done.theirs_ref.refs_2_, bf16[256,2048]{1,0:T(8,128)(2,1)} %collective-permute-done.11.refs_3_, ...), custom_call_target="tpu_custom_call" | custom-call | bytes 7340032 | tf_op jit(solution)/shard_map/pallas_call | solution.py:27
  128.6 12.8 %collective-permute-done.15.got_ref = bf16[1024,512]{1,0:T(8,128)(2,1)} collective-permute-done((bf16[1024,512]{1,0:T(8,128)(2,1)}, bf16[1024,512]{1,0:T(8,128)(2,1)}, u32[]{:S(2)}, u32[]{:S(2)}) %collective-permute-start.15) | collective-permute-done | bytes 1048608 | tf_op jit(solution)/shard_map/ppermute | solution.py:194
  142.9 2.9 %collective-permute-start.17 = (bf16[256,512]{1,0:T(8,128)(2,1)S(1)}, bf16[256,512]{1,0:T(8,128)(2,1)S(1)}, u32[]{:S(2)}, u32[]{:S(2)}) collective-permute-start(bf16[256,512]{1,0:T(8,128)(2,1)S(1)} %get-tuple-element.26), channel_id=1, source_target_pairs={{0,16},{4,20},{8,24},{12,28},{16,0},{20,4},{24,8},{28,12},{1,17},{... | collective-permute-start | bytes 786440 | tf_op jit(solution)/shard_map/ppermute | solution.py:197
  147.2 2.6 %collective-permute-done.16.refs_0_ = bf16[256,512]{1,0:T(8,128)(2,1)S(1)} collective-permute-done((bf16[256,512]{1,0:T(8,128)(2,1)S(1)}, bf16[256,512]{1,0:T(8,128)(2,1)S(1)}, u32[]{:S(2)}, u32[]{:S(2)}) %collective-permute-start.16) | collective-permute-done | bytes 262176 | tf_op jit(solution)/shard_map/ppermute | solution.py:197
  149.9 13.9 %collective-permute-done.17.refs_1_ = bf16[256,512]{1,0:T(8,128)(2,1)S(1)} collective-permute-done((bf16[256,512]{1,0:T(8,128)(2,1)S(1)}, bf16[256,512]{1,0:T(8,128)(2,1)S(1)}, u32[]{:S(2)}, u32[]{:S(2)}) %collective-permute-start.17) | collective-permute-done | bytes 262176 | tf_op jit(solution)/shard_map/ppermute | solution.py:197
  163.7 5.7 %collective-permute-done.18.refs_2_ = bf16[256,512]{1,0:T(8,128)(2,1)S(1)} collective-permute-done((bf16[256,512]{1,0:T(8,128)(2,1)S(1)}, bf16[256,512]{1,0:T(8,128)(2,1)S(1)}, u32[]{:S(2)}, u32[]{:S(2)}) %collective-permute-start.18) | collective-permute-done | bytes 262176 | tf_op jit(solution)/shard_map/ppermute | solution.py:197
  170.2 1.6 collective-permute-start.21
  171.8 4.2 %shard_map.87 = bf16[256,2048]{1,0:T(8,128)(2,1)} custom-call(bf16[256,1024]{1,0:T(8,128)(2,1)S(1)} %copy-done.5, bf16[256,1024]{1,0:T(8,128)(2,1)} %collective-permute-done.9.qb_ref, bf16[256,2048]{1,0:T(8,128)(2,1)S(1)} %bitcast.25, bf16[256,2048]{1,0:T(8,128)(2,1)S(1)} %bitcast.29, bf16[2048,128]{1,0:T(8,128)(2,1)} %bitcast.10.p_ref), custom_call_target="tpu_custom_call" | custom-call | bytes 4718592 | tf_op jit(solution)/shard_map/pallas_call | solution.py:27
  176.0 1.9 collective-permute-done.20.refs_2_
  177.9 5.9 %collective-permute-done.21.refs_3_ = bf16[256,512]{1,0:T(8,128)(2,1)S(1)} collective-permute-done((bf16[256,512]{1,0:T(8,128)(2,1)S(1)}, bf16[256,512]{1,0:T(8,128)(2,1)S(1)}, u32[]{:S(2)}, u32[]{:S(2)}) %collective-permute-start.21) | collective-permute-done | bytes 262176 | tf_op jit(solution)/shard_map/ppermute | solution.py:191
  186.3 7.7 %shard_map.90 = (bf16[256,2048]{1,0:T(8,128)(2,1)}, bf16[256,2048]{1,0:T(8,128)(2,1)}) custom-call(bf16[256,1024]{1,0:T(8,128)(2,1)S(1)} %copy-done.6, bf16[256,1024]{1,0:T(8,128)(2,1)} %collective-permute-done.9.qb_ref, bf16[256,2048]{1,0:T(8,128)(2,1)S(1)} %bitcast.26, bf16[256,2048]{1,0:T(8,128)(2,1)S(1)} %bitcast.30, bf16[256,2048]{1,0:T(8,128)(2,1)S(1)} %bitcast.33, ...), custom_call_target="tpu_custom_call" | custom-call | bytes 6815744 | tf_op jit(solution)/shard_map/pallas_call | solution.py:27
  (57 shorter events, 23.0 us)
Async XLA Ops:
  1.6 7.2 %collective-permute-start.2 = (bf16[1024,128]{1,0:T(8,128)(2,1)S(1)}, bf16[1024,128]{1,0:T(8,128)(2,1)S(1)}, u32[]{:S(2)}, u32[]{:S(2)}) collective-permute-start(bf16[1024,128]{1,0:T(8,128)(2,1)S(1)} %dynamic_slice.3), channel_id=1, source_target_pairs={{0,8},{4,12},{8,16},{12,20},{16,24},{20,28},{24,0},{28,4},{1,9},{5... | collective-permute-start | bytes 786440 | tf_op jit(solution)/shard_map/ppermute | solution.py:197
  3.0 21.8 %collective-permute-start.4 = (bf16[1024,128]{1,0:T(8,128)(2,1)S(1)}, bf16[1024,128]{1,0:T(8,128)(2,1)S(1)}, u32[]{:S(2)}, u32[]{:S(2)}) collective-permute-start(bf16[1024,128]{1,0:T(8,128)(2,1)S(1)} %dynamic_slice.3), channel_id=1, source_target_pairs={{0,16},{4,20},{8,24},{12,28},{16,0},{20,4},{24,8},{28,12},{1,17},{... | collective-permute-start | bytes 786440 | tf_op jit(solution)/shard_map/ppermute | solution.py:197
  4.1 23.6 %collective-permute-start.6 = (bf16[1024,128]{1,0:T(8,128)(2,1)S(1)}, bf16[1024,128]{1,0:T(8,128)(2,1)S(1)}, u32[]{:S(2)}, u32[]{:S(2)}) collective-permute-start(bf16[1024,128]{1,0:T(8,128)(2,1)S(1)} %dynamic_slice.3), channel_id=1, source_target_pairs={{0,24},{4,28},{8,0},{12,4},{16,8},{20,12},{24,16},{28,20},{1,25},{... | collective-permute-start | bytes 786440 | tf_op jit(solution)/shard_map/ppermute | solution.py:197
  5.5 22.4 %collective-permute-start.1 = (bf16[1024,128]{1,0:T(8,128)(2,1)S(1)}, bf16[1024,128]{1,0:T(8,128)(2,1)S(1)}, u32[]{:S(2)}, u32[]{:S(2)}) collective-permute-start(bf16[1024,128]{1,0:T(8,128)(2,1)S(1)} %dynamic_slice.3), channel_id=1, source_target_pairs={{0,4},{4,0},{8,12},{12,8},{16,20},{20,16},{24,28},{28,24},{1,5},{5... | collective-permute-start | bytes 786440 | tf_op jit(solution)/shard_map/ppermute | solution.py:194
  8.9 19.1 %collective-permute-start.3 = (bf16[1024,128]{1,0:T(8,128)(2,1)S(1)}, bf16[1024,128]{1,0:T(8,128)(2,1)S(1)}, u32[]{:S(2)}, u32[]{:S(2)}) collective-permute-start(bf16[1024,128]{1,0:T(8,128)(2,1)S(1)} %collective-permute-done.2), channel_id=1, source_target_pairs={{0,4},{4,0},{8,12},{12,8},{16,20},{20,16},{24,28},{28,24},{1,5},{5... | collective-permute-start | bytes 786440 | tf_op jit(solution)/shard_map/ppermute | solution.py:194
  24.8 7.0 %collective-permute-start.5 = (bf16[1024,128]{1,0:T(8,128)(2,1)S(1)}, bf16[1024,128]{1,0:T(8,128)(2,1)S(1)}, u32[]{:S(2)}, u32[]{:S(2)}) collective-permute-start(bf16[1024,128]{1,0:T(8,128)(2,1)S(1)} %collective-permute-done.4), channel_id=1, source_target_pairs={{0,4},{4,0},{8,12},{12,8},{16,20},{20,16},{24,28},{28,24},{1,5},{5... | collective-permute-start | bytes 786440 | tf_op jit(solution)/shard_map/ppermute | solution.py:194
  27.7 9.7 %collective-permute-start.7 = (bf16[1024,128]{1,0:T(8,128)(2,1)S(1)}, bf16[1024,128]{1,0:T(8,128)(2,1)S(1)}, u32[]{:S(2)}, u32[]{:S(2)}) collective-permute-start(bf16[1024,128]{1,0:T(8,128)(2,1)S(1)} %collective-permute-done.6), channel_id=1, source_target_pairs={{0,4},{4,0},{8,12},{12,8},{16,20},{20,16},{24,28},{28,24},{1,5},{5... | collective-permute-start | bytes 786440 | tf_op jit(solution)/shard_map/ppermute | solution.py:194
  37.5 3.7 %copy-start = (bf16[1,256,2048]{2,1,0:T(8,128)(2,1)S(1)}, bf16[1,256,2048]{2,1,0:T(8,128)(2,1)}, u32[]{:S(2)}) copy-start(bf16[1,256,2048]{2,1,0:T(8,128)(2,1)} %param.7) | copy-start | bytes 3145732
  37.5 3.7 %copy-start.1 = (bf16[1,256,2048]{2,1,0:T(8,128)(2,1)S(1)}, bf16[1,256,2048]{2,1,0:T(8,128)(2,1)}, u32[]{:S(2)}) copy-start(bf16[1,256,2048]{2,1,0:T(8,128)(2,1)} %param.8) | copy-start | bytes 3145732
  39.1 35.4 %collective-permute-start.8 = (bf16[4,1024,256]{2,1,0:T(8,128)(2,1)}, bf16[4,1024,256]{2,1,0:T(8,128)(2,1)}, u32[]{:S(2)}, u32[]{:S(2)}) collective-permute-start(bf16[4,1024,256]{2,1,0:T(8,128)(2,1)} %pad_maximum_fusion.near_ref), channel_id=1, source_target_pairs={{0,1},{1,0},{2,3},{3,2},{4,5},{5,4},{6,7},{7,6},{8,9},{9,8},{10,11... | collective-permute-start | bytes 6291464 | tf_op jit(solution)/shard_map/ppermute | solution.py:191
  42.4 18.1 %all-to-all-start = ((bf16[8,256,128]{2,1,0:T(8,128)(2,1)}), bf16[8,256,128]{2,1,0:T(8,128)(2,1)S(1)}, u32[]{:S(2)}, u32[]{:S(2)}) async-start(bf16[8,256,128]{2,1,0:T(8,128)(2,1)} %bitcast.7), calls=%async_computation | async-start | bytes 1048576 | tf_op jit(solution)/shard_map/all_to_all | solution.py:200
  48.6 23.8 %collective-permute-start = (bf16[256,2048]{1,0:T(8,128)(2,1)}, bf16[256,2048]{1,0:T(8,128)(2,1)}, u32[]{:S(2)}, u32[]{:S(2)}) collective-permute-start(bf16[256,2048]{1,0:T(8,128)(2,1)} %bitcast.mine_ref.refs_0_), channel_id=1, source_target_pairs={{0,2},{1,3},{2,0},{3,1},{4,6},{5,7},{6,4},{7,5},{8,10},{9,11},{10,... | collective-permute-start | bytes 3145736 | tf_op jit(solution)/shard_map/ppermute | solution.py:191
  61.4 20.1 %all-to-all-start.1 = ((bf16[8,256,128]{2,1,0:T(8,128)(2,1)}), bf16[8,256,128]{2,1,0:T(8,128)(2,1)}, u32[]{:S(2)}, u32[]{:S(2)}) async-start(bf16[8,256,128]{2,1,0:T(8,128)(2,1)} %bitcast.9), calls=%async_computation.1 | async-start | bytes 1048576 | tf_op jit(solution)/shard_map/all_to_all | solution.py:200
  67.8 13.8 %copy-start.2 = (bf16[1,256,2048]{2,1,0:T(8,128)(2,1)S(1)}, bf16[1,256,2048]{2,1,0:T(8,128)(2,1)}, u32[]{:S(2)}) copy-start(bf16[1,256,2048]{2,1,0:T(8,128)(2,1)} %param.9) | copy-start | bytes 3145732
  67.8 36.6 %collective-permute-start.10 = (bf16[256,2048]{1,0:T(8,128)(2,1)}, bf16[256,2048]{1,0:T(8,128)(2,1)}, u32[]{:S(2)}, u32[]{:S(2)}) collective-permute-start(bf16[256,2048]{1,0:T(8,128)(2,1)} %bitcast.mine_ref.refs_0_), channel_id=1, source_target_pairs={{0,1},{1,0},{2,3},{3,2},{4,5},{5,4},{6,7},{7,6},{8,9},{9,8},{10,11... | collective-permute-start | bytes 3145736 | tf_op jit(solution)/shard_map/ppermute | solution.py:191
  72.4 34.1 %collective-permute-start.11 = (bf16[256,2048]{1,0:T(8,128)(2,1)}, bf16[256,2048]{1,0:T(8,128)(2,1)}, u32[]{:S(2)}, u32[]{:S(2)}) collective-permute-start(bf16[256,2048]{1,0:T(8,128)(2,1)} %collective-permute-done.theirs_ref.refs_2_), channel_id=1, source_target_pairs={{0,1},{1,0},{2,3},{3,2},{4,5},{5,4},{6,7},{7,6},{8,9},{9,8},{10,11... | collective-permute-start | bytes 3145736 | tf_op jit(solution)/shard_map/ppermute | solution.py:191
  81.3 13.8 %collective-permute-start.9 = (bf16[256,1024]{1,0:T(8,128)(2,1)}, bf16[256,1024]{1,0:T(8,128)(2,1)}, u32[]{:S(2)}, u32[]{:S(2)}) collective-permute-start(bf16[256,1024]{1,0:T(8,128)(2,1)} %get-tuple-element.17), channel_id=1, source_target_pairs={{0,2},{1,3},{2,0},{3,1},{4,6},{5,7},{6,4},{7,5},{8,10},{9,11},{10,... | collective-permute-start | bytes 1572872 | tf_op jit(solution)/shard_map/ppermute | solution.py:191
  81.5 15.0 %copy-start.4 = (bf16[256,1024]{1,0:T(8,128)(2,1)S(1)}, bf16[256,1024]{1,0:T(8,128)(2,1)}, u32[]{:S(2)}) copy-start(bf16[256,1024]{1,0:T(8,128)(2,1)} %copy-done.3) | copy-start | bytes 1572868
  85.3 19.0 %collective-permute-start.12 = (bf16[256,512]{1,0:T(8,128)(2,1)}, bf16[256,512]{1,0:T(8,128)(2,1)}, u32[]{:S(2)}, u32[]{:S(2)}) collective-permute-start(bf16[256,512]{1,0:T(8,128)(2,1)} %get-tuple-element.21), channel_id=1, source_target_pairs={{0,1},{1,0},{2,3},{3,2},{4,5},{5,4},{6,7},{7,6},{8,9},{9,8},{10,11... | collective-permute-start | bytes 786440 | tf_op jit(solution)/shard_map/ppermute | solution.py:191
  85.6 18.7 %collective-permute-start.13 = (bf16[256,512]{1,0:T(8,128)(2,1)}, bf16[256,512]{1,0:T(8,128)(2,1)}, u32[]{:S(2)}, u32[]{:S(2)}) collective-permute-start(bf16[256,512]{1,0:T(8,128)(2,1)} %get-tuple-element.22), channel_id=1, source_target_pairs={{0,2},{1,3},{2,0},{3,1},{4,6},{5,7},{6,4},{7,5},{8,10},{9,11},{10,... | collective-permute-start | bytes 786440 | tf_op jit(solution)/shard_map/ppermute | solution.py:191
  95.1 11.4 %collective-permute-start.14 = (bf16[256,512]{1,0:T(8,128)(2,1)}, bf16[256,512]{1,0:T(8,128)(2,1)}, u32[]{:S(2)}, u32[]{:S(2)}) collective-permute-start(bf16[256,512]{1,0:T(8,128)(2,1)} %get-tuple-element.23), channel_id=1, source_target_pairs={{0,3},{1,2},{2,1},{3,0},{4,7},{5,6},{6,5},{7,4},{8,11},{9,10},{10,... | collective-permute-start | bytes 786440 | tf_op jit(solution)/shard_map/ppermute | solution.py:191
  98.9 17.5 %all-to-all-start.2 = ((bf16[8,256,128]{2,1,0:T(8,128)(2,1)}), bf16[8,256,128]{2,1,0:T(8,128)(2,1)}, u32[]{:S(2)}, u32[]{:S(2)}) async-start(bf16[8,256,128]{2,1,0:T(8,128)(2,1)} %bitcast.34), calls=%async_computation.2 | async-start | bytes 1048576 | tf_op jit(solution)/shard_map/all_to_all | solution.py:200
  111.1 30.3 %collective-permute-start.15 = (bf16[1024,512]{1,0:T(8,128)(2,1)}, bf16[1024,512]{1,0:T(8,128)(2,1)}, u32[]{:S(2)}, u32[]{:S(2)}) collective-permute-start(bf16[1024,512]{1,0:T(8,128)(2,1)} %shard_map.93), channel_id=1, source_target_pairs={{0,4},{4,0},{8,12},{12,8},{16,20},{20,16},{24,28},{28,24},{1,5},{5... | collective-permute-start | bytes 3145736 | tf_op jit(solution)/shard_map/ppermute | solution.py:194
  118.3 66.9 %all-to-all-start.3 = ((bf16[8,256,128]{2,1,0:T(8,128)(2,1)}), bf16[8,256,128]{2,1,0:T(8,128)(2,1)}, u32[]{:S(2)}, u32[]{:S(2)}) async-start(bf16[8,256,128]{2,1,0:T(8,128)(2,1)} %bitcast.35), calls=%async_computation.3 | async-start | bytes 1048576 | tf_op jit(solution)/shard_map/all_to_all | solution.py:200
  128.6 43.2 %copy-start.5 = (bf16[256,1024]{1,0:T(8,128)(2,1)S(1)}, bf16[256,1024]{1,0:T(8,128)(2,1)}, u32[]{:S(2)}) copy-start(bf16[256,1024]{1,0:T(8,128)(2,1)} %copy-done.3) | copy-start | bytes 1572868
  142.8 7.0 %collective-permute-start.16 = (bf16[256,512]{1,0:T(8,128)(2,1)S(1)}, bf16[256,512]{1,0:T(8,128)(2,1)S(1)}, u32[]{:S(2)}, u32[]{:S(2)}) collective-permute-start(bf16[256,512]{1,0:T(8,128)(2,1)S(1)} %get-tuple-element.25), channel_id=1, source_target_pairs={{0,8},{4,12},{8,16},{12,20},{16,24},{20,28},{24,0},{28,4},{1,9},{5... | collective-permute-start | bytes 786440 | tf_op jit(solution)/shard_map/ppermute | solution.py:197
  142.9 20.8 %collective-permute-start.17 = (bf16[256,512]{1,0:T(8,128)(2,1)S(1)}, bf16[256,512]{1,0:T(8,128)(2,1)S(1)}, u32[]{:S(2)}, u32[]{:S(2)}) collective-permute-start(bf16[256,512]{1,0:T(8,128)(2,1)S(1)} %get-tuple-element.26), channel_id=1, source_target_pairs={{0,16},{4,20},{8,24},{12,28},{16,0},{20,4},{24,8},{28,12},{1,17},{... | collective-permute-start | bytes 786440 | tf_op jit(solution)/shard_map/ppermute | solution.py:197
  145.8 23.6 %collective-permute-start.18 = (bf16[256,512]{1,0:T(8,128)(2,1)S(1)}, bf16[256,512]{1,0:T(8,128)(2,1)S(1)}, u32[]{:S(2)}, u32[]{:S(2)}) collective-permute-start(bf16[256,512]{1,0:T(8,128)(2,1)S(1)} %get-tuple-element.27), channel_id=1, source_target_pairs={{0,24},{4,28},{8,0},{12,4},{16,8},{20,12},{24,16},{28,20},{1,25},{... | collective-permute-start | bytes 786440 | tf_op jit(solution)/shard_map/ppermute | solution.py:197
  169.5 6.5 %collective-permute-start.19 = (bf16[256,512]{1,0:T(8,128)(2,1)S(1)}, bf16[256,512]{1,0:T(8,128)(2,1)S(1)}, u32[]{:S(2)}, u32[]{:S(2)}) collective-permute-start(bf16[256,512]{1,0:T(8,128)(2,1)S(1)} %shard_map.95.refs_0_), channel_id=1, source_target_pairs={{0,1},{1,0},{2,3},{3,2},{4,5},{5,4},{6,7},{7,6},{8,9},{9,8},{10,11... | collective-permute-start | bytes 786440 | tf_op jit(solution)/shard_map/ppermute | solution.py:191
  170.1 7.8 %collective-permute-start.20 = (bf16[256,512]{1,0:T(8,128)(2,1)S(1)}, bf16[256,512]{1,0:T(8,128)(2,1)S(1)}, u32[]{:S(2)}, u32[]{:S(2)}) collective-permute-start(bf16[256,512]{1,0:T(8,128)(2,1)S(1)} %shard_map.95.refs_0_), channel_id=1, source_target_pairs={{0,2},{1,3},{2,0},{3,1},{4,6},{5,7},{6,4},{7,5},{8,10},{9,11},{10,... | collective-permute-start | bytes 786440 | tf_op jit(solution)/shard_map/ppermute | solution.py:191
  170.2 13.6 %collective-permute-start.21 = (bf16[256,512]{1,0:T(8,128)(2,1)S(1)}, bf16[256,512]{1,0:T(8,128)(2,1)S(1)}, u32[]{:S(2)}, u32[]{:S(2)}) collective-permute-start(bf16[256,512]{1,0:T(8,128)(2,1)S(1)} %shard_map.95.refs_0_), channel_id=1, source_target_pairs={{0,3},{1,2},{2,1},{3,0},{4,7},{5,6},{6,5},{7,4},{8,11},{9,10},{10,... | collective-permute-start | bytes 786440 | tf_op jit(solution)/shard_map/ppermute | solution.py:191
  185.2 1.0 copy-start.6
  (3 other events, 2.4 us)

commit v2 on v1

--- a/solution.py
+++ b/solution.py
@@ -8,6 +8,7 @@
 from jax.experimental.pallas import tpu as pltpu
 from jax.sharding import PartitionSpec as P
 
+
 DH = 128
 F32 = jnp.float32
 BF16 = jnp.bfloat16
@@ -22,13 +23,14 @@
     return pl.ds(pl.multiple_of(index * width, DH), width)
 
 
-def call(kernel, outs, *args, flops=0):
+def call(kernel, outs, *args, flops=0, scratch=()):
     moved = sum(math.prod(a.shape) * a.dtype.itemsize for a in (*args, *outs))
     return pl.pallas_call(
         kernel,
         out_shape=tuple(outs),
         in_specs=[pl.BlockSpec(memory_space=pltpu.VMEM)] * len(args),
         out_specs=tuple([pl.BlockSpec(memory_space=pltpu.VMEM)] * len(outs)),
+        scratch_shapes=[pltpu.VMEM(a.shape, a.dtype) for a in scratch],
         cost_estimate=pl.CostEstimate(flops=flops, bytes_accessed=moved, transcendentals=0),
         compiler_params=pltpu.CompilerParams(vmem_limit_bytes=min(60 * MIB, 2 * moved + 8 * MIB)),
     )(*args)
@@ -58,18 +60,59 @@
     return source * 2 + lax.rem(d // 2 + half, 2)
 
 
-def kv_kernel(heads, k_ref, v_ref, o_ref):
-    for h in range(heads):
-        cols = pl.ds(h * DH, DH)
-        o_ref[pl.ds(h * DH, DH), :] = dot(k_ref[:, cols], v_ref[:, cols], (0, 0)).astype(BF16)
-
-
-def qg_kernel(heads, shards, inter, qa_ref, qb_ref, g_ref, o_ref):
+def kv_kernel(heads, k_ref, v_ref, *o_refs):
+    y = lax.rem(lax.axis_index("seq"), 2)
+    per = heads // len(o_refs)
+    for part, o_ref in enumerate(o_refs):
+        for j in range(per):
+            h = j if len(o_refs) == 1 else lax.rem(y + part, 2) * per + j
+            cols = lanes(h)
+            o_ref[pl.ds(j * DH, DH), :] = dot(k_ref[:, cols], v_ref[:, cols], (0, 0)).astype(
+                o_ref.dtype
+            )
+
+
+def qg_kernel(heads, shards, inter, qa_ref, qb_ref, g_ref, *o_refs):
+    y = lax.rem(lax.axis_index("seq"), 2)
+    total_ref = o_refs[-1]
     for slot in range(heads):
         ref = (qa_ref, qb_ref)[slot // (heads // 2)]
         h = head_of(slot, shards, inter)
         q = ref[:, pl.ds(slot % (heads // 2) * DH, DH)]
-        o_ref[lanes(h), :] = dot(q, g_ref[:, lanes(h)], (0, 0)).astype(BF16)
+        total_ref[lanes(h), :] = dot(q, g_ref[:, lanes(h)], (0, 0)).astype(total_ref.dtype)
+    half = total_ref.shape[0] // 2
+    for part, o_ref in enumerate(o_refs[:-1]):
+        o_ref[...] = total_ref[lanes(lax.rem(y + part, 2), half), :].astype(o_ref.dtype)
+
+
+def pair_kernel(keep_ref, got_ref, o_ref):
+    o_ref[...] = (keep_ref[...] + got_ref[...].astype(F32)).astype(BF16)
+
+
+def quad_kernel(keep_ref, got_ref, pair_ref, o_ref):
+    o_ref[...] = (
+        keep_ref[...] + got_ref[...].astype(F32) + pair_ref[...].astype(F32)
+    ).astype(BF16)
+
+
+def carry_kernel(backward, keep_ref, got_ref, pair_ref, quad_ref, mine_ref, theirs_ref):
+    s = lax.axis_index("seq")
+    y, z = lax.rem(s, 2), lax.rem(s // 2, 2)
+    later = 0 if backward else 1
+    base = quad_ref[...].astype(F32) + jnp.where(z == later, pair_ref[...].astype(F32), 0.0)
+    mine_ref[...] = (base + jnp.where(y == later, got_ref[...].astype(F32), 0.0)).astype(BF16)
+    theirs_ref[...] = (base + jnp.where(y == later, 0.0, keep_ref[...])).astype(BF16)
+
+
+def whole_state(refs):
+    if len(refs) == 1:
+        return refs[0]
+    mine_ref, other_ref, all_ref = refs
+    y = lax.rem(lax.axis_index("seq"), 2)
+    half = mine_ref.shape[0]
+    all_ref[lanes(y, half), :] = mine_ref[...]
+    all_ref[lanes(1 - y, half), :] = other_ref[...]
+    return all_ref
 
 
 def scan_kernel(count, backward, i_ref, o_ref):
@@ -82,7 +125,9 @@
         total = total + i_ref[block, :].astype(F32)
 
 
-def query_grad_kernel(factor, heads, k_ref, v_ref, g_ref, p_ref, *o_refs):
+def query_grad_kernel(factor, heads, states, k_ref, v_ref, g_ref, *refs):
+    o_refs = refs[states : len(refs) - states + 1]
+    p_ref = whole_state(refs[:states] + refs[len(refs) - states + 1 :])
     mask = causal(k_ref.shape[0])
     d = lax.axis_index("dp")
     per = heads // len(o_refs)
@@ -98,7 +143,9 @@
             ).astype(BF16)
 
 
-def attended_kernel(factor, heads, shards, inter, qa_ref, qb_ref, k_ref, v_ref, p_ref, o_ref):
+def attended_kernel(factor, heads, states, shards, inter, qa_ref, qb_ref, k_ref, v_ref, *refs):
+    o_ref = refs[states]
+    p_ref = whole_state(refs[:states] + refs[states + 1 :])
     mask = causal(k_ref.shape[0])
     for slot in range(heads):
         ref = (qa_ref, qb_ref)[slot // (heads // 2)]
@@ -111,8 +158,10 @@
 
 
 def pair_grad_kernel(
-    factor, heads, shards, inter, qa_ref, qb_ref, k_ref, v_ref, g_ref, s_ref, dk_ref, dv_ref
+    factor, heads, states, shards, inter, qa_ref, qb_ref, k_ref, v_ref, g_ref, *refs
 ):
+    dk_ref, dv_ref = refs[states : states + 2]
+    s_ref = whole_state(refs[:states] + refs[states + 2 :])
     mask = causal(k_ref.shape[0])
     for slot in range(heads):
         ref = (qa_ref, qb_ref)[slot // (heads // 2)]
@@ -142,25 +191,25 @@
             ).astype(BF16)
 
 
-def weight_kernel(count, other, *refs):
+def weight_kernel(count, other, steps, *refs):
     o_ref = refs[-1]
     pairs = len(refs) // 2
     rows = refs[0].shape[1] // count
     s = lax.axis_index("seq")
-    for step in range(count // 2):
+    for place, step in enumerate(steps):
         target = lax.rem(s // 2 + step, count // 2) * 2 + lax.rem(s + other, 2)
         total = None
         for t_ref, g_ref in zip(refs[:pairs], refs[pairs:-1]):
             term = dot(t_ref[:, lanes(target, rows)], g_ref[...], (0, 0))
             total = term if total is None else total + term
-        o_ref[pl.ds(step * rows, rows), :] = total.astype(o_ref.dtype)
-
-
-def fold_kernel(keep_ref, got_ref, *o_refs):
+        o_ref[pl.ds(place * rows, rows), :] = total.astype(o_ref.dtype)
+
+
+def fold_kernel(start, keep_ref, got_ref, *o_refs):
     rows = o_refs[0].shape[0]
-    for step, o_ref in enumerate(o_refs):
-        block = pl.ds(step * rows, rows)
-        o_ref[...] = (keep_ref[block, :] + got_ref[block, :].astype(F32)).astype(o_ref.dtype)
+    for place, o_ref in enumerate(o_refs):
+        kept = keep_ref[pl.ds((start + place) * rows, rows), :]
+        o_ref[...] = (kept + got_ref[pl.ds(place * rows, rows), :].astype(F32)).astype(o_ref.dtype)
 
 
 def sum_kernel(first_ref, *refs):
@@ -183,7 +232,7 @@
     heads = width // DH
     seqs, dps = lax.axis_size("seq"), lax.axis_size("dp")
     factor = 1.0 / math.sqrt(DH * rows * seqs)
-    split = query_weight.shape[1] == 2 * DH and seqs == 8 and dps == 4
+    split = splits(query_weight.shape[1], seqs, dps)
     toks, keys, values, grads = tokens[0], key_rows[0], value_rows[0], out_grad[0]
     state = out((heads * DH, DH), BF16)
 
@@ -200,8 +249,29 @@
         return lax.all_to_all(value, "seq", 0, 0, tiled=True)
 
     def carried(blocks, backward):
-        scan = functools.partial(scan_kernel, seqs, backward)
-        return swap(call(scan, [state], swap(blocks))[0])
+        if not split:
+            scan = functools.partial(scan_kernel, seqs, backward)
+            got = swap(blocks[0])
+            return [swap(call(scan, [state], got)[0])]
+        keep, send = blocks
+        part = out(send.shape, BF16)
+        got = flip_seq(send)
+        pair = call(pair_kernel, [part], keep, got)[0]
+        pair = lax.ppermute(pair, "seq", [(i, i ^ 2) for i in range(seqs)])
+        quad = call(quad_kernel, [part], keep, got, pair)[0]
+        low, high = range(4), range(4, 8)
+        quad = lax.ppermute(
+            quad, "seq", list(zip(high, low) if backward else zip(low, high))
+        )
+        mine, theirs = call(
+            functools.partial(carry_kernel, backward), [part, part], keep, got, pair, quad
+        )
+        return [mine, flip_seq(theirs)]
+
+    half_state = (heads * DH // 2, DH)
+    halves = [out(half_state, F32), out(half_state, BF16)] if split else [state]
+    scratch = [state] if split else []
+    states = len(halves)
 
     group = [toks] + [xor_dp(toks, step) for step in (1, 2) if step < dps]
     if split:
@@ -209,11 +279,14 @@
     else:
         group += [xor_dp(toks, step) for step in range(3, dps)]
 
+    block_kv = call(functools.partial(kv_kernel, heads), halves, keys, values)
+    prefix = carried(block_kv, False)
+
     if split:
         d = lax.axis_index("dp")
         half = model // 2
         piece = lax.dynamic_slice(query_weight, (d % 2 * half, d // 2 * DH), (half, DH))
-        column = [piece] + [turn_seq(piece, step) for step in range(1, seqs // 2)]
+        column = [piece] + [turn_seq(piece, k) for k in range(1, seqs // 2)]
         sides = [flip_seq(value) for value in column]
         near = jnp.stack([jnp.concatenate(two, axis=1) for two in zip(column, sides)])
         far = xor_dp(near, 1)
@@ -235,46 +308,45 @@
         ).astype(BF16)
         pair = (query_rows[:, : width // 2], query_rows[:, width // 2 :])
 
-    block_kv = call(functools.partial(kv_kernel, heads), [state], keys, values)[0]
-    prefix = carried(block_kv, False)
     grad_parts = call(
-        functools.partial(query_grad_kernel, factor, heads),
+        functools.partial(query_grad_kernel, factor, heads, states),
         [out((rows, width // dps), BF16)] * dps,
         keys,
         values,
         grads,
-        prefix,
+        *prefix,
+        scratch=scratch,
     )
     grad_group = [grad_parts[0]] + [xor_dp(grad_parts[step], step) for step in range(1, dps)]
 
     if split:
-        block = model // seqs
-        tall = (model // 2, width // dps)
-        send = call(
-            functools.partial(weight_kernel, seqs, 1),
-            [out(tall, BF16)],
-            *group,
-            *grad_group,
+        block = (model // seqs, width // dps)
+        cuts = ((2, 1), (3, 0))
+        weights = (*group, *grad_group)
+        gots = []
+        for steps in cuts:
+            send = call(
+                functools.partial(weight_kernel, seqs, 1, steps),
+                [out((len(steps) * block[0], block[1]), BF16)],
+                *weights,
+            )[0]
+            gots.append(flip_seq(send))
+        keep = call(
+            functools.partial(weight_kernel, seqs, 0, sum(cuts, ())),
+            [out((model // 2, block[1]), F32)],
+            *weights,
         )[0]
-        got = flip_seq(send)
-        keep = call(
-            functools.partial(weight_kernel, seqs, 0),
-            [out(tall, F32)],
-            *group,
-            *grad_group,
-        )[0]
-        folded = call(
-            fold_kernel,
-            [out((block, tall[1]), F32 if step == 0 else BF16) for step in range(seqs // 2)],
-            keep,
-            got,
-        )
-        share = call(
-            sum_kernel,
-            [out((block, tall[1]), BF16)],
-            folded[0],
-            *[turn_seq(folded[step], step) for step in range(1, seqs // 2)],
-        )[0]
+        terms = []
+        for part, steps in enumerate(cuts):
+            folded = call(
+                functools.partial(fold_kernel, part * len(steps)),
+                [out(block, BF16 if step else F32) for step in steps],
+                keep,
+                gots[part],
+            )
+            for step, value in zip(steps, folded):
+                terms.append(turn_seq(value, step) if step else value)
+        share = call(sum_kernel, [out(block, BF16)], *terms[::-1])[0]
     else:
         share = lax.psum_scatter(
             lax.dot_general(
@@ -295,31 +367,41 @@
     )[0]
 
     block_qg = call(
-        functools.partial(qg_kernel, heads, seqs, split), [state], *pair, grads
-    )[0]
+        functools.partial(qg_kernel, heads, seqs, split),
+        halves,
+        *pair,
+        grads,
+        scratch=[out((heads * DH, DH), F32)] if split else [],
+    )
     suffix = carried(block_qg, True)
     attended = call(
-        functools.partial(attended_kernel, factor, heads, seqs, split),
+        functools.partial(attended_kernel, factor, heads, states, seqs, split),
         [out((rows, width), BF16)],
         *pair,
         keys,
         values,
-        prefix,
+        *prefix,
+        scratch=scratch,
     )[0]
     key_grad, value_grad = call(
-        functools.partial(pair_grad_kernel, factor, heads, seqs, split),
+        functools.partial(pair_grad_kernel, factor, heads, states, seqs, split),
         [out((rows, width), BF16)] * 2,
         *pair,
         keys,
         values,
         grads,
-        suffix,
+        *suffix,
+        scratch=scratch,
     )
     return (attended[None], key_grad[None], value_grad[None], weight_grad)
 
 
+def splits(columns, seqs, dps):
+    return columns == 2 * DH and seqs == 8 and dps == 4
+
+
 def solution(mesh):
-    return jax.shard_map(
+    step = jax.shard_map(
         body,
         mesh=mesh,
         in_specs=(
@@ -337,3 +419,6 @@
         ),
         check_vma=False,
     )
+    if dict(mesh.shape) == {"seq": 8, "dp": 4}:
+        return step
+    return step

time: 195 us -> 201 us (1.031)
  waiting for transfers between devices: 104 us -> 143 us
  Pallas kernels: 37.9 us -> 20.4 us
  starting transfers between devices: 45.3 us -> 33.5 us
  local copies, waits for them, and re-layouts: 4.43 us -> 1 us
    all_to_all x4 -> x0, starting transfers between devices: 24.5 us -> none  [swap(): return lax.all_to_all(value, 'seq', 0, 0, tiled=True)]
    ppermute x5 -> x10, waiting for transfers between devices: 22.1 us -> 45.2 us  [flip_seq(): return lax.ppermute(value, 'seq', [(i, i ^ 1) for i in range(seqs)])]
    ppermute x11, waiting for transfers between devices: 21.2 us -> 41.4 us  [xor_dp(): return lax.ppermute(value, 'dp', [(i, i ^ step) for i in range(dps)])]
    pallas_call x13 -> x19, Pallas kernels: 37.9 us -> 20.4 us  [call(): pl.pallas_call(kernel, out_shape=tuple(outs), in_specs=[pl.BlockSpec(memo...]
    all_to_all x4 -> x0, waiting for transfers between devices: 16.7 us -> none  [swap(): return lax.all_to_all(value, 'seq', 0, 0, tiled=True)]
    ppermute x0 -> x4, waiting for transfers between devices: none -> 10.3 us  [the longest x2 9.17 us: carried(): lax.ppermute(quad, 'seq', list(zip(high, low) if backward else zip(low, h...]
    ppermute x0 -> x4, starting transfers between devices: none -> 6.32 us  [the longest x2 6.18 us: carried(): lax.ppermute(quad, 'seq', list(zip(high, low) if backward else zip(low, h...]
    ppermute x5 -> x10, starting transfers between devices: 1.22 us -> 5.66 us  [flip_seq(): return lax.ppermute(value, 'seq', [(i, i ^ 1) for i in range(seqs)])]
  transfers between devices with their start and end apart: 26 -> 31, of which waited for: 16 -> 18; matrix products, arithmetic and copies ran while one was open for 0% -> 0% of each run, Pallas kernels for 16% -> 7%
where the time goes in v2:
time: 201 us; the launch traced here: 199 us
  waiting for transfers between devices  143 us (71%)
  starting transfers between devices  33.5 us (17%)
  Pallas kernels  20.4 us (10%)
    ppermute x6, waiting for transfers between devices, turn_seq(): lax.ppermute(value, 'seq', [(i, (i + 2 * step) % seqs) for i in range(seq...  46 us
    ppermute x10, waiting for transfers between devices, flip_seq(): return lax.ppermute(value, 'seq', [(i, i ^ 1) for i in range(seqs)])  45.2 us
    ppermute x11, waiting for transfers between devices, xor_dp(): return lax.ppermute(value, 'dp', [(i, i ^ step) for i in range(dps)])  41.4 us
    pallas_call x19, Pallas kernels, call(): pl.pallas_call(kernel, out_shape=tuple(outs), in_specs=[pl.BlockSpec(memo...  20.4 us
    ppermute x11, starting transfers between devices, xor_dp(): return lax.ppermute(value, 'dp', [(i, i ^ step) for i in range(dps)])  12.9 us
    ppermute x2, waiting for transfers between devices, carried(): lax.ppermute(quad, 'seq', list(zip(high, low) if backward else zip(low, h...  9.17 us
    ppermute x6, starting transfers between devices, turn_seq(): lax.ppermute(value, 'seq', [(i, (i + 2 * step) % seqs) for i in range(seq...  8.62 us
    ppermute x2, starting transfers between devices, carried(): lax.ppermute(quad, 'seq', list(zip(high, low) if backward else zip(low, h...  6.18 us
  transfers between devices with their start and end apart: 31, of which 18 were waited for; matrix products, arithmetic and copies ran while one was open for 0% of the time, Pallas kernels for 7%

profile of v2, /device:TPU:15, one launch (start us, length us, event | category | flops | bytes accessed | tf_op | source)
XLA Modules:
  0.0 199.3 jit_solution(15124592439808620187)
XLA Ops:
  4.1 1.4 collective-permute-start.6
  5.7 3.2 %collective-permute-done.2 = bf16[1024,128]{1,0:T(8,128)(2,1)S(1)} collective-permute-done((bf16[1024,128]{1,0:T(8,128)(2,1)S(1)}, bf16[1024,128]{1,0:T(8,128)(2,1)S(1)}, u32[]{:S(2)}, u32[]{:S(2)}) %collective-permute-start.2) | collective-permute-done | bytes 262176 | tf_op jit(solution)/shard_map/ppermute | solution.py:246
  9.1 15.7 %collective-permute-done.4 = bf16[1024,128]{1,0:T(8,128)(2,1)S(1)} collective-permute-done((bf16[1024,128]{1,0:T(8,128)(2,1)S(1)}, bf16[1024,128]{1,0:T(8,128)(2,1)S(1)}, u32[]{:S(2)}, u32[]{:S(2)}) %collective-permute-start.4) | collective-permute-done | bytes 262176 | tf_op jit(solution)/shard_map/ppermute | solution.py:246
  25.1 2.6 %collective-permute-done.6 = bf16[1024,128]{1,0:T(8,128)(2,1)S(1)} collective-permute-done((bf16[1024,128]{1,0:T(8,128)(2,1)S(1)}, bf16[1024,128]{1,0:T(8,128)(2,1)S(1)}, u32[]{:S(2)}, u32[]{:S(2)}) %collective-permute-start.6) | collective-permute-done | bytes 262176 | tf_op jit(solution)/shard_map/ppermute | solution.py:246
  28.0 3.8 %collective-permute-done.5 = bf16[1024,128]{1,0:T(8,128)(2,1)S(1)} collective-permute-done((bf16[1024,128]{1,0:T(8,128)(2,1)S(1)}, bf16[1024,128]{1,0:T(8,128)(2,1)S(1)}, u32[]{:S(2)}, u32[]{:S(2)}) %collective-permute-start.5) | collective-permute-done | bytes 262176 | tf_op jit(solution)/shard_map/ppermute | solution.py:243
  31.8 5.6 %collective-permute-done.7 = bf16[1024,128]{1,0:T(8,128)(2,1)S(1)} collective-permute-done((bf16[1024,128]{1,0:T(8,128)(2,1)S(1)}, bf16[1024,128]{1,0:T(8,128)(2,1)S(1)}, u32[]{:S(2)}, u32[]{:S(2)}) %collective-permute-start.7) | collective-permute-done | bytes 262176 | tf_op jit(solution)/shard_map/ppermute | solution.py:243
  37.8 2.1 %collective-permute-start.8 = (bf16[4,1024,256]{2,1,0:T(8,128)(2,1)S(1)}, bf16[4,1024,256]{2,1,0:T(8,128)(2,1)S(1)}, u32[]{:S(2)}, u32[]{:S(2)}) collective-permute-start(bf16[4,1024,256]{2,1,0:T(8,128)(2,1)S(1)} %pad_maximum_fusion.near_ref), channel_id=1, source_target_pairs={{0,1},{1,0},{2,3},{3,2},{4,5},{5,4},{6,7},{7,6},{8,9},{9,8},{10,11... | collective-permute-start | bytes 6291464 | tf_op jit(solution)/shard_map/ppermute | solution.py:240
  41.3 1.5 collective-permute-start.18
  42.8 4.9 %collective-permute-done.10.got_ref = bf16[1024,128]{1,0:T(8,128)(2,1)S(1)} collective-permute-done((bf16[1024,128]{1,0:T(8,128)(2,1)S(1)}, bf16[1024,128]{1,0:T(8,128)(2,1)S(1)}, u32[]{:S(2)}, u32[]{:S(2)}) %collective-permute-start.10) | collective-permute-done | bytes 262176 | tf_op jit(solution)/shard_map/ppermute | solution.py:243
  47.8 15.9 %collective-permute-done.theirs_ref.refs_2_ = bf16[256,2048]{1,0:T(8,128)(2,1)S(1)} collective-permute-done((bf16[256,2048]{1,0:T(8,128)(2,1)S(1)}, bf16[256,2048]{1,0:T(8,128)(2,1)S(1)}, u32[]{:S(2)}, u32[]{:S(2)}) %collective-permute-start) | collective-permute-done | bytes 1048608 | tf_op jit(solution)/shard_map/ppermute | solution.py:240
  63.8 1.7 collective-permute-start.19
  65.6 4.7 %collective-permute-start.12 = (bf16[1024,128]{1,0:T(8,128)(2,1)S(1)}, bf16[1024,128]{1,0:T(8,128)(2,1)S(1)}, u32[]{:S(2)}, u32[]{:S(2)}) collective-permute-start(bf16[1024,128]{1,0:T(8,128)(2,1)S(1)} %shard_map.87), channel_id=1, source_target_pairs={{0,16},{4,20},{8,24},{12,28},{1,17},{5,21},{9,25},{13,29},{2,18},{... | collective-permute-start | bytes 786440 | tf_op jit(solution)/shard_map/ppermute | solution.py:263
  70.3 9.2 %collective-permute-done.12.quad_ref = bf16[1024,128]{1,0:T(8,128)(2,1)S(1)} collective-permute-done((bf16[1024,128]{1,0:T(8,128)(2,1)S(1)}, bf16[1024,128]{1,0:T(8,128)(2,1)S(1)}, u32[]{:S(2)}, u32[]{:S(2)}) %collective-permute-start.12) | collective-permute-done | bytes 262176 | tf_op jit(solution)/shard_map/ppermute | solution.py:263
  80.0 2.3 %shard_map.84 = (bf16[256,1024]{1,0:T(8,128)(2,1)S(1)}, bf16[256,1024]{1,0:T(8,128)(2,1)S(1)}) custom-call(bf16[256,2048]{1,0:T(8,128)(2,1)S(1)} %bitcast.28, bf16[256,2048]{1,0:T(8,128)(2,1)S(1)} %collective-permute-done.theirs_ref.refs_2_, bf16[4,1024,256]{2,1,0:T(8,128)(2,1)S(1)} %pad_maximum_fusion.near_ref, ...), custom_call_target="tpu_custom_call" | custom-call | flops 2147483648 | bytes 7340032 | tf_op jit(solution)/shard_map/pallas_call | solution.py:28
  82.6 4.5 %collective-permute-done.13.refs_1_ = bf16[1024,128]{1,0:T(8,128)(2,1)S(1)} collective-permute-done((bf16[1024,128]{1,0:T(8,128)(2,1)S(1)}, bf16[1024,128]{1,0:T(8,128)(2,1)S(1)}, u32[]{:S(2)}, u32[]{:S(2)}) %collective-permute-start.13) | collective-permute-done | bytes 262176 | tf_op jit(solution)/shard_map/ppermute | solution.py:243
  87.1 2.0 %shard_map.95 = (bf16[256,512]{1,0:T(8,128)(2,1)S(1)}, bf16[256,512]{1,0:T(8,128)(2,1)S(1)}, bf16[256,512]{1,0:T(8,128)(2,1)S(1)}, bf16[256,512]{1,0:T(8,128)(2,1)S(1)}) custom-call(bf16[256,2048]{1,0:T(8,128)(2,1)S(1)} %bitcast.16, bf16[256,2048]{1,0:T(8,128)(2,1)S(1)} %bitcast.20, bf16[256,2048]{1,0:T(8,128)(2,1)S(1)} %bitcast.23, ...), custom_call_target="tpu_custom_call" | custom-call | bytes 4718592 | tf_op jit(solution)/shard_map/pallas_call | solution.py:28
  90.8 1.5 collective-permute-start.22
  92.2 8.5 %collective-permute-done.21.refs_6_ = bf16[256,512]{1,0:T(8,128)(2,1)S(1)} collective-permute-done((bf16[256,512]{1,0:T(8,128)(2,1)S(1)}, bf16[256,512]{1,0:T(8,128)(2,1)S(1)}, u32[]{:S(2)}, u32[]{:S(2)}) %collective-permute-start.21) | collective-permute-done | bytes 262176 | tf_op jit(solution)/shard_map/ppermute | solution.py:240
  100.7 6.5 %collective-permute-done.22.refs_7_ = bf16[256,512]{1,0:T(8,128)(2,1)S(1)} collective-permute-done((bf16[256,512]{1,0:T(8,128)(2,1)S(1)}, bf16[256,512]{1,0:T(8,128)(2,1)S(1)}, u32[]{:S(2)}, u32[]{:S(2)}) %collective-permute-start.22) | collective-permute-done | bytes 262176 | tf_op jit(solution)/shard_map/ppermute | solution.py:240
  112.3 26.5 %collective-permute-done.14.got_ref = bf16[1024,128]{1,0:T(8,128)(2,1)S(1)} collective-permute-done((bf16[1024,128]{1,0:T(8,128)(2,1)S(1)}, bf16[1024,128]{1,0:T(8,128)(2,1)S(1)}, u32[]{:S(2)}, u32[]{:S(2)}) %collective-permute-start.14) | collective-permute-done | bytes 262176 | tf_op jit(solution)/shard_map/ppermute | solution.py:243
  140.3 3.5 %collective-permute-start.26 = (bf16[256,512]{1,0:T(8,128)(2,1)S(1)}, bf16[256,512]{1,0:T(8,128)(2,1)S(1)}, u32[]{:S(2)}, u32[]{:S(2)}) collective-permute-start(bf16[256,512]{1,0:T(8,128)(2,1)S(1)} %get-tuple-element.42), channel_id=1, source_target_pairs={{0,8},{4,12},{8,16},{12,20},{16,24},{20,28},{24,0},{28,4},{1,9},{5... | collective-permute-start | bytes 786440 | tf_op jit(solution)/shard_map/ppermute | solution.py:246
  146.4 1.5 collective-permute-start.16
  147.9 4.1 %collective-permute-done.26.refs_1_ = bf16[256,512]{1,0:T(8,128)(2,1)S(1)} collective-permute-done((bf16[256,512]{1,0:T(8,128)(2,1)S(1)}, bf16[256,512]{1,0:T(8,128)(2,1)S(1)}, u32[]{:S(2)}, u32[]{:S(2)}) %collective-permute-start.26) | collective-permute-done | bytes 262176 | tf_op jit(solution)/shard_map/ppermute | solution.py:246
  152.0 13.7 %collective-permute-done.27.refs_2_ = bf16[256,512]{1,0:T(8,128)(2,1)S(1)} collective-permute-done((bf16[256,512]{1,0:T(8,128)(2,1)S(1)}, bf16[256,512]{1,0:T(8,128)(2,1)S(1)}, u32[]{:S(2)}, u32[]{:S(2)}) %collective-permute-start.27) | collective-permute-done | bytes 262176 | tf_op jit(solution)/shard_map/ppermute | solution.py:246
  165.7 6.8 %collective-permute-done.24.refs_0_ = bf16[256,512]{1,0:T(8,128)(2,1)S(1)} collective-permute-done((bf16[256,512]{1,0:T(8,128)(2,1)S(1)}, bf16[256,512]{1,0:T(8,128)(2,1)S(1)}, u32[]{:S(2)}, u32[]{:S(2)}) %collective-permute-start.24) | collective-permute-done | bytes 262176 | tf_op jit(solution)/shard_map/ppermute | solution.py:246
  172.5 2.2 %collective-permute-start.28 = (bf16[256,512]{1,0:T(8,128)(2,1)S(1)}, bf16[256,512]{1,0:T(8,128)(2,1)S(1)}, u32[]{:S(2)}, u32[]{:S(2)}) collective-permute-start(bf16[256,512]{1,0:T(8,128)(2,1)S(1)} %shard_map.101.refs_0_), channel_id=1, source_target_pairs={{0,1},{1,0},{2,3},{3,2},{4,5},{5,4},{6,7},{7,6},{8,9},{9,8},{10,11... | collective-permute-start | bytes 786440 | tf_op jit(solution)/shard_map/ppermute | solution.py:240
  175.0 1.4 collective-permute-start.30
  177.9 4.6 %collective-permute-done.29.refs_2_ = bf16[256,512]{1,0:T(8,128)(2,1)S(1)} collective-permute-done((bf16[256,512]{1,0:T(8,128)(2,1)S(1)}, bf16[256,512]{1,0:T(8,128)(2,1)S(1)}, u32[]{:S(2)}, u32[]{:S(2)}) %collective-permute-start.29) | collective-permute-done | bytes 262176 | tf_op jit(solution)/shard_map/ppermute | solution.py:240
  182.5 5.9 %collective-permute-done.30.refs_3_ = bf16[256,512]{1,0:T(8,128)(2,1)S(1)} collective-permute-done((bf16[256,512]{1,0:T(8,128)(2,1)S(1)}, bf16[256,512]{1,0:T(8,128)(2,1)S(1)}, u32[]{:S(2)}, u32[]{:S(2)}) %collective-permute-start.30) | collective-permute-done | bytes 262176 | tf_op jit(solution)/shard_map/ppermute | solution.py:240
  188.4 1.5 shard_map.102
  189.8 3.0 %shard_map.89 = bf16[256,2048]{1,0:T(8,128)(2,1)} custom-call(bf16[256,1024]{1,0:T(8,128)(2,1)S(1)} %get-tuple-element.24.qa_ref, bf16[256,1024]{1,0:T(8,128)(2,1)S(1)} %collective-permute-done.9.qb_ref, bf16[256,2048]{1,0:T(8,128)(2,1)S(1)} %bitcast.17, bf16[256,2048]{1,0:T(8,128)(2,1)S(1)} %bitcast.21, bf16[1024,128]{1,0:T(8,128)(2,1)S(1)} %get-tuple-element.28.refs_0_, ...), custom_call_target="tpu_custom_call" | custom-call | bytes 4718592 | tf_op jit(solution)/shard_map/pallas_call | solution.py:28
  192.8 6.5 %shard_map.94 = (bf16[256,2048]{1,0:T(8,128)(2,1)}, bf16[256,2048]{1,0:T(8,128)(2,1)}) custom-call(bf16[256,1024]{1,0:T(8,128)(2,1)S(1)} %get-tuple-element.24.qa_ref, bf16[256,1024]{1,0:T(8,128)(2,1)S(1)} %collective-permute-done.9.qb_ref, bf16[256,2048]{1,0:T(8,128)(2,1)S(1)} %bitcast.18, bf16[256,2048]{1,0:T(8,128)(2,1)S(1)} %bitcast.22, ...), custom_call_target="tpu_custom_call" | custom-call | bytes 6815744 | tf_op jit(solution)/shard_map/pallas_call | solution.py:28
  (63 shorter events, 19.9 us)
Async XLA Ops:
  1.6 7.2 %collective-permute-start.2 = (bf16[1024,128]{1,0:T(8,128)(2,1)S(1)}, bf16[1024,128]{1,0:T(8,128)(2,1)S(1)}, u32[]{:S(2)}, u32[]{:S(2)}) collective-permute-start(bf16[1024,128]{1,0:T(8,128)(2,1)S(1)} %dynamic_slice.3), channel_id=1, source_target_pairs={{0,8},{4,12},{8,16},{12,20},{16,24},{20,28},{24,0},{28,4},{1,9},{5... | collective-permute-start | bytes 786440 | tf_op jit(solution)/shard_map/ppermute | solution.py:246
  3.0 21.8 %collective-permute-start.4 = (bf16[1024,128]{1,0:T(8,128)(2,1)S(1)}, bf16[1024,128]{1,0:T(8,128)(2,1)S(1)}, u32[]{:S(2)}, u32[]{:S(2)}) collective-permute-start(bf16[1024,128]{1,0:T(8,128)(2,1)S(1)} %dynamic_slice.3), channel_id=1, source_target_pairs={{0,16},{4,20},{8,24},{12,28},{16,0},{20,4},{24,8},{28,12},{1,17},{... | collective-permute-start | bytes 786440 | tf_op jit(solution)/shard_map/ppermute | solution.py:246
  4.1 23.6 %collective-permute-start.6 = (bf16[1024,128]{1,0:T(8,128)(2,1)S(1)}, bf16[1024,128]{1,0:T(8,128)(2,1)S(1)}, u32[]{:S(2)}, u32[]{:S(2)}) collective-permute-start(bf16[1024,128]{1,0:T(8,128)(2,1)S(1)} %dynamic_slice.3), channel_id=1, source_target_pairs={{0,24},{4,28},{8,0},{12,4},{16,8},{20,12},{24,16},{28,20},{1,25},{... | collective-permute-start | bytes 786440 | tf_op jit(solution)/shard_map/ppermute | solution.py:246
  5.5 22.4 %collective-permute-start.1 = (bf16[1024,128]{1,0:T(8,128)(2,1)S(1)}, bf16[1024,128]{1,0:T(8,128)(2,1)S(1)}, u32[]{:S(2)}, u32[]{:S(2)}) collective-permute-start(bf16[1024,128]{1,0:T(8,128)(2,1)S(1)} %dynamic_slice.3), channel_id=1, source_target_pairs={{0,4},{4,0},{8,12},{12,8},{16,20},{20,16},{24,28},{28,24},{1,5},{5... | collective-permute-start | bytes 786440 | tf_op jit(solution)/shard_map/ppermute | solution.py:243
  8.9 19.1 %collective-permute-start.3 = (bf16[1024,128]{1,0:T(8,128)(2,1)S(1)}, bf16[1024,128]{1,0:T(8,128)(2,1)S(1)}, u32[]{:S(2)}, u32[]{:S(2)}) collective-permute-start(bf16[1024,128]{1,0:T(8,128)(2,1)S(1)} %collective-permute-done.2), channel_id=1, source_target_pairs={{0,4},{4,0},{8,12},{12,8},{16,20},{20,16},{24,28},{28,24},{1,5},{5... | collective-permute-start | bytes 786440 | tf_op jit(solution)/shard_map/ppermute | solution.py:243
  24.8 7.0 %collective-permute-start.5 = (bf16[1024,128]{1,0:T(8,128)(2,1)S(1)}, bf16[1024,128]{1,0:T(8,128)(2,1)S(1)}, u32[]{:S(2)}, u32[]{:S(2)}) collective-permute-start(bf16[1024,128]{1,0:T(8,128)(2,1)S(1)} %collective-permute-done.4), channel_id=1, source_target_pairs={{0,4},{4,0},{8,12},{12,8},{16,20},{20,16},{24,28},{28,24},{1,5},{5... | collective-permute-start | bytes 786440 | tf_op jit(solution)/shard_map/ppermute | solution.py:243
  27.7 9.7 %collective-permute-start.7 = (bf16[1024,128]{1,0:T(8,128)(2,1)S(1)}, bf16[1024,128]{1,0:T(8,128)(2,1)S(1)}, u32[]{:S(2)}, u32[]{:S(2)}) collective-permute-start(bf16[1024,128]{1,0:T(8,128)(2,1)S(1)} %collective-permute-done.6), channel_id=1, source_target_pairs={{0,4},{4,0},{8,12},{12,8},{16,20},{20,16},{24,28},{28,24},{1,5},{5... | collective-permute-start | bytes 786440 | tf_op jit(solution)/shard_map/ppermute | solution.py:243
  37.8 42.2 %collective-permute-start.8 = (bf16[4,1024,256]{2,1,0:T(8,128)(2,1)S(1)}, bf16[4,1024,256]{2,1,0:T(8,128)(2,1)S(1)}, u32[]{:S(2)}, u32[]{:S(2)}) collective-permute-start(bf16[4,1024,256]{2,1,0:T(8,128)(2,1)S(1)} %pad_maximum_fusion.near_ref), channel_id=1, source_target_pairs={{0,1},{1,0},{2,3},{3,2},{4,5},{5,4},{6,7},{7,6},{8,9},{9,8},{10,11... | collective-permute-start | bytes 6291464 | tf_op jit(solution)/shard_map/ppermute | solution.py:240
  39.9 23.9 %collective-permute-start = (bf16[256,2048]{1,0:T(8,128)(2,1)S(1)}, bf16[256,2048]{1,0:T(8,128)(2,1)S(1)}, u32[]{:S(2)}, u32[]{:S(2)}) collective-permute-start(bf16[256,2048]{1,0:T(8,128)(2,1)S(1)} %bitcast.26), channel_id=1, source_target_pairs={{0,2},{1,3},{2,0},{3,1},{4,6},{5,7},{6,4},{7,5},{8,10},{9,11},{10,... | collective-permute-start | bytes 3145736 | tf_op jit(solution)/shard_map/ppermute | solution.py:240
  41.0 6.7 %collective-permute-start.10 = (bf16[1024,128]{1,0:T(8,128)(2,1)S(1)}, bf16[1024,128]{1,0:T(8,128)(2,1)S(1)}, u32[]{:S(2)}, u32[]{:S(2)}) collective-permute-start(bf16[1024,128]{1,0:T(8,128)(2,1)S(1)} %get-tuple-element.27), channel_id=1, source_target_pairs={{0,4},{4,0},{8,12},{12,8},{16,20},{20,16},{24,28},{28,24},{1,5},{5... | collective-permute-start | bytes 786440 | tf_op jit(solution)/shard_map/ppermute | solution.py:243
  41.3 49.5 %collective-permute-start.18 = (bf16[256,2048]{1,0:T(8,128)(2,1)S(1)}, bf16[256,2048]{1,0:T(8,128)(2,1)S(1)}, u32[]{:S(2)}, u32[]{:S(2)}) collective-permute-start(bf16[256,2048]{1,0:T(8,128)(2,1)S(1)} %bitcast.27), channel_id=1, source_target_pairs={{0,1},{1,0},{2,3},{3,2},{4,5},{5,4},{6,7},{7,6},{8,9},{9,8},{10,11... | collective-permute-start | bytes 3145736 | tf_op jit(solution)/shard_map/ppermute | solution.py:240
  47.8 17.7 %collective-permute-start.11 = (bf16[1024,128]{1,0:T(8,128)(2,1)S(1)}, bf16[1024,128]{1,0:T(8,128)(2,1)S(1)}, u32[]{:S(2)}, u32[]{:S(2)}) collective-permute-start(bf16[1024,128]{1,0:T(8,128)(2,1)S(1)} %shard_map.86), channel_id=1, source_target_pairs={{0,8},{4,12},{8,0},{12,4},{16,24},{20,28},{24,16},{28,20},{1,9},{5... | collective-permute-start | bytes 786440 | tf_op jit(solution)/shard_map/ppermute | solution.py:260
  63.8 43.5 %collective-permute-start.19 = (bf16[256,2048]{1,0:T(8,128)(2,1)S(1)}, bf16[256,2048]{1,0:T(8,128)(2,1)S(1)}, u32[]{:S(2)}, u32[]{:S(2)}) collective-permute-start(bf16[256,2048]{1,0:T(8,128)(2,1)S(1)} %collective-permute-done.theirs_ref.refs_2_), channel_id=1, source_target_pairs={{0,1},{1,0},{2,3},{3,2},{4,5},{5,4},{6,7},{7,6},{8,9},{9,8},{10,11... | collective-permute-start | bytes 3145736 | tf_op jit(solution)/shard_map/ppermute | solution.py:240
  65.6 13.9 %collective-permute-start.12 = (bf16[1024,128]{1,0:T(8,128)(2,1)S(1)}, bf16[1024,128]{1,0:T(8,128)(2,1)S(1)}, u32[]{:S(2)}, u32[]{:S(2)}) collective-permute-start(bf16[1024,128]{1,0:T(8,128)(2,1)S(1)} %shard_map.87), channel_id=1, source_target_pairs={{0,16},{4,20},{8,24},{12,28},{1,17},{5,21},{9,25},{13,29},{2,18},{... | collective-permute-start | bytes 786440 | tf_op jit(solution)/shard_map/ppermute | solution.py:263
  79.7 7.5 %copy-start.2 = (bf16[1,256,2048]{2,1,0:T(8,128)(2,1)S(1)}, bf16[1,256,2048]{2,1,0:T(8,128)(2,1)}, u32[]{:S(2)}) copy-start(bf16[1,256,2048]{2,1,0:T(8,128)(2,1)} %param.9) | copy-start | bytes 3145732
  79.7 7.5 %collective-permute-start.13 = (bf16[1024,128]{1,0:T(8,128)(2,1)S(1)}, bf16[1024,128]{1,0:T(8,128)(2,1)S(1)}, u32[]{:S(2)}, u32[]{:S(2)}) collective-permute-start(bf16[1024,128]{1,0:T(8,128)(2,1)S(1)} %get-tuple-element.29), channel_id=1, source_target_pairs={{0,4},{4,0},{8,12},{12,8},{16,20},{20,16},{24,28},{28,24},{1,5},{5... | collective-permute-start | bytes 786440 | tf_op jit(solution)/shard_map/ppermute | solution.py:243
  82.3 28.1 %collective-permute-start.9 = (bf16[256,1024]{1,0:T(8,128)(2,1)S(1)}, bf16[256,1024]{1,0:T(8,128)(2,1)S(1)}, u32[]{:S(2)}, u32[]{:S(2)}) collective-permute-start(bf16[256,1024]{1,0:T(8,128)(2,1)S(1)} %get-tuple-element.25), channel_id=1, source_target_pairs={{0,2},{1,3},{2,0},{3,1},{4,6},{5,7},{6,4},{7,5},{8,10},{9,11},{10,... | collective-permute-start | bytes 1572872 | tf_op jit(solution)/shard_map/ppermute | solution.py:240
  89.1 3.1 %collective-permute-start.20 = (bf16[256,512]{1,0:T(8,128)(2,1)S(1)}, bf16[256,512]{1,0:T(8,128)(2,1)S(1)}, u32[]{:S(2)}, u32[]{:S(2)}) collective-permute-start(bf16[256,512]{1,0:T(8,128)(2,1)S(1)} %get-tuple-element.37), channel_id=1, source_target_pairs={{0,1},{1,0},{2,3},{3,2},{4,5},{5,4},{6,7},{7,6},{8,9},{9,8},{10,11... | collective-permute-start | bytes 786440 | tf_op jit(solution)/shard_map/ppermute | solution.py:240
  90.5 10.2 %collective-permute-start.21 = (bf16[256,512]{1,0:T(8,128)(2,1)S(1)}, bf16[256,512]{1,0:T(8,128)(2,1)S(1)}, u32[]{:S(2)}, u32[]{:S(2)}) collective-permute-start(bf16[256,512]{1,0:T(8,128)(2,1)S(1)} %get-tuple-element.38), channel_id=1, source_target_pairs={{0,2},{1,3},{2,0},{3,1},{4,6},{5,7},{6,4},{7,5},{8,10},{9,11},{10,... | collective-permute-start | bytes 786440 | tf_op jit(solution)/shard_map/ppermute | solution.py:240
  90.8 16.5 %collective-permute-start.22 = (bf16[256,512]{1,0:T(8,128)(2,1)S(1)}, bf16[256,512]{1,0:T(8,128)(2,1)S(1)}, u32[]{:S(2)}, u32[]{:S(2)}) collective-permute-start(bf16[256,512]{1,0:T(8,128)(2,1)S(1)} %get-tuple-element.39), channel_id=1, source_target_pairs={{0,3},{1,2},{2,1},{3,0},{4,7},{5,6},{6,5},{7,4},{8,11},{9,10},{10,... | collective-permute-start | bytes 786440 | tf_op jit(solution)/shard_map/ppermute | solution.py:240
  108.0 32.2 %collective-permute-start.25 = (bf16[512,512]{1,0:T(8,128)(2,1)S(1)}, bf16[512,512]{1,0:T(8,128)(2,1)S(1)}, u32[]{:S(2)}, u32[]{:S(2)}) collective-permute-start(bf16[512,512]{1,0:T(8,128)(2,1)S(1)} %shard_map.99), channel_id=1, source_target_pairs={{0,4},{4,0},{8,12},{12,8},{16,20},{20,16},{24,28},{28,24},{1,5},{5... | collective-permute-start | bytes 1572872 | tf_op jit(solution)/shard_map/ppermute | solution.py:243
  110.1 33.8 %collective-permute-start.23 = (bf16[512,512]{1,0:T(8,128)(2,1)S(1)}, bf16[512,512]{1,0:T(8,128)(2,1)S(1)}, u32[]{:S(2)}, u32[]{:S(2)}) collective-permute-start(bf16[512,512]{1,0:T(8,128)(2,1)S(1)} %shard_map.97), channel_id=1, source_target_pairs={{0,4},{4,0},{8,12},{12,8},{16,20},{20,16},{24,28},{28,24},{1,5},{5... | collective-permute-start | bytes 1572872 | tf_op jit(solution)/shard_map/ppermute | solution.py:243
  111.0 27.8 %collective-permute-start.14 = (bf16[1024,128]{1,0:T(8,128)(2,1)S(1)}, bf16[1024,128]{1,0:T(8,128)(2,1)S(1)}, u32[]{:S(2)}, u32[]{:S(2)}) collective-permute-start(bf16[1024,128]{1,0:T(8,128)(2,1)S(1)} %get-tuple-element.31), channel_id=1, source_target_pairs={{0,4},{4,0},{8,12},{12,8},{16,20},{20,16},{24,28},{28,24},{1,5},{5... | collective-permute-start | bytes 786440 | tf_op jit(solution)/shard_map/ppermute | solution.py:243
  138.8 7.5 %collective-permute-start.15 = (bf16[1024,128]{1,0:T(8,128)(2,1)S(1)}, bf16[1024,128]{1,0:T(8,128)(2,1)S(1)}, u32[]{:S(2)}, u32[]{:S(2)}) collective-permute-start(bf16[1024,128]{1,0:T(8,128)(2,1)S(1)} %shard_map.91), channel_id=1, source_target_pairs={{0,8},{4,12},{8,0},{12,4},{16,24},{20,28},{24,16},{28,20},{1,9},{5... | collective-permute-start | bytes 786440 | tf_op jit(solution)/shard_map/ppermute | solution.py:260
  140.3 11.6 %collective-permute-start.26 = (bf16[256,512]{1,0:T(8,128)(2,1)S(1)}, bf16[256,512]{1,0:T(8,128)(2,1)S(1)}, u32[]{:S(2)}, u32[]{:S(2)}) collective-permute-start(bf16[256,512]{1,0:T(8,128)(2,1)S(1)} %get-tuple-element.42), channel_id=1, source_target_pairs={{0,8},{4,12},{8,16},{12,20},{16,24},{20,28},{24,0},{28,4},{1,9},{5... | collective-permute-start | bytes 786440 | tf_op jit(solution)/shard_map/ppermute | solution.py:246
  143.8 21.8 %collective-permute-start.27 = (bf16[256,512]{1,0:T(8,128)(2,1)S(1)}, bf16[256,512]{1,0:T(8,128)(2,1)S(1)}, u32[]{:S(2)}, u32[]{:S(2)}) collective-permute-start(bf16[256,512]{1,0:T(8,128)(2,1)S(1)} %get-tuple-element.43), channel_id=1, source_target_pairs={{0,16},{4,20},{8,24},{12,28},{16,0},{20,4},{24,8},{28,12},{1,17},{... | collective-permute-start | bytes 786440 | tf_op jit(solution)/shard_map/ppermute | solution.py:246
  144.0 28.4 %collective-permute-start.24 = (bf16[256,512]{1,0:T(8,128)(2,1)S(1)}, bf16[256,512]{1,0:T(8,128)(2,1)S(1)}, u32[]{:S(2)}, u32[]{:S(2)}) collective-permute-start(bf16[256,512]{1,0:T(8,128)(2,1)S(1)} %get-tuple-element.41), channel_id=1, source_target_pairs={{0,24},{4,28},{8,0},{12,4},{16,8},{20,12},{24,16},{28,20},{1,25},{... | collective-permute-start | bytes 786440 | tf_op jit(solution)/shard_map/ppermute | solution.py:246
  146.4 30.0 %collective-permute-start.16 = (bf16[1024,128]{1,0:T(8,128)(2,1)S(1)}, bf16[1024,128]{1,0:T(8,128)(2,1)S(1)}, u32[]{:S(2)}, u32[]{:S(2)}) collective-permute-start(bf16[1024,128]{1,0:T(8,128)(2,1)S(1)} %shard_map.92), channel_id=1, source_target_pairs={{16,0},{20,4},{24,8},{28,12},{17,1},{21,5},{25,9},{29,13},{18,2},{... | collective-permute-start | bytes 786440 | tf_op jit(solution)/shard_map/ppermute | solution.py:263
  172.5 5.4 %collective-permute-start.28 = (bf16[256,512]{1,0:T(8,128)(2,1)S(1)}, bf16[256,512]{1,0:T(8,128)(2,1)S(1)}, u32[]{:S(2)}, u32[]{:S(2)}) collective-permute-start(bf16[256,512]{1,0:T(8,128)(2,1)S(1)} %shard_map.101.refs_0_), channel_id=1, source_target_pairs={{0,1},{1,0},{2,3},{3,2},{4,5},{5,4},{6,7},{7,6},{8,9},{9,8},{10,11... | collective-permute-start | bytes 786440 | tf_op jit(solution)/shard_map/ppermute | solution.py:240
  174.7 7.8 %collective-permute-start.29 = (bf16[256,512]{1,0:T(8,128)(2,1)S(1)}, bf16[256,512]{1,0:T(8,128)(2,1)S(1)}, u32[]{:S(2)}, u32[]{:S(2)}) collective-permute-start(bf16[256,512]{1,0:T(8,128)(2,1)S(1)} %shard_map.101.refs_0_), channel_id=1, source_target_pairs={{0,2},{1,3},{2,0},{3,1},{4,6},{5,7},{6,4},{7,5},{8,10},{9,11},{10,... | collective-permute-start | bytes 786440 | tf_op jit(solution)/shard_map/ppermute | solution.py:240
  175.0 13.4 %collective-permute-start.30 = (bf16[256,512]{1,0:T(8,128)(2,1)S(1)}, bf16[256,512]{1,0:T(8,128)(2,1)S(1)}, u32[]{:S(2)}, u32[]{:S(2)}) collective-permute-start(bf16[256,512]{1,0:T(8,128)(2,1)S(1)} %shard_map.101.refs_0_), channel_id=1, source_target_pairs={{0,3},{1,2},{2,1},{3,0},{4,7},{5,6},{6,5},{7,4},{8,11},{9,10},{10,... | collective-permute-start | bytes 786440 | tf_op jit(solution)/shard_map/ppermute | solution.py:240
  176.6 16.2 %collective-permute-start.17 = (bf16[1024,128]{1,0:T(8,128)(2,1)S(1)}, bf16[1024,128]{1,0:T(8,128)(2,1)S(1)}, u32[]{:S(2)}, u32[]{:S(2)}) collective-permute-start(bf16[1024,128]{1,0:T(8,128)(2,1)S(1)} %get-tuple-element.33), channel_id=1, source_target_pairs={{0,4},{4,0},{8,12},{12,8},{16,20},{20,16},{24,28},{28,24},{1,5},{5... | collective-permute-start | bytes 786440 | tf_op jit(solution)/shard_map/ppermute | solution.py:243
  (3 other events, 7.8 us)

commit v3 on v2

--- a/solution.py
+++ b/solution.py
@@ -56,7 +56,7 @@
     s, d = lax.axis_index("seq"), lax.axis_index("dp")
     half, rest = divmod(slot, shards)
     step, side = divmod(rest, 2)
-    source = lax.rem(s // 2 + (shards // 2 - step), shards // 2) * 2 + lax.rem(s + side, 2)
+    source = jnp.bitwise_xor(s, step * 2 + side)
     return source * 2 + lax.rem(d // 2 + half, 2)
 
 
@@ -72,13 +72,14 @@
             )
 
 
-def qg_kernel(heads, shards, inter, qa_ref, qb_ref, g_ref, *o_refs):
+def qg_kernel(heads, shards, inter, count, *refs):
+    q_refs, g_ref, o_refs = refs[:count], refs[count], refs[count + 1 :]
     y = lax.rem(lax.axis_index("seq"), 2)
     total_ref = o_refs[-1]
     for slot in range(heads):
-        ref = (qa_ref, qb_ref)[slot // (heads // 2)]
+        ref = q_refs[slot * count // heads]
         h = head_of(slot, shards, inter)
-        q = ref[:, pl.ds(slot % (heads // 2) * DH, DH)]
+        q = ref[:, pl.ds(slot % (heads // count) * DH, DH)]
         total_ref[lanes(h), :] = dot(q, g_ref[:, lanes(h)], (0, 0)).astype(total_ref.dtype)
     half = total_ref.shape[0] // 2
     for part, o_ref in enumerate(o_refs[:-1]):
@@ -143,30 +144,30 @@
             ).astype(BF16)
 
 
-def attended_kernel(factor, heads, states, shards, inter, qa_ref, qb_ref, k_ref, v_ref, *refs):
+def attended_kernel(factor, heads, states, shards, inter, count, *refs):
+    q_refs, (k_ref, v_ref), refs = refs[:count], refs[count : count + 2], refs[count + 2 :]
     o_ref = refs[states]
     p_ref = whole_state(refs[:states] + refs[states + 1 :])
     mask = causal(k_ref.shape[0])
     for slot in range(heads):
-        ref = (qa_ref, qb_ref)[slot // (heads // 2)]
+        ref = q_refs[slot * count // heads]
         cols = lanes(head_of(slot, shards, inter))
-        q = ref[:, pl.ds(slot % (heads // 2) * DH, DH)]
+        q = ref[:, pl.ds(slot % (heads // count) * DH, DH)]
         key_scores = scores(q, k_ref[:, cols], mask, factor)
         o_ref[:, cols] = (
             dot(key_scores, v_ref[:, cols], (1, 0)) + factor * dot(q, p_ref[cols, :], (1, 0))
         ).astype(BF16)
 
 
-def pair_grad_kernel(
-    factor, heads, states, shards, inter, qa_ref, qb_ref, k_ref, v_ref, g_ref, *refs
-):
+def pair_grad_kernel(factor, heads, states, shards, inter, count, *refs):
+    q_refs, (k_ref, v_ref, g_ref), refs = refs[:count], refs[count : count + 3], refs[count + 3 :]
     dk_ref, dv_ref = refs[states : states + 2]
     s_ref = whole_state(refs[:states] + refs[states + 2 :])
     mask = causal(k_ref.shape[0])
     for slot in range(heads):
-        ref = (qa_ref, qb_ref)[slot // (heads // 2)]
+        ref = q_refs[slot * count // heads]
         cols = lanes(head_of(slot, shards, inter))
-        q = ref[:, pl.ds(slot % (heads // 2) * DH, DH)]
+        q = ref[:, pl.ds(slot % (heads // count) * DH, DH)]
         k, v, g, suffix = k_ref[:, cols], v_ref[:, cols], g_ref[:, cols], s_ref[cols, :]
         key_scores = scores(q, k, mask, factor)
         grad_scores = scores(g, v, mask, factor)
@@ -197,7 +198,7 @@
     rows = refs[0].shape[1] // count
     s = lax.axis_index("seq")
     for place, step in enumerate(steps):
-        target = lax.rem(s // 2 + step, count // 2) * 2 + lax.rem(s + other, 2)
+        target = jnp.bitwise_xor(s, step * 2 + other)
         total = None
         for t_ref, g_ref in zip(refs[:pairs], refs[pairs:-1]):
             term = dot(t_ref[:, lanes(target, rows)], g_ref[...], (0, 0))
@@ -205,11 +206,20 @@
         o_ref[pl.ds(place * rows, rows), :] = total.astype(o_ref.dtype)
 
 
-def fold_kernel(start, keep_ref, got_ref, *o_refs):
-    rows = o_refs[0].shape[0]
-    for place, o_ref in enumerate(o_refs):
-        kept = keep_ref[pl.ds((start + place) * rows, rows), :]
-        o_ref[...] = (kept + got_ref[pl.ds(place * rows, rows), :].astype(F32)).astype(o_ref.dtype)
+def fold_kernel(keep_ref, got_ref, o_ref):
+    rows = o_ref.shape[0]
+    o_ref[...] = (keep_ref[pl.ds(0, rows), :] + got_ref[...].astype(F32)).astype(BF16)
+
+
+def cross_kernel(keep_ref, got_ref, pair_ref, far_ref, near_ref):
+    rows = far_ref.shape[0]
+    kept = keep_ref.shape[0] - 2 * rows
+    for place, o_ref in enumerate((far_ref, near_ref)):
+        o_ref[...] = (
+            keep_ref[pl.ds(kept + place * rows, rows), :]
+            + got_ref[pl.ds(place * rows, rows), :].astype(F32)
+            + pair_ref[pl.ds((1 - place) * rows, rows), :].astype(F32)
+        ).astype(o_ref.dtype)
 
 
 def sum_kernel(first_ref, *refs):
@@ -239,11 +249,8 @@
     def xor_dp(value, step):
         return lax.ppermute(value, "dp", [(i, i ^ step) for i in range(dps)])
 
-    def flip_seq(value):
-        return lax.ppermute(value, "seq", [(i, i ^ 1) for i in range(seqs)])
-
-    def turn_seq(value, step):
-        return lax.ppermute(value, "seq", [(i, (i + 2 * step) % seqs) for i in range(seqs)])
+    def flip_seq(value, bits=1):
+        return lax.ppermute(value, "seq", [(i, i ^ bits) for i in range(seqs)])
 
     def swap(value):
         return lax.all_to_all(value, "seq", 0, 0, tiled=True)
@@ -257,7 +264,7 @@
         part = out(send.shape, BF16)
         got = flip_seq(send)
         pair = call(pair_kernel, [part], keep, got)[0]
-        pair = lax.ppermute(pair, "seq", [(i, i ^ 2) for i in range(seqs)])
+        pair = flip_seq(pair, 2)
         quad = call(quad_kernel, [part], keep, got, pair)[0]
         low, high = range(4), range(4, 8)
         quad = lax.ppermute(
@@ -286,20 +293,27 @@
         d = lax.axis_index("dp")
         half = model // 2
         piece = lax.dynamic_slice(query_weight, (d % 2 * half, d // 2 * DH), (half, DH))
-        column = [piece] + [turn_seq(piece, k) for k in range(1, seqs // 2)]
+        column = [piece, flip_seq(piece, 2), flip_seq(piece, 4)]
+        column.append(flip_seq(column[2], 2))
         sides = [flip_seq(value) for value in column]
-        near = jnp.stack([jnp.concatenate(two, axis=1) for two in zip(column, sides)])
-        far = xor_dp(near, 1)
-        qs = call(
-            project_kernel,
-            [out((rows, width // 2), BF16)] * 2,
-            toks,
-            group[2],
-            near,
-            far,
-            flops=2 * rows * model * width,
-        )
-        pair = (qs[0], xor_dp(qs[1], 2))
+        mine, theirs = [], []
+        for part in range(2):
+            cut = slice(2 * part, 2 * part + 2)
+            near = jnp.stack(
+                [jnp.concatenate(two, axis=1) for two in zip(column[cut], sides[cut])]
+            )
+            qs = call(
+                project_kernel,
+                [out((rows, width // 4), BF16)] * 2,
+                toks,
+                group[2],
+                near,
+                xor_dp(near, 1),
+                flops=rows * model * width,
+            )
+            mine.append(qs[0])
+            theirs.append(xor_dp(qs[1], 2))
+        pair = (*mine, *theirs)
     else:
         query_rows = jnp.dot(
             toks,
@@ -321,7 +335,7 @@
 
     if split:
         block = (model // seqs, width // dps)
-        cuts = ((2, 1), (3, 0))
+        cuts = ((1, 3), (2, 0))
         weights = (*group, *grad_group)
         gots = []
         for steps in cuts:
@@ -336,17 +350,11 @@
             [out((model // 2, block[1]), F32)],
             *weights,
         )[0]
-        terms = []
-        for part, steps in enumerate(cuts):
-            folded = call(
-                functools.partial(fold_kernel, part * len(steps)),
-                [out(block, BF16 if step else F32) for step in steps],
-                keep,
-                gots[part],
-            )
-            for step, value in zip(steps, folded):
-                terms.append(turn_seq(value, step) if step else value)
-        share = call(sum_kernel, [out(block, BF16)], *terms[::-1])[0]
+        near = call(fold_kernel, [out((2 * block[0], block[1]), BF16)], keep, gots[0])[0]
+        folded = call(
+            cross_kernel, [out(block, BF16), out(block, F32)], keep, gots[1], flip_seq(near, 2)
+        )
+        share = call(sum_kernel, [out(block, BF16)], folded[1], flip_seq(folded[0], 4))[0]
     else:
         share = lax.psum_scatter(
             lax.dot_general(
@@ -367,7 +375,7 @@
     )[0]
 
     block_qg = call(
-        functools.partial(qg_kernel, heads, seqs, split),
+        functools.partial(qg_kernel, heads, seqs, split, len(pair)),
         halves,
         *pair,
         grads,
@@ -375,7 +383,7 @@
     )
     suffix = carried(block_qg, True)
     attended = call(
-        functools.partial(attended_kernel, factor, heads, states, seqs, split),
+        functools.partial(attended_kernel, factor, heads, states, seqs, split, len(pair)),
         [out((rows, width), BF16)],
         *pair,
         keys,
@@ -384,7 +392,7 @@
         scratch=scratch,
     )[0]
     key_grad, value_grad = call(
-        functools.partial(pair_grad_kernel, factor, heads, states, seqs, split),
+        functools.partial(pair_grad_kernel, factor, heads, states, seqs, split, len(pair)),
         [out((rows, width), BF16)] * 2,
         *pair,
         keys,

time: 201 us -> 154 us (0.77)
  the two profiles are of different devices: /device:TPU:15 before, /device:TPU:0 now
where the time goes in v3:
time: 154 us; the launch traced here: 153 us
  waiting for transfers between devices  86.7 us (56%)
  starting transfers between devices  41.4 us (27%)
  Pallas kernels  20.6 us (13%)
  local copies, waits for them, and re-layouts  3.44 us (2%)
    ppermute x17, waiting for transfers between devices, flip_seq(): return lax.ppermute(value, 'seq', [(i, i ^ bits) for i in range(seqs)])  44.7 us
    ppermute x17, starting transfers between devices, flip_seq(): return lax.ppermute(value, 'seq', [(i, i ^ bits) for i in range(seqs)])  27.9 us
    ppermute x13, waiting for transfers between devices, xor_dp(): return lax.ppermute(value, 'dp', [(i, i ^ step) for i in range(dps)])  25.9 us
    pallas_call x20, Pallas kernels, call(): pl.pallas_call(kernel, out_shape=tuple(outs), in_specs=[pl.BlockSpec(memo...  20.6 us
    ppermute x2, waiting for transfers between devices, carried(): lax.ppermute(quad, 'seq', list(zip(high, low) if backward else zip(low, h...  16.2 us
    ppermute x13, starting transfers between devices, xor_dp(): return lax.ppermute(value, 'dp', [(i, i ^ step) for i in range(dps)])  8.8 us
    ppermute x2, starting transfers between devices, carried(): lax.ppermute(quad, 'seq', list(zip(high, low) if backward else zip(low, h...  4.7 us
  transfers between devices with their start and end apart: 32, of which 17 were waited for; matrix products, arithmetic and copies ran while one was open for 1% of the time, Pallas kernels for 12%

profile of v3, /device:TPU:0, one launch (start us, length us, event | category | flops | bytes accessed | tf_op | source)
XLA Modules:
  0.0 153.5 jit_solution(9947181081504950047)
XLA Ops:
  0.6 3.0 %collective-permute-start = (bf16[256,2048]{1,0:T(8,128)(2,1)}, bf16[256,2048]{1,0:T(8,128)(2,1)S(1)}, u32[]{:S(2)}, u32[]{:S(2)}) collective-permute-start(bf16[256,2048]{1,0:T(8,128)(2,1)} %bitcast.15), channel_id=1, source_target_pairs={{0,2},{1,3},{2,0},{3,1},{4,6},{5,7},{6,4},{7,5},{8,10},{9,11},{10,... | collective-permute-start | bytes 3145736 | tf_op jit(solution)/shard_map/ppermute | solution.py:250
  6.9 1.6 %collective-permute-start.12 = (bf16[1024,128]{1,0:T(8,128)(2,1)S(1)}, bf16[1024,128]{1,0:T(8,128)(2,1)S(1)}, u32[]{:S(2)}, u32[]{:S(2)}) collective-permute-start(bf16[1024,128]{1,0:T(8,128)(2,1)S(1)} %get-tuple-element.29), channel_id=1, source_target_pairs={{0,4},{4,0},{8,12},{12,8},{16,20},{20,16},{24,28},{28,24},{1,5},{5... | collective-permute-start | bytes 786440 | tf_op jit(solution)/shard_map/ppermute | solution.py:253
  9.5 2.7 %collective-permute-start.5 = (bf16[1024,128]{1,0:T(8,128)(2,1)S(1)}, bf16[1024,128]{1,0:T(8,128)(2,1)S(1)}, u32[]{:S(2)}, u32[]{:S(2)}) collective-permute-start(bf16[1024,128]{1,0:T(8,128)(2,1)S(1)} %dynamic_slice.3), channel_id=1, source_target_pairs={{0,16},{4,20},{8,24},{12,28},{16,0},{20,4},{24,8},{28,12},{1,17},{... | collective-permute-start | bytes 786440 | tf_op jit(solution)/shard_map/ppermute | solution.py:253
  12.1 1.6 %collective-permute-start.2 = (bf16[1024,128]{1,0:T(8,128)(2,1)S(1)}, bf16[1024,128]{1,0:T(8,128)(2,1)S(1)}, u32[]{:S(2)}, u32[]{:S(2)}) collective-permute-start(bf16[1024,128]{1,0:T(8,128)(2,1)S(1)} %dynamic_slice.3), channel_id=1, source_target_pairs={{0,8},{4,12},{8,0},{12,4},{16,24},{20,28},{24,16},{28,20},{1,9},{5... | collective-permute-start | bytes 786440 | tf_op jit(solution)/shard_map/ppermute | solution.py:253
  14.8 2.5 %collective-permute-start.13 = (bf16[1024,128]{1,0:T(8,128)(2,1)S(1)}, bf16[1024,128]{1,0:T(8,128)(2,1)S(1)}, u32[]{:S(2)}, u32[]{:S(2)}) collective-permute-start(bf16[1024,128]{1,0:T(8,128)(2,1)S(1)} %shard_map.87), channel_id=1, source_target_pairs={{0,8},{4,12},{8,0},{12,4},{16,24},{20,28},{24,16},{28,20},{1,9},{5... | collective-permute-start | bytes 786440 | tf_op jit(solution)/shard_map/ppermute | solution.py:253
  17.3 6.3 %collective-permute-done.5 = bf16[1024,128]{1,0:T(8,128)(2,1)S(1)} collective-permute-done((bf16[1024,128]{1,0:T(8,128)(2,1)S(1)}, bf16[1024,128]{1,0:T(8,128)(2,1)S(1)}, u32[]{:S(2)}, u32[]{:S(2)}) %collective-permute-start.5) | collective-permute-done | bytes 262176 | tf_op jit(solution)/shard_map/ppermute | solution.py:253
  24.3 1.5 %collective-permute-done.2 = bf16[1024,128]{1,0:T(8,128)(2,1)S(1)} collective-permute-done((bf16[1024,128]{1,0:T(8,128)(2,1)S(1)}, bf16[1024,128]{1,0:T(8,128)(2,1)S(1)}, u32[]{:S(2)}, u32[]{:S(2)}) %collective-permute-start.2) | collective-permute-done | bytes 262176 | tf_op jit(solution)/shard_map/ppermute | solution.py:253
  26.4 5.0 %collective-permute-done.13.pair_ref = bf16[1024,128]{1,0:T(8,128)(2,1)S(1)} collective-permute-done((bf16[1024,128]{1,0:T(8,128)(2,1)S(1)}, bf16[1024,128]{1,0:T(8,128)(2,1)S(1)}, u32[]{:S(2)}, u32[]{:S(2)}) %collective-permute-start.13) | collective-permute-done | bytes 262176 | tf_op jit(solution)/shard_map/ppermute | solution.py:253
  32.0 3.1 %collective-permute-done.7 = bf16[1024,128]{1,0:T(8,128)(2,1)S(1)} collective-permute-done((bf16[1024,128]{1,0:T(8,128)(2,1)S(1)}, bf16[1024,128]{1,0:T(8,128)(2,1)S(1)}, u32[]{:S(2)}, u32[]{:S(2)}) %collective-permute-start.7) | collective-permute-done | bytes 262176 | tf_op jit(solution)/shard_map/ppermute | solution.py:253
  35.1 3.2 %collective-permute-start.14 = (bf16[1024,128]{1,0:T(8,128)(2,1)S(1)}, bf16[1024,128]{1,0:T(8,128)(2,1)S(1)}, u32[]{:S(2)}, u32[]{:S(2)}) collective-permute-start(bf16[1024,128]{1,0:T(8,128)(2,1)S(1)} %shard_map.88), channel_id=1, source_target_pairs={{0,16},{4,20},{8,24},{12,28},{1,17},{5,21},{9,25},{13,29},{2,18},{... | collective-permute-start | bytes 786440 | tf_op jit(solution)/shard_map/ppermute | solution.py:270
  39.9 5.0 %collective-permute-done.8 = bf16[1024,128]{1,0:T(8,128)(2,1)S(1)} collective-permute-done((bf16[1024,128]{1,0:T(8,128)(2,1)S(1)}, bf16[1024,128]{1,0:T(8,128)(2,1)S(1)}, u32[]{:S(2)}, u32[]{:S(2)}) %collective-permute-start.8) | collective-permute-done | bytes 262176 | tf_op jit(solution)/shard_map/ppermute | solution.py:253
  45.9 8.1 %collective-permute-done.15.refs_7_.refs_1_ = bf16[1024,128]{1,0:T(8,128)(2,1)S(1)} collective-permute-done((bf16[1024,128]{1,0:T(8,128)(2,1)S(1)}, bf16[1024,128]{1,0:T(8,128)(2,1)S(1)}, u32[]{:S(2)}, u32[]{:S(2)}) %collective-permute-start.15) | collective-permute-done | bytes 262176 | tf_op jit(solution)/shard_map/ppermute | solution.py:253
  54.0 2.0 %shard_map.96 = (bf16[256,512]{1,0:T(8,128)(2,1)S(1)}, bf16[256,512]{1,0:T(8,128)(2,1)S(1)}, bf16[256,512]{1,0:T(8,128)(2,1)S(1)}, bf16[256,512]{1,0:T(8,128)(2,1)S(1)}) custom-call(bf16[256,2048]{1,0:T(8,128)(2,1)S(1)} %bitcast.23, bf16[256,2048]{1,0:T(8,128)(2,1)S(1)} %bitcast.27, bf16[256,2048]{1,0:T(8,128)(2,1)S(1)} %bitcast.30, ...), custom_call_target="tpu_custom_call" | custom-call | bytes 4718592 | tf_op jit(solution)/shard_map/pallas_call | solution.py:28
  58.0 7.4 %collective-permute-done.23.refs_6_ = bf16[256,512]{1,0:T(8,128)(2,1)S(1)} collective-permute-done((bf16[256,512]{1,0:T(8,128)(2,1)S(1)}, bf16[256,512]{1,0:T(8,128)(2,1)S(1)}, u32[]{:S(2)}, u32[]{:S(2)}) %collective-permute-start.23) | collective-permute-done | bytes 262176 | tf_op jit(solution)/shard_map/ppermute | solution.py:250
  65.4 4.5 %collective-permute-done.24.refs_7_ = bf16[256,512]{1,0:T(8,128)(2,1)S(1)} collective-permute-done((bf16[256,512]{1,0:T(8,128)(2,1)S(1)}, bf16[256,512]{1,0:T(8,128)(2,1)S(1)}, u32[]{:S(2)}, u32[]{:S(2)}) %collective-permute-start.24) | collective-permute-done | bytes 262176 | tf_op jit(solution)/shard_map/ppermute | solution.py:250
  74.4 1.6 %collective-permute-start.11 = (bf16[256,512]{1,0:T(8,128)(2,1)S(1)}, bf16[256,512]{1,0:T(8,128)(2,1)S(1)}, u32[]{:S(2)}, u32[]{:S(2)}) collective-permute-start(bf16[256,512]{1,0:T(8,128)(2,1)S(1)} %get-tuple-element.27), channel_id=1, source_target_pairs={{0,2},{1,3},{2,0},{3,1},{4,6},{5,7},{6,4},{7,5},{8,10},{9,11},{10,... | collective-permute-start | bytes 786440 | tf_op jit(solution)/shard_map/ppermute | solution.py:250
  76.0 5.8 %collective-permute-done.10.refs_2_ = bf16[256,512]{1,0:T(8,128)(2,1)S(1)} collective-permute-done((bf16[256,512]{1,0:T(8,128)(2,1)S(1)}, bf16[256,512]{1,0:T(8,128)(2,1)S(1)}, u32[]{:S(2)}, u32[]{:S(2)}) %collective-permute-start.10) | collective-permute-done | bytes 262176 | tf_op jit(solution)/shard_map/ppermute | solution.py:250
  81.8 4.7 %collective-permute-done.11.refs_3_ = bf16[256,512]{1,0:T(8,128)(2,1)S(1)} collective-permute-done((bf16[256,512]{1,0:T(8,128)(2,1)S(1)}, bf16[256,512]{1,0:T(8,128)(2,1)S(1)}, u32[]{:S(2)}, u32[]{:S(2)}) %collective-permute-start.11) | collective-permute-done | bytes 262176 | tf_op jit(solution)/shard_map/ppermute | solution.py:250
  87.1 1.5 collective-permute-start.16
  90.1 1.3 shard_map.97.keep_ref
  91.5 4.1 %collective-permute-start.27 = (bf16[512,512]{1,0:T(8,128)(2,1)S(1)}, bf16[512,512]{1,0:T(8,128)(2,1)S(1)}, u32[]{:S(2)}, u32[]{:S(2)}) collective-permute-start(bf16[512,512]{1,0:T(8,128)(2,1)S(1)} %shard_map.100), channel_id=1, source_target_pairs={{0,8},{4,12},{8,0},{12,4},{16,24},{20,28},{24,16},{28,20},{1,9},{5... | collective-permute-start | bytes 1572872 | tf_op jit(solution)/shard_map/ppermute | solution.py:253
  96.4 4.1 %collective-permute-start.17 = (bf16[1024,128]{1,0:T(8,128)(2,1)S(1)}, bf16[1024,128]{1,0:T(8,128)(2,1)S(1)}, u32[]{:S(2)}, u32[]{:S(2)}) collective-permute-start(bf16[1024,128]{1,0:T(8,128)(2,1)S(1)} %shard_map.92), channel_id=1, source_target_pairs={{0,8},{4,12},{8,0},{12,4},{16,24},{20,28},{24,16},{28,20},{1,9},{5... | collective-permute-start | bytes 786440 | tf_op jit(solution)/shard_map/ppermute | solution.py:253
  100.5 11.4 %collective-permute-done.17.pair_ref = bf16[1024,128]{1,0:T(8,128)(2,1)S(1)} collective-permute-done((bf16[1024,128]{1,0:T(8,128)(2,1)S(1)}, bf16[1024,128]{1,0:T(8,128)(2,1)S(1)}, u32[]{:S(2)}, u32[]{:S(2)}) %collective-permute-start.17) | collective-permute-done | bytes 262176 | tf_op jit(solution)/shard_map/ppermute | solution.py:253
  112.0 1.5 collective-permute-start.18
  113.7 3.6 %collective-permute-start.28 = (bf16[256,512]{1,0:T(8,128)(2,1)S(1)}, bf16[256,512]{1,0:T(8,128)(2,1)S(1)}, u32[]{:S(2)}, u32[]{:S(2)}) collective-permute-start(bf16[256,512]{1,0:T(8,128)(2,1)S(1)} %get-tuple-element.43), channel_id=1, source_target_pairs={{0,16},{4,20},{8,24},{12,28},{16,0},{20,4},{24,8},{28,12},{1,17},{... | collective-permute-start | bytes 786440 | tf_op jit(solution)/shard_map/ppermute | solution.py:253
  117.3 16.2 %collective-permute-done.18.quad_ref = bf16[1024,128]{1,0:T(8,128)(2,1)S(1)} collective-permute-done((bf16[1024,128]{1,0:T(8,128)(2,1)S(1)}, bf16[1024,128]{1,0:T(8,128)(2,1)S(1)}, u32[]{:S(2)}, u32[]{:S(2)}) %collective-permute-start.18) | collective-permute-done | bytes 262176 | tf_op jit(solution)/shard_map/ppermute | solution.py:270
  133.7 1.6 %collective-permute-start.19 = (bf16[1024,128]{1,0:T(8,128)(2,1)S(1)}, bf16[1024,128]{1,0:T(8,128)(2,1)S(1)}, u32[]{:S(2)}, u32[]{:S(2)}) collective-permute-start(bf16[1024,128]{1,0:T(8,128)(2,1)S(1)} %get-tuple-element.35), channel_id=1, source_target_pairs={{0,4},{4,0},{8,12},{12,8},{16,20},{20,16},{24,28},{28,24},{1,5},{5... | collective-permute-start | bytes 786440 | tf_op jit(solution)/shard_map/ppermute | solution.py:253
  135.3 2.9 %collective-permute-done.28.refs_0_ = bf16[256,512]{1,0:T(8,128)(2,1)S(1)} collective-permute-done((bf16[256,512]{1,0:T(8,128)(2,1)S(1)}, bf16[256,512]{1,0:T(8,128)(2,1)S(1)}, u32[]{:S(2)}, u32[]{:S(2)}) %collective-permute-start.28) | collective-permute-done | bytes 262176 | tf_op jit(solution)/shard_map/ppermute | solution.py:253
  140.1 3.0 %shard_map.90 = bf16[256,2048]{1,0:T(8,128)(2,1)} custom-call(bf16[256,512]{1,0:T(8,128)(2,1)S(1)} %get-tuple-element.24.refs_0_, bf16[256,512]{1,0:T(8,128)(2,1)S(1)} %get-tuple-element.25.refs_1_, bf16[256,512]{1,0:T(8,128)(2,1)S(1)} %collective-permute-done.10.refs_2_, bf16[256,512]{1,0:T(8,128)(2,1)S(1)} %collective-permute-done.11.refs_3_, ...), custom_call_target="tpu_custom_call" | custom-call | bytes 4718592 | tf_op jit(solution)/shard_map/pallas_call | solution.py:28
  143.1 6.5 %shard_map.95 = (bf16[256,2048]{1,0:T(8,128)(2,1)}, bf16[256,2048]{1,0:T(8,128)(2,1)}) custom-call(bf16[256,512]{1,0:T(8,128)(2,1)S(1)} %get-tuple-element.24.refs_0_, bf16[256,512]{1,0:T(8,128)(2,1)S(1)} %get-tuple-element.25.refs_1_, bf16[256,512]{1,0:T(8,128)(2,1)S(1)} %collective-permute-done.10.refs_2_, ...), custom_call_target="tpu_custom_call" | custom-call | bytes 6815744 | tf_op jit(solution)/shard_map/pallas_call | solution.py:28
  149.6 2.4 %collective-permute-done.31.refs_3_ = bf16[256,512]{1,0:T(8,128)(2,1)S(1)} collective-permute-done((bf16[256,512]{1,0:T(8,128)(2,1)S(1)}, bf16[256,512]{1,0:T(8,128)(2,1)S(1)}, u32[]{:S(2)}, u32[]{:S(2)}) %collective-permute-start.31) | collective-permute-done | bytes 262176 | tf_op jit(solution)/shard_map/ppermute | solution.py:250
  152.0 1.5 shard_map.103
  (71 shorter events, 21.3 us)
Async XLA Ops:
  0.6 38.6 %collective-permute-start = (bf16[256,2048]{1,0:T(8,128)(2,1)}, bf16[256,2048]{1,0:T(8,128)(2,1)S(1)}, u32[]{:S(2)}, u32[]{:S(2)}) collective-permute-start(bf16[256,2048]{1,0:T(8,128)(2,1)} %bitcast.15), channel_id=1, source_target_pairs={{0,2},{1,3},{2,0},{3,1},{4,6},{5,7},{6,4},{7,5},{8,10},{9,11},{10,... | collective-permute-start | bytes 3145736 | tf_op jit(solution)/shard_map/ppermute | solution.py:250
  6.9 7.8 %collective-permute-start.12 = (bf16[1024,128]{1,0:T(8,128)(2,1)S(1)}, bf16[1024,128]{1,0:T(8,128)(2,1)S(1)}, u32[]{:S(2)}, u32[]{:S(2)}) collective-permute-start(bf16[1024,128]{1,0:T(8,128)(2,1)S(1)} %get-tuple-element.29), channel_id=1, source_target_pairs={{0,4},{4,0},{8,12},{12,8},{16,20},{20,16},{24,28},{28,24},{1,5},{5... | collective-permute-start | bytes 786440 | tf_op jit(solution)/shard_map/ppermute | solution.py:253
  9.5 14.2 %collective-permute-start.5 = (bf16[1024,128]{1,0:T(8,128)(2,1)S(1)}, bf16[1024,128]{1,0:T(8,128)(2,1)S(1)}, u32[]{:S(2)}, u32[]{:S(2)}) collective-permute-start(bf16[1024,128]{1,0:T(8,128)(2,1)S(1)} %dynamic_slice.3), channel_id=1, source_target_pairs={{0,16},{4,20},{8,24},{12,28},{16,0},{20,4},{24,8},{28,12},{1,17},{... | collective-permute-start | bytes 786440 | tf_op jit(solution)/shard_map/ppermute | solution.py:253
  12.1 13.7 %collective-permute-start.2 = (bf16[1024,128]{1,0:T(8,128)(2,1)S(1)}, bf16[1024,128]{1,0:T(8,128)(2,1)S(1)}, u32[]{:S(2)}, u32[]{:S(2)}) collective-permute-start(bf16[1024,128]{1,0:T(8,128)(2,1)S(1)} %dynamic_slice.3), channel_id=1, source_target_pairs={{0,8},{4,12},{8,0},{12,4},{16,24},{20,28},{24,16},{28,20},{1,9},{5... | collective-permute-start | bytes 786440 | tf_op jit(solution)/shard_map/ppermute | solution.py:253
  13.7 12.6 %collective-permute-start.1 = (bf16[1024,128]{1,0:T(8,128)(2,1)S(1)}, bf16[1024,128]{1,0:T(8,128)(2,1)S(1)}, u32[]{:S(2)}, u32[]{:S(2)}) collective-permute-start(bf16[1024,128]{1,0:T(8,128)(2,1)S(1)} %dynamic_slice.3), channel_id=1, source_target_pairs={{0,4},{4,0},{8,12},{12,8},{16,20},{20,16},{24,28},{28,24},{1,5},{5... | collective-permute-start | bytes 786440 | tf_op jit(solution)/shard_map/ppermute | solution.py:253
  14.8 16.6 %collective-permute-start.13 = (bf16[1024,128]{1,0:T(8,128)(2,1)S(1)}, bf16[1024,128]{1,0:T(8,128)(2,1)S(1)}, u32[]{:S(2)}, u32[]{:S(2)}) collective-permute-start(bf16[1024,128]{1,0:T(8,128)(2,1)S(1)} %shard_map.87), channel_id=1, source_target_pairs={{0,8},{4,12},{8,0},{12,4},{16,24},{20,28},{24,16},{28,20},{1,9},{5... | collective-permute-start | bytes 786440 | tf_op jit(solution)/shard_map/ppermute | solution.py:253
  23.7 11.4 %collective-permute-start.7 = (bf16[1024,128]{1,0:T(8,128)(2,1)S(1)}, bf16[1024,128]{1,0:T(8,128)(2,1)S(1)}, u32[]{:S(2)}, u32[]{:S(2)}) collective-permute-start(bf16[1024,128]{1,0:T(8,128)(2,1)S(1)} %collective-permute-done.5), channel_id=1, source_target_pairs={{0,8},{4,12},{8,0},{12,4},{16,24},{20,28},{24,16},{28,20},{1,9},{5... | collective-permute-start | bytes 786440 | tf_op jit(solution)/shard_map/ppermute | solution.py:253
  25.8 12.5 %collective-permute-start.3 = (bf16[1024,128]{1,0:T(8,128)(2,1)S(1)}, bf16[1024,128]{1,0:T(8,128)(2,1)S(1)}, u32[]{:S(2)}, u32[]{:S(2)}) collective-permute-start(bf16[1024,128]{1,0:T(8,128)(2,1)S(1)} %collective-permute-done.2), channel_id=1, source_target_pairs={{0,4},{4,0},{8,12},{12,8},{16,20},{20,16},{24,28},{28,24},{1,5},{5... | collective-permute-start | bytes 786440 | tf_op jit(solution)/shard_map/ppermute | solution.py:253
  26.3 29.8 %collective-permute-start.20 = (bf16[256,2048]{1,0:T(8,128)(2,1)S(1)}, bf16[256,2048]{1,0:T(8,128)(2,1)S(1)}, u32[]{:S(2)}, u32[]{:S(2)}) collective-permute-start(bf16[256,2048]{1,0:T(8,128)(2,1)S(1)} %bitcast.16), channel_id=1, source_target_pairs={{0,1},{1,0},{2,3},{3,2},{4,5},{5,4},{6,7},{7,6},{8,9},{9,8},{10,11... | collective-permute-start | bytes 3145736 | tf_op jit(solution)/shard_map/ppermute | solution.py:250
  31.5 7.6 %collective-permute-start.6 = (bf16[1024,128]{1,0:T(8,128)(2,1)S(1)}, bf16[1024,128]{1,0:T(8,128)(2,1)S(1)}, u32[]{:S(2)}, u32[]{:S(2)}) collective-permute-start(bf16[1024,128]{1,0:T(8,128)(2,1)S(1)} %collective-permute-done.5), channel_id=1, source_target_pairs={{0,4},{4,0},{8,12},{12,8},{16,20},{20,16},{24,28},{28,24},{1,5},{5... | collective-permute-start | bytes 786440 | tf_op jit(solution)/shard_map/ppermute | solution.py:253
  35.1 10.0 %collective-permute-start.14 = (bf16[1024,128]{1,0:T(8,128)(2,1)S(1)}, bf16[1024,128]{1,0:T(8,128)(2,1)S(1)}, u32[]{:S(2)}, u32[]{:S(2)}) collective-permute-start(bf16[1024,128]{1,0:T(8,128)(2,1)S(1)} %shard_map.88), channel_id=1, source_target_pairs={{0,16},{4,20},{8,24},{12,28},{1,17},{5,21},{9,25},{13,29},{2,18},{... | collective-permute-start | bytes 786440 | tf_op jit(solution)/shard_map/ppermute | solution.py:270
  38.3 6.5 %collective-permute-start.8 = (bf16[1024,128]{1,0:T(8,128)(2,1)S(1)}, bf16[1024,128]{1,0:T(8,128)(2,1)S(1)}, u32[]{:S(2)}, u32[]{:S(2)}) collective-permute-start(bf16[1024,128]{1,0:T(8,128)(2,1)S(1)} %collective-permute-done.7), channel_id=1, source_target_pairs={{0,4},{4,0},{8,12},{12,8},{16,20},{20,16},{24,28},{28,24},{1,5},{5... | collective-permute-start | bytes 786440 | tf_op jit(solution)/shard_map/ppermute | solution.py:253
  39.1 32.2 %collective-permute-start.4 = (bf16[2,1024,256]{2,1,0:T(8,128)(2,1)S(1)}, bf16[2,1024,256]{2,1,0:T(8,128)(2,1)S(1)}, u32[]{:S(2)}, u32[]{:S(2)}) collective-permute-start(bf16[2,1024,256]{2,1,0:T(8,128)(2,1)S(1)} %pad_maximum_fusion.near_ref), channel_id=1, source_target_pairs={{0,1},{1,0},{2,3},{3,2},{4,5},{5,4},{6,7},{7,6},{8,9},{9,8},{10,11... | collective-permute-start | bytes 3145736 | tf_op jit(solution)/shard_map/ppermute | solution.py:250
  39.3 30.6 %collective-permute-start.21 = (bf16[256,2048]{1,0:T(8,128)(2,1)S(1)}, bf16[256,2048]{1,0:T(8,128)(2,1)S(1)}, u32[]{:S(2)}, u32[]{:S(2)}) collective-permute-start(bf16[256,2048]{1,0:T(8,128)(2,1)S(1)} %collective-permute-done.theirs_ref.refs_2_), channel_id=1, source_target_pairs={{0,1},{1,0},{2,3},{3,2},{4,5},{5,4},{6,7},{7,6},{8,9},{9,8},{10,11... | collective-permute-start | bytes 3145736 | tf_op jit(solution)/shard_map/ppermute | solution.py:250
  45.0 28.2 %collective-permute-start.9 = (bf16[2,1024,256]{2,1,0:T(8,128)(2,1)S(1)}, bf16[2,1024,256]{2,1,0:T(8,128)(2,1)S(1)}, u32[]{:S(2)}, u32[]{:S(2)}) collective-permute-start(bf16[2,1024,256]{2,1,0:T(8,128)(2,1)S(1)} %pad_maximum_fusion.1.near_ref), channel_id=1, source_target_pairs={{0,1},{1,0},{2,3},{3,2},{4,5},{5,4},{6,7},{7,6},{8,9},{9,8},{10,11... | collective-permute-start | bytes 3145736 | tf_op jit(solution)/shard_map/ppermute | solution.py:250
  45.3 8.8 %collective-permute-start.15 = (bf16[1024,128]{1,0:T(8,128)(2,1)S(1)}, bf16[1024,128]{1,0:T(8,128)(2,1)S(1)}, u32[]{:S(2)}, u32[]{:S(2)}) collective-permute-start(bf16[1024,128]{1,0:T(8,128)(2,1)S(1)} %get-tuple-element.31), channel_id=1, source_target_pairs={{0,4},{4,0},{8,12},{12,8},{16,20},{20,16},{24,28},{28,24},{1,5},{5... | collective-permute-start | bytes 786440 | tf_op jit(solution)/shard_map/ppermute | solution.py:253
  56.0 1.6 %collective-permute-start.22 = (bf16[256,512]{1,0:T(8,128)(2,1)S(1)}, bf16[256,512]{1,0:T(8,128)(2,1)S(1)}, u32[]{:S(2)}, u32[]{:S(2)}) collective-permute-start(bf16[256,512]{1,0:T(8,128)(2,1)S(1)} %get-tuple-element.39), channel_id=1, source_target_pairs={{0,1},{1,0},{2,3},{3,2},{4,5},{5,4},{6,7},{7,6},{8,9},{9,8},{10,11... | collective-permute-start | bytes 786440 | tf_op jit(solution)/shard_map/ppermute | solution.py:250
  56.1 9.2 %collective-permute-start.23 = (bf16[256,512]{1,0:T(8,128)(2,1)S(1)}, bf16[256,512]{1,0:T(8,128)(2,1)S(1)}, u32[]{:S(2)}, u32[]{:S(2)}) collective-permute-start(bf16[256,512]{1,0:T(8,128)(2,1)S(1)} %get-tuple-element.40), channel_id=1, source_target_pairs={{0,2},{1,3},{2,0},{3,1},{4,6},{5,7},{6,4},{7,5},{8,10},{9,11},{10,... | collective-permute-start | bytes 786440 | tf_op jit(solution)/shard_map/ppermute | solution.py:250
  57.6 12.3 %collective-permute-start.24 = (bf16[256,512]{1,0:T(8,128)(2,1)S(1)}, bf16[256,512]{1,0:T(8,128)(2,1)S(1)}, u32[]{:S(2)}, u32[]{:S(2)}) collective-permute-start(bf16[256,512]{1,0:T(8,128)(2,1)S(1)} %get-tuple-element.41), channel_id=1, source_target_pairs={{0,3},{1,2},{2,1},{3,0},{4,7},{5,6},{6,5},{7,4},{8,11},{9,10},{10,... | collective-permute-start | bytes 786440 | tf_op jit(solution)/shard_map/ppermute | solution.py:250
  70.7 20.7 %collective-permute-start.26 = (bf16[512,512]{1,0:T(8,128)(2,1)S(1)}, bf16[512,512]{1,0:T(8,128)(2,1)S(1)}, u32[]{:S(2)}, u32[]{:S(2)}) collective-permute-start(bf16[512,512]{1,0:T(8,128)(2,1)S(1)} %shard_map.99), channel_id=1, source_target_pairs={{0,4},{4,0},{8,12},{12,8},{16,20},{20,16},{24,28},{28,24},{1,5},{5... | collective-permute-start | bytes 1572872 | tf_op jit(solution)/shard_map/ppermute | solution.py:253
  72.6 9.2 %collective-permute-start.10 = (bf16[256,512]{1,0:T(8,128)(2,1)S(1)}, bf16[256,512]{1,0:T(8,128)(2,1)S(1)}, u32[]{:S(2)}, u32[]{:S(2)}) collective-permute-start(bf16[256,512]{1,0:T(8,128)(2,1)S(1)} %get-tuple-element.26), channel_id=1, source_target_pairs={{0,2},{1,3},{2,0},{3,1},{4,6},{5,7},{6,4},{7,5},{8,10},{9,11},{10,... | collective-permute-start | bytes 786440 | tf_op jit(solution)/shard_map/ppermute | solution.py:250
  74.4 12.1 %collective-permute-start.11 = (bf16[256,512]{1,0:T(8,128)(2,1)S(1)}, bf16[256,512]{1,0:T(8,128)(2,1)S(1)}, u32[]{:S(2)}, u32[]{:S(2)}) collective-permute-start(bf16[256,512]{1,0:T(8,128)(2,1)S(1)} %get-tuple-element.27), channel_id=1, source_target_pairs={{0,2},{1,3},{2,0},{3,1},{4,6},{5,7},{6,4},{7,5},{8,10},{9,11},{10,... | collective-permute-start | bytes 786440 | tf_op jit(solution)/shard_map/ppermute | solution.py:250
  87.1 9.2 %collective-permute-start.16 = (bf16[1024,128]{1,0:T(8,128)(2,1)S(1)}, bf16[1024,128]{1,0:T(8,128)(2,1)S(1)}, u32[]{:S(2)}, u32[]{:S(2)}) collective-permute-start(bf16[1024,128]{1,0:T(8,128)(2,1)S(1)} %get-tuple-element.33), channel_id=1, source_target_pairs={{0,4},{4,0},{8,12},{12,8},{16,20},{20,16},{24,28},{28,24},{1,5},{5... | collective-permute-start | bytes 786440 | tf_op jit(solution)/shard_map/ppermute | solution.py:253
  89.4 24.1 %collective-permute-start.25 = (bf16[512,512]{1,0:T(8,128)(2,1)S(1)}, bf16[512,512]{1,0:T(8,128)(2,1)S(1)}, u32[]{:S(2)}, u32[]{:S(2)}) collective-permute-start(bf16[512,512]{1,0:T(8,128)(2,1)S(1)} %shard_map.98), channel_id=1, source_target_pairs={{0,4},{4,0},{8,12},{12,8},{16,20},{20,16},{24,28},{28,24},{1,5},{5... | collective-permute-start | bytes 1572872 | tf_op jit(solution)/shard_map/ppermute | solution.py:253
  91.5 22.1 %collective-permute-start.27 = (bf16[512,512]{1,0:T(8,128)(2,1)S(1)}, bf16[512,512]{1,0:T(8,128)(2,1)S(1)}, u32[]{:S(2)}, u32[]{:S(2)}) collective-permute-start(bf16[512,512]{1,0:T(8,128)(2,1)S(1)} %shard_map.100), channel_id=1, source_target_pairs={{0,8},{4,12},{8,0},{12,4},{16,24},{20,28},{24,16},{28,20},{1,9},{5... | collective-permute-start | bytes 1572872 | tf_op jit(solution)/shard_map/ppermute | solution.py:253
  96.4 15.5 %collective-permute-start.17 = (bf16[1024,128]{1,0:T(8,128)(2,1)S(1)}, bf16[1024,128]{1,0:T(8,128)(2,1)S(1)}, u32[]{:S(2)}, u32[]{:S(2)}) collective-permute-start(bf16[1024,128]{1,0:T(8,128)(2,1)S(1)} %shard_map.92), channel_id=1, source_target_pairs={{0,8},{4,12},{8,0},{12,4},{16,24},{20,28},{24,16},{28,20},{1,9},{5... | collective-permute-start | bytes 786440 | tf_op jit(solution)/shard_map/ppermute | solution.py:253
  112.0 21.5 %collective-permute-start.18 = (bf16[1024,128]{1,0:T(8,128)(2,1)S(1)}, bf16[1024,128]{1,0:T(8,128)(2,1)S(1)}, u32[]{:S(2)}, u32[]{:S(2)}) collective-permute-start(bf16[1024,128]{1,0:T(8,128)(2,1)S(1)} %shard_map.93), channel_id=1, source_target_pairs={{16,0},{20,4},{24,8},{28,12},{17,1},{21,5},{25,9},{29,13},{18,2},{... | collective-permute-start | bytes 786440 | tf_op jit(solution)/shard_map/ppermute | solution.py:270
  113.7 24.4 %collective-permute-start.28 = (bf16[256,512]{1,0:T(8,128)(2,1)S(1)}, bf16[256,512]{1,0:T(8,128)(2,1)S(1)}, u32[]{:S(2)}, u32[]{:S(2)}) collective-permute-start(bf16[256,512]{1,0:T(8,128)(2,1)S(1)} %get-tuple-element.43), channel_id=1, source_target_pairs={{0,16},{4,20},{8,24},{12,28},{16,0},{20,4},{24,8},{28,12},{1,17},{... | collective-permute-start | bytes 786440 | tf_op jit(solution)/shard_map/ppermute | solution.py:253
  133.7 9.4 %collective-permute-start.19 = (bf16[1024,128]{1,0:T(8,128)(2,1)S(1)}, bf16[1024,128]{1,0:T(8,128)(2,1)S(1)}, u32[]{:S(2)}, u32[]{:S(2)}) collective-permute-start(bf16[1024,128]{1,0:T(8,128)(2,1)S(1)} %get-tuple-element.35), channel_id=1, source_target_pairs={{0,4},{4,0},{8,12},{12,8},{16,20},{20,16},{24,28},{28,24},{1,5},{5... | collective-permute-start | bytes 786440 | tf_op jit(solution)/shard_map/ppermute | solution.py:253
  138.2 11.4 %collective-permute-start.29 = (bf16[256,512]{1,0:T(8,128)(2,1)S(1)}, bf16[256,512]{1,0:T(8,128)(2,1)S(1)}, u32[]{:S(2)}, u32[]{:S(2)}) collective-permute-start(bf16[256,512]{1,0:T(8,128)(2,1)S(1)} %shard_map.102.refs_0_), channel_id=1, source_target_pairs={{0,1},{1,0},{2,3},{3,2},{4,5},{5,4},{6,7},{7,6},{8,9},{9,8},{10,11... | collective-permute-start | bytes 786440 | tf_op jit(solution)/shard_map/ppermute | solution.py:250
  138.2 11.3 %collective-permute-start.30 = (bf16[256,512]{1,0:T(8,128)(2,1)S(1)}, bf16[256,512]{1,0:T(8,128)(2,1)S(1)}, u32[]{:S(2)}, u32[]{:S(2)}) collective-permute-start(bf16[256,512]{1,0:T(8,128)(2,1)S(1)} %shard_map.102.refs_0_), channel_id=1, source_target_pairs={{0,2},{1,3},{2,0},{3,1},{4,6},{5,7},{6,4},{7,5},{8,10},{9,11},{10,... | collective-permute-start | bytes 786440 | tf_op jit(solution)/shard_map/ppermute | solution.py:250
  138.8 13.2 %collective-permute-start.31 = (bf16[256,512]{1,0:T(8,128)(2,1)S(1)}, bf16[256,512]{1,0:T(8,128)(2,1)S(1)}, u32[]{:S(2)}, u32[]{:S(2)}) collective-permute-start(bf16[256,512]{1,0:T(8,128)(2,1)S(1)} %shard_map.102.refs_0_), channel_id=1, source_target_pairs={{0,3},{1,2},{2,1},{3,0},{4,7},{5,6},{6,5},{7,4},{8,11},{9,10},{10,... | collective-permute-start | bytes 786440 | tf_op jit(solution)/shard_map/ppermute | solution.py:250
  (6 other events, 72.5 us)

commit v4 on v3

--- a/solution.py
+++ b/solution.py
@@ -159,23 +159,35 @@
         ).astype(BF16)
 
 
-def pair_grad_kernel(factor, heads, states, shards, inter, count, *refs):
-    q_refs, (k_ref, v_ref, g_ref), refs = refs[:count], refs[count : count + 3], refs[count + 3 :]
-    dk_ref, dv_ref = refs[states : states + 2]
-    s_ref = whole_state(refs[:states] + refs[states + 2 :])
+def key_grad_kernel(factor, heads, states, shards, inter, count, *refs):
+    q_refs, (v_ref, g_ref), refs = refs[:count], refs[count : count + 2], refs[count + 2 :]
+    o_ref = refs[states]
+    s_ref = whole_state(refs[:states] + refs[states + 1 :])
+    mask = causal(v_ref.shape[0])
+    for slot in range(heads):
+        ref = q_refs[slot * count // heads]
+        cols = lanes(head_of(slot, shards, inter))
+        q = ref[:, pl.ds(slot % (heads // count) * DH, DH)]
+        v = v_ref[:, cols]
+        grad_scores = scores(g_ref[:, cols], v, mask, factor)
+        o_ref[:, cols] = (
+            dot(grad_scores, q, (0, 0)) + factor * dot(v, s_ref[cols, :], (1, 1))
+        ).astype(BF16)
+
+
+def value_grad_kernel(factor, heads, states, shards, inter, count, *refs):
+    q_refs, (k_ref, g_ref), refs = refs[:count], refs[count : count + 2], refs[count + 2 :]
+    o_ref = refs[states]
+    s_ref = whole_state(refs[:states] + refs[states + 1 :])
     mask = causal(k_ref.shape[0])
     for slot in range(heads):
         ref = q_refs[slot * count // heads]
         cols = lanes(head_of(slot, shards, inter))
         q = ref[:, pl.ds(slot % (heads // count) * DH, DH)]
-        k, v, g, suffix = k_ref[:, cols], v_ref[:, cols], g_ref[:, cols], s_ref[cols, :]
+        k = k_ref[:, cols]
         key_scores = scores(q, k, mask, factor)
-        grad_scores = scores(g, v, mask, factor)
-        dk_ref[:, cols] = (
-            dot(grad_scores, q, (0, 0)) + factor * dot(v, suffix, (1, 1))
-        ).astype(BF16)
-        dv_ref[:, cols] = (
-            dot(key_scores, g, (0, 0)) + factor * dot(k, suffix, (1, 0))
+        o_ref[:, cols] = (
+            dot(key_scores, g_ref[:, cols], (0, 0)) + factor * dot(k, s_ref[cols, :], (1, 0))
         ).astype(BF16)
 
 
@@ -192,34 +204,16 @@
             ).astype(BF16)
 
 
-def weight_kernel(count, other, steps, *refs):
-    o_ref = refs[-1]
-    pairs = len(refs) // 2
+def weight_kernel(count, pairs, other, steps, *refs):
     rows = refs[0].shape[1] // count
     s = lax.axis_index("seq")
-    for place, step in enumerate(steps):
+    for step, o_ref in zip(steps, refs[2 * pairs :]):
         target = jnp.bitwise_xor(s, step * 2 + other)
         total = None
-        for t_ref, g_ref in zip(refs[:pairs], refs[pairs:-1]):
+        for t_ref, g_ref in zip(refs[:pairs], refs[pairs : 2 * pairs]):
             term = dot(t_ref[:, lanes(target, rows)], g_ref[...], (0, 0))
             total = term if total is None else total + term
-        o_ref[pl.ds(place * rows, rows), :] = total.astype(o_ref.dtype)
-
-
-def fold_kernel(keep_ref, got_ref, o_ref):
-    rows = o_ref.shape[0]
-    o_ref[...] = (keep_ref[pl.ds(0, rows), :] + got_ref[...].astype(F32)).astype(BF16)
-
-
-def cross_kernel(keep_ref, got_ref, pair_ref, far_ref, near_ref):
-    rows = far_ref.shape[0]
-    kept = keep_ref.shape[0] - 2 * rows
-    for place, o_ref in enumerate((far_ref, near_ref)):
-        o_ref[...] = (
-            keep_ref[pl.ds(kept + place * rows, rows), :]
-            + got_ref[pl.ds(place * rows, rows), :].astype(F32)
-            + pair_ref[pl.ds((1 - place) * rows, rows), :].astype(F32)
-        ).astype(o_ref.dtype)
+        o_ref[...] = total.astype(o_ref.dtype)
 
 
 def sum_kernel(first_ref, *refs):
@@ -335,26 +329,23 @@
 
     if split:
         block = (model // seqs, width // dps)
-        cuts = ((1, 3), (2, 0))
         weights = (*group, *grad_group)
-        gots = []
-        for steps in cuts:
-            send = call(
-                functools.partial(weight_kernel, seqs, 1, steps),
-                [out((len(steps) * block[0], block[1]), BF16)],
-                *weights,
-            )[0]
-            gots.append(flip_seq(send))
-        keep = call(
-            functools.partial(weight_kernel, seqs, 0, sum(cuts, ())),
-            [out((model // 2, block[1]), F32)],
-            *weights,
-        )[0]
-        near = call(fold_kernel, [out((2 * block[0], block[1]), BF16)], keep, gots[0])[0]
-        folded = call(
-            cross_kernel, [out(block, BF16), out(block, F32)], keep, gots[1], flip_seq(near, 2)
-        )
-        share = call(sum_kernel, [out(block, BF16)], folded[1], flip_seq(folded[0], 4))[0]
+
+        def formed(other, steps, dtype):
+            kernel = functools.partial(weight_kernel, seqs, dps, other, steps)
+            return dict(zip(steps, call(kernel, [out(block, dtype)] * len(steps), *weights)))
+
+        def added(dtype, *terms):
+            return call(sum_kernel, [out(block, dtype)], *terms)[0]
+
+        order = (3, 2, 1, 0)
+        sends = {**formed(1, order[:1], BF16), **formed(1, order[1:], BF16)}
+        got = {step: flip_seq(sends[step]) for step in order}
+        keep = formed(0, order, F32)
+        near = flip_seq(added(BF16, keep[3], got[3]), 2)
+        cross = flip_seq(added(BF16, keep[2], got[2], near), 4)
+        near = flip_seq(added(BF16, keep[1], got[1]), 2)
+        share = added(BF16, keep[0], got[0], near, cross)
     else:
         share = lax.psum_scatter(
             lax.dot_general(
@@ -367,12 +358,12 @@
             scatter_dimension=0,
             tiled=True,
         )
-    weight_grad = call(
-        join_kernel,
-        [out((share.shape[0], width), F32)],
-        share,
-        *[xor_dp(share, step) for step in range(1, dps)],
-    )[0]
+    shares = [share] + [xor_dp(share, step) for step in (1, 2) if step < dps]
+    if split:
+        shares.append(xor_dp(shares[2], 1))
+    else:
+        shares += [xor_dp(share, step) for step in range(3, dps)]
+    weight_grad = call(join_kernel, [out((share.shape[0], width), F32)], *shares)[0]
 
     block_qg = call(
         functools.partial(qg_kernel, heads, seqs, split, len(pair)),
@@ -391,15 +382,17 @@
         *prefix,
         scratch=scratch,
     )[0]
-    key_grad, value_grad = call(
-        functools.partial(pair_grad_kernel, factor, heads, states, seqs, split, len(pair)),
-        [out((rows, width), BF16)] * 2,
-        *pair,
-        keys,
-        values,
-        grads,
-        *suffix,
-        scratch=scratch,
+    key_grad, value_grad = (
+        call(
+            functools.partial(kernel, factor, heads, states, seqs, split, len(pair)),
+            [out((rows, width), BF16)],
+            *pair,
+            operand,
+            grads,
+            *suffix,
+            scratch=scratch,
+        )[0]
+        for kernel, operand in ((key_grad_kernel, values), (value_grad_kernel, keys))
     )
     return (attended[None], key_grad[None], value_grad[None], weight_grad)
 

time: 154 us -> 165 us (1.071)
  starting transfers between devices: 41.4 us -> 53.1 us
    ppermute x17 -> x20, waiting for transfers between devices: 44.7 us -> 59.1 us  [flip_seq(): return lax.ppermute(value, 'seq', [(i, i ^ bits) for i in range(seqs)])]
    ppermute x17 -> x20, starting transfers between devices: 27.9 us -> 39 us  [flip_seq(): return lax.ppermute(value, 'seq', [(i, i ^ bits) for i in range(seqs)])]
    ppermute x2, waiting for transfers between devices: 16.2 us -> 6.89 us  [carried(): lax.ppermute(quad, 'seq', list(zip(high, low) if backward else zip(low, h...]
    ppermute x13, waiting for transfers between devices: 25.9 us -> 19.3 us  [xor_dp(): return lax.ppermute(value, 'dp', [(i, i ^ step) for i in range(dps)])]
    ppermute x2, starting transfers between devices: 4.7 us -> 6.77 us  [carried(): lax.ppermute(quad, 'seq', list(zip(high, low) if backward else zip(low, h...]
    pallas_call x20 -> x22, Pallas kernels: 20.6 us -> 21.7 us  [call(): pl.pallas_call(kernel, out_shape=tuple(outs), in_specs=[pl.BlockSpec(memo...]
  transfers between devices with their start and end apart: 32 -> 35, of which waited for: 17 -> 17; matrix products, arithmetic and copies ran while one was open for 1% -> 0% of each run, Pallas kernels for 12% -> 12%
where the time goes in v4:
time: 165 us
  waiting for transfers between devices  85.3 us (52%)
  starting transfers between devices  53.1 us (32%)
  Pallas kernels  21.7 us (13%)
  local copies, waits for them, and re-layouts  3.45 us (2%)
    ppermute x20, waiting for transfers between devices, flip_seq(): return lax.ppermute(value, 'seq', [(i, i ^ bits) for i in range(seqs)])  59.1 us
    ppermute x20, starting transfers between devices, flip_seq(): return lax.ppermute(value, 'seq', [(i, i ^ bits) for i in range(seqs)])  39 us
    pallas_call x22, Pallas kernels, call(): pl.pallas_call(kernel, out_shape=tuple(outs), in_specs=[pl.BlockSpec(memo...  21.7 us
    ppermute x13, waiting for transfers between devices, xor_dp(): return lax.ppermute(value, 'dp', [(i, i ^ step) for i in range(dps)])  19.3 us
    ppermute x13, starting transfers between devices, xor_dp(): return lax.ppermute(value, 'dp', [(i, i ^ step) for i in range(dps)])  7.31 us
    ppermute x2, waiting for transfers between devices, carried(): lax.ppermute(quad, 'seq', list(zip(high, low) if backward else zip(low, h...  6.89 us
    ppermute x2, starting transfers between devices, carried(): lax.ppermute(quad, 'seq', list(zip(high, low) if backward else zip(low, h...  6.77 us
  transfers between devices with their start and end apart: 35, of which 17 were waited for; matrix products, arithmetic and copies ran while one was open for 0% of the time, Pallas kernels for 12%

profile of v4, /device:TPU:0, one launch (start us, length us, event | category | flops | bytes accessed | tf_op | source)
XLA Modules:
  0.0 164.9 jit_solution(12806662164755494622)
XLA Ops:
  1.6 4.1 %collective-permute-start.5 = (bf16[1024,128]{1,0:T(8,128)(2,1)S(1)}, bf16[1024,128]{1,0:T(8,128)(2,1)S(1)}, u32[]{:S(2)}, u32[]{:S(2)}) collective-permute-start(bf16[1024,128]{1,0:T(8,128)(2,1)S(1)} %dynamic_slice.3), channel_id=1, source_target_pairs={{0,16},{4,20},{8,24},{12,28},{16,0},{20,4},{24,8},{28,12},{1,17},{... | collective-permute-start | bytes 786440 | tf_op jit(solution)/shard_map/ppermute | solution.py:247
  5.8 1.6 collective-permute-start.2
  7.3 1.5 collective-permute-start.1
  8.9 8.9 %collective-permute-done.5 = bf16[1024,128]{1,0:T(8,128)(2,1)S(1)} collective-permute-done((bf16[1024,128]{1,0:T(8,128)(2,1)S(1)}, bf16[1024,128]{1,0:T(8,128)(2,1)S(1)}, u32[]{:S(2)}, u32[]{:S(2)}) %collective-permute-start.5) | collective-permute-done | bytes 262176 | tf_op jit(solution)/shard_map/ppermute | solution.py:247
  18.4 1.5 collective-permute-start.3
  19.9 1.5 collective-permute-start
  25.3 1.5 collective-permute-start.6
  27.7 11.9 %collective-permute-done.6 = bf16[1024,128]{1,0:T(8,128)(2,1)S(1)} collective-permute-done((bf16[1024,128]{1,0:T(8,128)(2,1)S(1)}, bf16[1024,128]{1,0:T(8,128)(2,1)S(1)}, u32[]{:S(2)}, u32[]{:S(2)}) %collective-permute-start.6) | collective-permute-done | bytes 262176 | tf_op jit(solution)/shard_map/ppermute | solution.py:247
  39.6 3.8 %collective-permute-done.8 = bf16[1024,128]{1,0:T(8,128)(2,1)S(1)} collective-permute-done((bf16[1024,128]{1,0:T(8,128)(2,1)S(1)}, bf16[1024,128]{1,0:T(8,128)(2,1)S(1)}, u32[]{:S(2)}, u32[]{:S(2)}) %collective-permute-start.8) | collective-permute-done | bytes 262176 | tf_op jit(solution)/shard_map/ppermute | solution.py:247
  44.7 7.8 %collective-permute-done.13.pair_ref = bf16[1024,128]{1,0:T(8,128)(2,1)S(1)} collective-permute-done((bf16[1024,128]{1,0:T(8,128)(2,1)S(1)}, bf16[1024,128]{1,0:T(8,128)(2,1)S(1)}, u32[]{:S(2)}, u32[]{:S(2)}) %collective-permute-start.13) | collective-permute-done | bytes 262176 | tf_op jit(solution)/shard_map/ppermute | solution.py:247
  52.6 5.3 %collective-permute-start.14 = (bf16[1024,128]{1,0:T(8,128)(2,1)S(1)}, bf16[1024,128]{1,0:T(8,128)(2,1)S(1)}, u32[]{:S(2)}, u32[]{:S(2)}) collective-permute-start(bf16[1024,128]{1,0:T(8,128)(2,1)S(1)} %shard_map.88), channel_id=1, source_target_pairs={{0,16},{4,20},{8,24},{12,28},{1,17},{5,21},{9,25},{13,29},{2,18},{... | collective-permute-start | bytes 786440 | tf_op jit(solution)/shard_map/ppermute | solution.py:264
  57.9 5.4 %collective-permute-done.14.quad_ref = bf16[1024,128]{1,0:T(8,128)(2,1)S(1)} collective-permute-done((bf16[1024,128]{1,0:T(8,128)(2,1)S(1)}, bf16[1024,128]{1,0:T(8,128)(2,1)S(1)}, u32[]{:S(2)}, u32[]{:S(2)}) %collective-permute-start.14) | collective-permute-done | bytes 262176 | tf_op jit(solution)/shard_map/ppermute | solution.py:264
  64.9 5.7 %collective-permute-done.15.refs_7_.refs_1_ = bf16[1024,128]{1,0:T(8,128)(2,1)S(1)} collective-permute-done((bf16[1024,128]{1,0:T(8,128)(2,1)S(1)}, bf16[1024,128]{1,0:T(8,128)(2,1)S(1)}, u32[]{:S(2)}, u32[]{:S(2)}) %collective-permute-start.15) | collective-permute-done | bytes 262176 | tf_op jit(solution)/shard_map/ppermute | solution.py:247
  70.5 2.0 %shard_map.97 = (bf16[256,512]{1,0:T(8,128)(2,1)S(1)}, bf16[256,512]{1,0:T(8,128)(2,1)S(1)}, bf16[256,512]{1,0:T(8,128)(2,1)S(1)}, bf16[256,512]{1,0:T(8,128)(2,1)S(1)}) custom-call(bf16[256,2048]{1,0:T(8,128)(2,1)S(1)} %bitcast.23, bf16[256,2048]{1,0:T(8,128)(2,1)S(1)} %bitcast.27, bf16[256,2048]{1,0:T(8,128)(2,1)S(1)} %bitcast.30, ...), custom_call_target="tpu_custom_call" | custom-call | bytes 4718592 | tf_op jit(solution)/shard_map/pallas_call | solution.py:28
  79.1 2.8 %collective-permute-done.23.refs_6_ = bf16[256,512]{1,0:T(8,128)(2,1)S(1)} collective-permute-done((bf16[256,512]{1,0:T(8,128)(2,1)S(1)}, bf16[256,512]{1,0:T(8,128)(2,1)S(1)}, u32[]{:S(2)}, u32[]{:S(2)}) %collective-permute-start.23) | collective-permute-done | bytes 262176 | tf_op jit(solution)/shard_map/ppermute | solution.py:244
  81.9 4.5 %collective-permute-done.24.refs_7_ = bf16[256,512]{1,0:T(8,128)(2,1)S(1)} collective-permute-done((bf16[256,512]{1,0:T(8,128)(2,1)S(1)}, bf16[256,512]{1,0:T(8,128)(2,1)S(1)}, u32[]{:S(2)}, u32[]{:S(2)}) %collective-permute-start.24) | collective-permute-done | bytes 262176 | tf_op jit(solution)/shard_map/ppermute | solution.py:244
  86.9 1.5 collective-permute-start.29
  88.4 4.7 %collective-permute-done.10.refs_2_ = bf16[256,512]{1,0:T(8,128)(2,1)S(1)} collective-permute-done((bf16[256,512]{1,0:T(8,128)(2,1)S(1)}, bf16[256,512]{1,0:T(8,128)(2,1)S(1)}, u32[]{:S(2)}, u32[]{:S(2)}) %collective-permute-start.10) | collective-permute-done | bytes 262176 | tf_op jit(solution)/shard_map/ppermute | solution.py:244
  93.1 5.1 %collective-permute-done.11.refs_3_ = bf16[256,512]{1,0:T(8,128)(2,1)S(1)} collective-permute-done((bf16[256,512]{1,0:T(8,128)(2,1)S(1)}, bf16[256,512]{1,0:T(8,128)(2,1)S(1)}, u32[]{:S(2)}, u32[]{:S(2)}) %collective-permute-start.11) | collective-permute-done | bytes 262176 | tf_op jit(solution)/shard_map/ppermute | solution.py:244
  104.7 5.9 %collective-permute-start.30 = (bf16[256,512]{1,0:T(8,128)(2,1)S(1)}, bf16[256,512]{1,0:T(8,128)(2,1)S(1)}, u32[]{:S(2)}, u32[]{:S(2)}) collective-permute-start(bf16[256,512]{1,0:T(8,128)(2,1)S(1)} %shard_map.102), channel_id=1, source_target_pairs={{0,8},{4,12},{8,0},{12,4},{16,24},{20,28},{24,16},{28,20},{1,9},{5... | collective-permute-start | bytes 786440 | tf_op jit(solution)/shard_map/ppermute | solution.py:247
  111.4 2.6 %collective-permute-start.17 = (bf16[1024,128]{1,0:T(8,128)(2,1)S(1)}, bf16[1024,128]{1,0:T(8,128)(2,1)S(1)}, u32[]{:S(2)}, u32[]{:S(2)}) collective-permute-start(bf16[1024,128]{1,0:T(8,128)(2,1)S(1)} %shard_map.92), channel_id=1, source_target_pairs={{0,8},{4,12},{8,0},{12,4},{16,24},{20,28},{24,16},{28,20},{1,9},{5... | collective-permute-start | bytes 786440 | tf_op jit(solution)/shard_map/ppermute | solution.py:247
  114.0 5.2 %collective-permute-done.26.refs_0_ = bf16[256,512]{1,0:T(8,128)(2,1)S(1)} collective-permute-done((bf16[256,512]{1,0:T(8,128)(2,1)S(1)}, bf16[256,512]{1,0:T(8,128)(2,1)S(1)}, u32[]{:S(2)}, u32[]{:S(2)}) %collective-permute-start.26) | collective-permute-done | bytes 262176 | tf_op jit(solution)/shard_map/ppermute | solution.py:247
  119.3 5.9 %collective-permute-start.27 = (bf16[256,512]{1,0:T(8,128)(2,1)S(1)}, bf16[256,512]{1,0:T(8,128)(2,1)S(1)}, u32[]{:S(2)}, u32[]{:S(2)}) collective-permute-start(bf16[256,512]{1,0:T(8,128)(2,1)S(1)} %shard_map.100), channel_id=1, source_target_pairs={{0,8},{4,12},{8,0},{12,4},{16,24},{20,28},{24,16},{28,20},{1,9},{5... | collective-permute-start | bytes 786440 | tf_op jit(solution)/shard_map/ppermute | solution.py:247
  125.3 3.4 %collective-permute-start.31 = (bf16[256,512]{1,0:T(8,128)(2,1)S(1)}, bf16[256,512]{1,0:T(8,128)(2,1)S(1)}, u32[]{:S(2)}, u32[]{:S(2)}) collective-permute-start(bf16[256,512]{1,0:T(8,128)(2,1)S(1)} %shard_map.103), channel_id=1, source_target_pairs={{0,16},{4,20},{8,24},{12,28},{16,0},{20,4},{24,8},{28,12},{1,17},{... | collective-permute-start | bytes 786440 | tf_op jit(solution)/shard_map/ppermute | solution.py:247
  128.9 1.5 collective-permute-start.18
  130.4 3.6 %collective-permute-done.27.refs_1_ = bf16[256,512]{1,0:T(8,128)(2,1)S(1)} collective-permute-done((bf16[256,512]{1,0:T(8,128)(2,1)S(1)}, bf16[256,512]{1,0:T(8,128)(2,1)S(1)}, u32[]{:S(2)}, u32[]{:S(2)}) %collective-permute-start.27) | collective-permute-done | bytes 262176 | tf_op jit(solution)/shard_map/ppermute | solution.py:247
  134.0 12.2 %collective-permute-done.31.refs_2_ = bf16[256,512]{1,0:T(8,128)(2,1)S(1)} collective-permute-done((bf16[256,512]{1,0:T(8,128)(2,1)S(1)}, bf16[256,512]{1,0:T(8,128)(2,1)S(1)}, u32[]{:S(2)}, u32[]{:S(2)}) %collective-permute-start.31) | collective-permute-done | bytes 262176 | tf_op jit(solution)/shard_map/ppermute | solution.py:247
  147.7 1.5 collective-permute-done.18.quad_ref
  150.8 1.9 %collective-permute-done.33.refs_2_ = bf16[256,512]{1,0:T(8,128)(2,1)S(1)} collective-permute-done((bf16[256,512]{1,0:T(8,128)(2,1)S(1)}, bf16[256,512]{1,0:T(8,128)(2,1)S(1)}, u32[]{:S(2)}, u32[]{:S(2)}) %collective-permute-start.33) | collective-permute-done | bytes 262176 | tf_op jit(solution)/shard_map/ppermute | solution.py:244
  152.7 3.0 %shard_map.90 = bf16[256,2048]{1,0:T(8,128)(2,1)} custom-call(bf16[256,512]{1,0:T(8,128)(2,1)S(1)} %get-tuple-element.27.refs_0_, bf16[256,512]{1,0:T(8,128)(2,1)S(1)} %get-tuple-element.28.refs_1_, bf16[256,512]{1,0:T(8,128)(2,1)S(1)} %collective-permute-done.10.refs_2_, bf16[256,512]{1,0:T(8,128)(2,1)S(1)} %collective-permute-done.11.refs_3_, ...), custom_call_target="tpu_custom_call" | custom-call | bytes 4718592 | tf_op jit(solution)/shard_map/pallas_call | solution.py:28
  155.8 3.8 %shard_map.96 = bf16[256,2048]{1,0:T(8,128)(2,1)} custom-call(bf16[256,512]{1,0:T(8,128)(2,1)S(1)} %get-tuple-element.27.refs_0_, bf16[256,512]{1,0:T(8,128)(2,1)S(1)} %get-tuple-element.28.refs_1_, bf16[256,512]{1,0:T(8,128)(2,1)S(1)} %collective-permute-done.10.refs_2_, bf16[256,512]{1,0:T(8,128)(2,1)S(1)} %collective-permute-done.11.refs_3_, ...), custom_call_target="tpu_custom_call" | custom-call | bytes 4718592 | tf_op jit(solution)/shard_map/pallas_call | solution.py:28
  159.6 3.8 %shard_map.95 = bf16[256,2048]{1,0:T(8,128)(2,1)} custom-call(bf16[256,512]{1,0:T(8,128)(2,1)S(1)} %get-tuple-element.27.refs_0_, bf16[256,512]{1,0:T(8,128)(2,1)S(1)} %get-tuple-element.28.refs_1_, bf16[256,512]{1,0:T(8,128)(2,1)S(1)} %collective-permute-done.10.refs_2_, bf16[256,512]{1,0:T(8,128)(2,1)S(1)} %collective-permute-done.11.refs_3_, ...), custom_call_target="tpu_custom_call" | custom-call | bytes 4718592 | tf_op jit(solution)/shard_map/pallas_call | solution.py:28
  (79 shorter events, 28.4 us)
Async XLA Ops:
  1.6 16.2 %collective-permute-start.5 = (bf16[1024,128]{1,0:T(8,128)(2,1)S(1)}, bf16[1024,128]{1,0:T(8,128)(2,1)S(1)}, u32[]{:S(2)}, u32[]{:S(2)}) collective-permute-start(bf16[1024,128]{1,0:T(8,128)(2,1)S(1)} %dynamic_slice.3), channel_id=1, source_target_pairs={{0,16},{4,20},{8,24},{12,28},{16,0},{20,4},{24,8},{28,12},{1,17},{... | collective-permute-start | bytes 786440 | tf_op jit(solution)/shard_map/ppermute | solution.py:247
  5.8 12.6 %collective-permute-start.2 = (bf16[1024,128]{1,0:T(8,128)(2,1)S(1)}, bf16[1024,128]{1,0:T(8,128)(2,1)S(1)}, u32[]{:S(2)}, u32[]{:S(2)}) collective-permute-start(bf16[1024,128]{1,0:T(8,128)(2,1)S(1)} %dynamic_slice.3), channel_id=1, source_target_pairs={{0,8},{4,12},{8,0},{12,4},{16,24},{20,28},{24,16},{28,20},{1,9},{5... | collective-permute-start | bytes 786440 | tf_op jit(solution)/shard_map/ppermute | solution.py:247
  7.3 17.9 %collective-permute-start.1 = (bf16[1024,128]{1,0:T(8,128)(2,1)S(1)}, bf16[1024,128]{1,0:T(8,128)(2,1)S(1)}, u32[]{:S(2)}, u32[]{:S(2)}) collective-permute-start(bf16[1024,128]{1,0:T(8,128)(2,1)S(1)} %dynamic_slice.3), channel_id=1, source_target_pairs={{0,4},{4,0},{8,12},{12,8},{16,20},{20,16},{24,28},{28,24},{1,5},{5... | collective-permute-start | bytes 786440 | tf_op jit(solution)/shard_map/ppermute | solution.py:247
  17.8 9.1 %collective-permute-start.7 = (bf16[1024,128]{1,0:T(8,128)(2,1)S(1)}, bf16[1024,128]{1,0:T(8,128)(2,1)S(1)}, u32[]{:S(2)}, u32[]{:S(2)}) collective-permute-start(bf16[1024,128]{1,0:T(8,128)(2,1)S(1)} %collective-permute-done.5), channel_id=1, source_target_pairs={{0,8},{4,12},{8,0},{12,4},{16,24},{20,28},{24,16},{28,20},{1,9},{5... | collective-permute-start | bytes 786440 | tf_op jit(solution)/shard_map/ppermute | solution.py:247
  18.4 9.0 %collective-permute-start.3 = (bf16[1024,128]{1,0:T(8,128)(2,1)S(1)}, bf16[1024,128]{1,0:T(8,128)(2,1)S(1)}, u32[]{:S(2)}, u32[]{:S(2)}) collective-permute-start(bf16[1024,128]{1,0:T(8,128)(2,1)S(1)} %collective-permute-done.2), channel_id=1, source_target_pairs={{0,4},{4,0},{8,12},{12,8},{16,20},{20,16},{24,28},{28,24},{1,5},{5... | collective-permute-start | bytes 786440 | tf_op jit(solution)/shard_map/ppermute | solution.py:247
  19.9 24.7 %collective-permute-start = (bf16[256,2048]{1,0:T(8,128)(2,1)}, bf16[256,2048]{1,0:T(8,128)(2,1)S(1)}, u32[]{:S(2)}, u32[]{:S(2)}) collective-permute-start(bf16[256,2048]{1,0:T(8,128)(2,1)} %bitcast.15), channel_id=1, source_target_pairs={{0,2},{1,3},{2,0},{3,1},{4,6},{5,7},{6,4},{7,5},{8,10},{9,11},{10,... | collective-permute-start | bytes 3145736 | tf_op jit(solution)/shard_map/ppermute | solution.py:244
  24.7 19.0 %collective-permute-start.12 = (bf16[1024,128]{1,0:T(8,128)(2,1)S(1)}, bf16[1024,128]{1,0:T(8,128)(2,1)S(1)}, u32[]{:S(2)}, u32[]{:S(2)}) collective-permute-start(bf16[1024,128]{1,0:T(8,128)(2,1)S(1)} %get-tuple-element.32), channel_id=1, source_target_pairs={{0,4},{4,0},{8,12},{12,8},{16,20},{20,16},{24,28},{28,24},{1,5},{5... | collective-permute-start | bytes 786440 | tf_op jit(solution)/shard_map/ppermute | solution.py:247
  25.3 14.3 %collective-permute-start.6 = (bf16[1024,128]{1,0:T(8,128)(2,1)S(1)}, bf16[1024,128]{1,0:T(8,128)(2,1)S(1)}, u32[]{:S(2)}, u32[]{:S(2)}) collective-permute-start(bf16[1024,128]{1,0:T(8,128)(2,1)S(1)} %collective-permute-done.5), channel_id=1, source_target_pairs={{0,4},{4,0},{8,12},{12,8},{16,20},{20,16},{24,28},{28,24},{1,5},{5... | collective-permute-start | bytes 786440 | tf_op jit(solution)/shard_map/ppermute | solution.py:247
  26.9 16.5 %collective-permute-start.8 = (bf16[1024,128]{1,0:T(8,128)(2,1)S(1)}, bf16[1024,128]{1,0:T(8,128)(2,1)S(1)}, u32[]{:S(2)}, u32[]{:S(2)}) collective-permute-start(bf16[1024,128]{1,0:T(8,128)(2,1)S(1)} %collective-permute-done.7), channel_id=1, source_target_pairs={{0,4},{4,0},{8,12},{12,8},{16,20},{20,16},{24,28},{28,24},{1,5},{5... | collective-permute-start | bytes 786440 | tf_op jit(solution)/shard_map/ppermute | solution.py:247
  27.6 45.0 %collective-permute-start.4 = (bf16[2,1024,256]{2,1,0:T(8,128)(2,1)S(1)}, bf16[2,1024,256]{2,1,0:T(8,128)(2,1)S(1)}, u32[]{:S(2)}, u32[]{:S(2)}) collective-permute-start(bf16[2,1024,256]{2,1,0:T(8,128)(2,1)S(1)} %pad_maximum_fusion.near_ref), channel_id=1, source_target_pairs={{0,1},{1,0},{2,3},{3,2},{4,5},{5,4},{6,7},{7,6},{8,9},{9,8},{10,11... | collective-permute-start | bytes 3145736 | tf_op jit(solution)/shard_map/ppermute | solution.py:244
  43.6 30.4 %collective-permute-start.9 = (bf16[2,1024,256]{2,1,0:T(8,128)(2,1)S(1)}, bf16[2,1024,256]{2,1,0:T(8,128)(2,1)S(1)}, u32[]{:S(2)}, u32[]{:S(2)}) collective-permute-start(bf16[2,1024,256]{2,1,0:T(8,128)(2,1)S(1)} %pad_maximum_fusion.1.near_ref), channel_id=1, source_target_pairs={{0,1},{1,0},{2,3},{3,2},{4,5},{5,4},{6,7},{7,6},{8,9},{9,8},{10,11... | collective-permute-start | bytes 3145736 | tf_op jit(solution)/shard_map/ppermute | solution.py:244
  43.7 8.8 %collective-permute-start.13 = (bf16[1024,128]{1,0:T(8,128)(2,1)S(1)}, bf16[1024,128]{1,0:T(8,128)(2,1)S(1)}, u32[]{:S(2)}, u32[]{:S(2)}) collective-permute-start(bf16[1024,128]{1,0:T(8,128)(2,1)S(1)} %shard_map.87), channel_id=1, source_target_pairs={{0,8},{4,12},{8,0},{12,4},{16,24},{20,28},{24,16},{28,20},{1,9},{5... | collective-permute-start | bytes 786440 | tf_op jit(solution)/shard_map/ppermute | solution.py:247
  44.2 32.8 %collective-permute-start.20 = (bf16[256,2048]{1,0:T(8,128)(2,1)S(1)}, bf16[256,2048]{1,0:T(8,128)(2,1)S(1)}, u32[]{:S(2)}, u32[]{:S(2)}) collective-permute-start(bf16[256,2048]{1,0:T(8,128)(2,1)S(1)} %bitcast.16), channel_id=1, source_target_pairs={{0,1},{1,0},{2,3},{3,2},{4,5},{5,4},{6,7},{7,6},{8,9},{9,8},{10,11... | collective-permute-start | bytes 3145736 | tf_op jit(solution)/shard_map/ppermute | solution.py:244
  44.7 41.7 %collective-permute-start.21 = (bf16[256,2048]{1,0:T(8,128)(2,1)S(1)}, bf16[256,2048]{1,0:T(8,128)(2,1)S(1)}, u32[]{:S(2)}, u32[]{:S(2)}) collective-permute-start(bf16[256,2048]{1,0:T(8,128)(2,1)S(1)} %collective-permute-done.theirs_ref.refs_2_), channel_id=1, source_target_pairs={{0,1},{1,0},{2,3},{3,2},{4,5},{5,4},{6,7},{7,6},{8,9},{9,8},{10,11... | collective-permute-start | bytes 3145736 | tf_op jit(solution)/shard_map/ppermute | solution.py:244
  52.6 10.7 %collective-permute-start.14 = (bf16[1024,128]{1,0:T(8,128)(2,1)S(1)}, bf16[1024,128]{1,0:T(8,128)(2,1)S(1)}, u32[]{:S(2)}, u32[]{:S(2)}) collective-permute-start(bf16[1024,128]{1,0:T(8,128)(2,1)S(1)} %shard_map.88), channel_id=1, source_target_pairs={{0,16},{4,20},{8,24},{12,28},{1,17},{5,21},{9,25},{13,29},{2,18},{... | collective-permute-start | bytes 786440 | tf_op jit(solution)/shard_map/ppermute | solution.py:264
  63.4 7.1 %collective-permute-start.15 = (bf16[1024,128]{1,0:T(8,128)(2,1)S(1)}, bf16[1024,128]{1,0:T(8,128)(2,1)S(1)}, u32[]{:S(2)}, u32[]{:S(2)}) collective-permute-start(bf16[1024,128]{1,0:T(8,128)(2,1)S(1)} %get-tuple-element.34), channel_id=1, source_target_pairs={{0,4},{4,0},{8,12},{12,8},{16,20},{20,16},{24,28},{28,24},{1,5},{5... | collective-permute-start | bytes 786440 | tf_op jit(solution)/shard_map/ppermute | solution.py:247
  72.6 9.2 %collective-permute-start.23 = (bf16[256,512]{1,0:T(8,128)(2,1)S(1)}, bf16[256,512]{1,0:T(8,128)(2,1)S(1)}, u32[]{:S(2)}, u32[]{:S(2)}) collective-permute-start(bf16[256,512]{1,0:T(8,128)(2,1)S(1)} %get-tuple-element.41), channel_id=1, source_target_pairs={{0,2},{1,3},{2,0},{3,1},{4,6},{5,7},{6,4},{7,5},{8,10},{9,11},{10,... | collective-permute-start | bytes 786440 | tf_op jit(solution)/shard_map/ppermute | solution.py:244
  74.0 12.4 %collective-permute-start.24 = (bf16[256,512]{1,0:T(8,128)(2,1)S(1)}, bf16[256,512]{1,0:T(8,128)(2,1)S(1)}, u32[]{:S(2)}, u32[]{:S(2)}) collective-permute-start(bf16[256,512]{1,0:T(8,128)(2,1)S(1)} %get-tuple-element.42), channel_id=1, source_target_pairs={{0,3},{1,2},{2,1},{3,0},{4,7},{5,6},{6,5},{7,4},{8,11},{9,10},{10,... | collective-permute-start | bytes 786440 | tf_op jit(solution)/shard_map/ppermute | solution.py:244
  77.0 16.1 %collective-permute-start.10 = (bf16[256,512]{1,0:T(8,128)(2,1)S(1)}, bf16[256,512]{1,0:T(8,128)(2,1)S(1)}, u32[]{:S(2)}, u32[]{:S(2)}) collective-permute-start(bf16[256,512]{1,0:T(8,128)(2,1)S(1)} %get-tuple-element.29), channel_id=1, source_target_pairs={{0,2},{1,3},{2,0},{3,1},{4,6},{5,7},{6,4},{7,5},{8,10},{9,11},{10,... | collective-permute-start | bytes 786440 | tf_op jit(solution)/shard_map/ppermute | solution.py:244
  78.4 19.8 %collective-permute-start.11 = (bf16[256,512]{1,0:T(8,128)(2,1)S(1)}, bf16[256,512]{1,0:T(8,128)(2,1)S(1)}, u32[]{:S(2)}, u32[]{:S(2)}) collective-permute-start(bf16[256,512]{1,0:T(8,128)(2,1)S(1)} %get-tuple-element.30), channel_id=1, source_target_pairs={{0,2},{1,3},{2,0},{3,1},{4,6},{5,7},{6,4},{7,5},{8,10},{9,11},{10,... | collective-permute-start | bytes 786440 | tf_op jit(solution)/shard_map/ppermute | solution.py:244
  86.9 17.7 %collective-permute-start.29 = (bf16[256,512]{1,0:T(8,128)(2,1)S(1)}, bf16[256,512]{1,0:T(8,128)(2,1)S(1)}, u32[]{:S(2)}, u32[]{:S(2)}) collective-permute-start(bf16[256,512]{1,0:T(8,128)(2,1)S(1)} %shard_map.101), channel_id=1, source_target_pairs={{0,4},{4,0},{8,12},{12,8},{16,20},{20,16},{24,28},{28,24},{1,5},{5... | collective-permute-start | bytes 786440 | tf_op jit(solution)/shard_map/ppermute | solution.py:247
  98.8 12.6 %collective-permute-start.16 = (bf16[1024,128]{1,0:T(8,128)(2,1)S(1)}, bf16[1024,128]{1,0:T(8,128)(2,1)S(1)}, u32[]{:S(2)}, u32[]{:S(2)}) collective-permute-start(bf16[1024,128]{1,0:T(8,128)(2,1)S(1)} %get-tuple-element.36), channel_id=1, source_target_pairs={{0,4},{4,0},{8,12},{12,8},{16,20},{20,16},{24,28},{28,24},{1,5},{5... | collective-permute-start | bytes 786440 | tf_op jit(solution)/shard_map/ppermute | solution.py:247
  101.2 24.0 %collective-permute-start.28 = (bf16[256,512]{1,0:T(8,128)(2,1)S(1)}, bf16[256,512]{1,0:T(8,128)(2,1)S(1)}, u32[]{:S(2)}, u32[]{:S(2)}) collective-permute-start(bf16[256,512]{1,0:T(8,128)(2,1)S(1)} %get-tuple-element.48), channel_id=1, source_target_pairs={{0,4},{4,0},{8,12},{12,8},{16,20},{20,16},{24,28},{28,24},{1,5},{5... | collective-permute-start | bytes 786440 | tf_op jit(solution)/shard_map/ppermute | solution.py:247
  102.0 17.3 %collective-permute-start.26 = (bf16[256,512]{1,0:T(8,128)(2,1)S(1)}, bf16[256,512]{1,0:T(8,128)(2,1)S(1)}, u32[]{:S(2)}, u32[]{:S(2)}) collective-permute-start(bf16[256,512]{1,0:T(8,128)(2,1)S(1)} %get-tuple-element.46), channel_id=1, source_target_pairs={{0,4},{4,0},{8,12},{12,8},{16,20},{20,16},{24,28},{28,24},{1,5},{5... | collective-permute-start | bytes 786440 | tf_op jit(solution)/shard_map/ppermute | solution.py:247
  104.7 20.5 %collective-permute-start.30 = (bf16[256,512]{1,0:T(8,128)(2,1)S(1)}, bf16[256,512]{1,0:T(8,128)(2,1)S(1)}, u32[]{:S(2)}, u32[]{:S(2)}) collective-permute-start(bf16[256,512]{1,0:T(8,128)(2,1)S(1)} %shard_map.102), channel_id=1, source_target_pairs={{0,8},{4,12},{8,0},{12,4},{16,24},{20,28},{24,16},{28,20},{1,9},{5... | collective-permute-start | bytes 786440 | tf_op jit(solution)/shard_map/ppermute | solution.py:247
  110.6 19.7 %collective-permute-start.25 = (bf16[256,512]{1,0:T(8,128)(2,1)S(1)}, bf16[256,512]{1,0:T(8,128)(2,1)S(1)}, u32[]{:S(2)}, u32[]{:S(2)}) collective-permute-start(bf16[256,512]{1,0:T(8,128)(2,1)S(1)} %get-tuple-element.44), channel_id=1, source_target_pairs={{0,4},{4,0},{8,12},{12,8},{16,20},{20,16},{24,28},{28,24},{1,5},{5... | collective-permute-start | bytes 786440 | tf_op jit(solution)/shard_map/ppermute | solution.py:247
  111.4 17.4 %collective-permute-start.17 = (bf16[1024,128]{1,0:T(8,128)(2,1)S(1)}, bf16[1024,128]{1,0:T(8,128)(2,1)S(1)}, u32[]{:S(2)}, u32[]{:S(2)}) collective-permute-start(bf16[1024,128]{1,0:T(8,128)(2,1)S(1)} %shard_map.92), channel_id=1, source_target_pairs={{0,8},{4,12},{8,0},{12,4},{16,24},{20,28},{24,16},{28,20},{1,9},{5... | collective-permute-start | bytes 786440 | tf_op jit(solution)/shard_map/ppermute | solution.py:247
  119.3 14.7 %collective-permute-start.27 = (bf16[256,512]{1,0:T(8,128)(2,1)S(1)}, bf16[256,512]{1,0:T(8,128)(2,1)S(1)}, u32[]{:S(2)}, u32[]{:S(2)}) collective-permute-start(bf16[256,512]{1,0:T(8,128)(2,1)S(1)} %shard_map.100), channel_id=1, source_target_pairs={{0,8},{4,12},{8,0},{12,4},{16,24},{20,28},{24,16},{28,20},{1,9},{5... | collective-permute-start | bytes 786440 | tf_op jit(solution)/shard_map/ppermute | solution.py:247
  125.3 20.8 %collective-permute-start.31 = (bf16[256,512]{1,0:T(8,128)(2,1)S(1)}, bf16[256,512]{1,0:T(8,128)(2,1)S(1)}, u32[]{:S(2)}, u32[]{:S(2)}) collective-permute-start(bf16[256,512]{1,0:T(8,128)(2,1)S(1)} %shard_map.103), channel_id=1, source_target_pairs={{0,16},{4,20},{8,24},{12,28},{16,0},{20,4},{24,8},{28,12},{1,17},{... | collective-permute-start | bytes 786440 | tf_op jit(solution)/shard_map/ppermute | solution.py:247
  128.9 20.3 %collective-permute-start.18 = (bf16[1024,128]{1,0:T(8,128)(2,1)S(1)}, bf16[1024,128]{1,0:T(8,128)(2,1)S(1)}, u32[]{:S(2)}, u32[]{:S(2)}) collective-permute-start(bf16[1024,128]{1,0:T(8,128)(2,1)S(1)} %shard_map.93), channel_id=1, source_target_pairs={{16,0},{20,4},{24,8},{28,12},{17,1},{21,5},{25,9},{29,13},{18,2},{... | collective-permute-start | bytes 786440 | tf_op jit(solution)/shard_map/ppermute | solution.py:264
  150.8 12.6 %collective-permute-start.32 = (bf16[256,512]{1,0:T(8,128)(2,1)S(1)}, bf16[256,512]{1,0:T(8,128)(2,1)S(1)}, u32[]{:S(2)}, u32[]{:S(2)}) collective-permute-start(bf16[256,512]{1,0:T(8,128)(2,1)S(1)} %shard_map.104.refs_0_), channel_id=1, source_target_pairs={{0,1},{1,0},{2,3},{3,2},{4,5},{5,4},{6,7},{7,6},{8,9},{9,8},{10,11... | collective-permute-start | bytes 786440 | tf_op jit(solution)/shard_map/ppermute | solution.py:244
  152.7 10.7 %collective-permute-start.34 = (bf16[256,512]{1,0:T(8,128)(2,1)S(1)}, bf16[256,512]{1,0:T(8,128)(2,1)S(1)}, u32[]{:S(2)}, u32[]{:S(2)}) collective-permute-start(bf16[256,512]{1,0:T(8,128)(2,1)S(1)} %collective-permute-done.33.refs_2_), channel_id=1, source_target_pairs={{0,1},{1,0},{2,3},{3,2},{4,5},{5,4},{6,7},{7,6},{8,9},{9,8},{10,11... | collective-permute-start | bytes 786440 | tf_op jit(solution)/shard_map/ppermute | solution.py:244
  (9 other events, 106.7 us)

commit v5 on v4

--- a/solution.py
+++ b/solution.py
@@ -40,10 +40,9 @@
     return jax.ShapeDtypeStruct(shape, dtype)
 
 
-def causal(rows):
-    return lax.broadcasted_iota(jnp.int32, (rows, rows), 0) >= lax.broadcasted_iota(
-        jnp.int32, (rows, rows), 1
-    )
+def causal(rows, query_axis=0):
+    axes = [lax.broadcasted_iota(jnp.int32, (rows, rows), axis) for axis in (0, 1)]
+    return axes[query_axis] >= axes[1 - query_axis]
 
 
 def scores(a, b, mask, factor):
@@ -91,18 +90,32 @@
 
 
 def quad_kernel(keep_ref, got_ref, pair_ref, o_ref):
+    z = lax.rem(lax.axis_index("seq") // 2, 2)
+    rows = o_ref.shape[0]
+    if rows == keep_ref.shape[0]:
+        part = pl.ds(0, rows)
+    else:
+        part = lanes(z, rows)
     o_ref[...] = (
-        keep_ref[...] + got_ref[...].astype(F32) + pair_ref[...].astype(F32)
+        keep_ref[part, :] + got_ref[part, :].astype(F32) + pair_ref[part, :].astype(F32)
     ).astype(BF16)
 
 
-def carry_kernel(backward, keep_ref, got_ref, pair_ref, quad_ref, mine_ref, theirs_ref):
+def carry_kernel(backward, keep_ref, got_ref, pair_ref, *refs):
+    *quad_refs, mine_ref, theirs_ref = refs
     s = lax.axis_index("seq")
     y, z = lax.rem(s, 2), lax.rem(s // 2, 2)
     later = 0 if backward else 1
-    base = quad_ref[...].astype(F32) + jnp.where(z == later, pair_ref[...].astype(F32), 0.0)
-    mine_ref[...] = (base + jnp.where(y == later, got_ref[...].astype(F32), 0.0)).astype(BF16)
-    theirs_ref[...] = (base + jnp.where(y == later, 0.0, keep_ref[...])).astype(BF16)
+    rows = quad_refs[0].shape[0]
+    for n, quad_ref in enumerate(quad_refs):
+        part = pl.ds(0, rows) if len(quad_refs) == 1 else lanes(lax.rem(z + n, 2), rows)
+        base = quad_ref[...].astype(F32) + jnp.where(
+            z == later, pair_ref[part, :].astype(F32), 0.0
+        )
+        mine_ref[part, :] = (
+            base + jnp.where(y == later, got_ref[part, :].astype(F32), 0.0)
+        ).astype(BF16)
+        theirs_ref[part, :] = (base + jnp.where(y == later, 0.0, keep_ref[part, :])).astype(BF16)
 
 
 def whole_state(refs):
@@ -126,14 +139,14 @@
         total = total + i_ref[block, :].astype(F32)
 
 
-def query_grad_kernel(factor, heads, states, k_ref, v_ref, g_ref, *refs):
+def query_grad_kernel(factor, heads, states, part, parts, k_ref, v_ref, g_ref, *refs):
     o_refs = refs[states : len(refs) - states + 1]
     p_ref = whole_state(refs[:states] + refs[len(refs) - states + 1 :])
     mask = causal(k_ref.shape[0])
     d = lax.axis_index("dp")
-    per = heads // len(o_refs)
+    per = heads // len(o_refs) // parts
     for step, o_ref in enumerate(o_refs):
-        base = jnp.bitwise_xor(d, step) * per
+        base = (jnp.bitwise_xor(d, step) * parts + part) * per
         for j in range(per):
             cols = lanes(base + j)
             g = g_ref[:, cols]
@@ -163,15 +176,15 @@
     q_refs, (v_ref, g_ref), refs = refs[:count], refs[count : count + 2], refs[count + 2 :]
     o_ref = refs[states]
     s_ref = whole_state(refs[:states] + refs[states + 1 :])
-    mask = causal(v_ref.shape[0])
+    mask = causal(v_ref.shape[0], 1)
     for slot in range(heads):
         ref = q_refs[slot * count // heads]
         cols = lanes(head_of(slot, shards, inter))
         q = ref[:, pl.ds(slot % (heads // count) * DH, DH)]
         v = v_ref[:, cols]
-        grad_scores = scores(g_ref[:, cols], v, mask, factor)
+        grad_scores = scores(v, g_ref[:, cols], mask, factor)
         o_ref[:, cols] = (
-            dot(grad_scores, q, (0, 0)) + factor * dot(v, s_ref[cols, :], (1, 1))
+            dot(grad_scores, q, (1, 0)) + factor * dot(v, s_ref[cols, :], (1, 1))
         ).astype(BF16)
 
 
@@ -179,15 +192,15 @@
     q_refs, (k_ref, g_ref), refs = refs[:count], refs[count : count + 2], refs[count + 2 :]
     o_ref = refs[states]
     s_ref = whole_state(refs[:states] + refs[states + 1 :])
-    mask = causal(k_ref.shape[0])
+    mask = causal(k_ref.shape[0], 1)
     for slot in range(heads):
         ref = q_refs[slot * count // heads]
         cols = lanes(head_of(slot, shards, inter))
         q = ref[:, pl.ds(slot % (heads // count) * DH, DH)]
         k = k_ref[:, cols]
-        key_scores = scores(q, k, mask, factor)
+        key_scores = scores(k, q, mask, factor)
         o_ref[:, cols] = (
-            dot(key_scores, g_ref[:, cols], (0, 0)) + factor * dot(k, s_ref[cols, :], (1, 0))
+            dot(key_scores, g_ref[:, cols], (1, 0)) + factor * dot(k, s_ref[cols, :], (1, 0))
         ).astype(BF16)
 
 
@@ -207,20 +220,39 @@
 def weight_kernel(count, pairs, other, steps, *refs):
     rows = refs[0].shape[1] // count
     s = lax.axis_index("seq")
-    for step, o_ref in zip(steps, refs[2 * pairs :]):
+    t_refs, g_refs, o_ref = refs[:pairs], refs[pairs:-1], refs[-1]
+    width = g_refs[0].shape[1]
+    for place, step in enumerate(steps):
         target = jnp.bitwise_xor(s, step * 2 + other)
-        total = None
-        for t_ref, g_ref in zip(refs[:pairs], refs[pairs : 2 * pairs]):
-            term = dot(t_ref[:, lanes(target, rows)], g_ref[...], (0, 0))
-            total = term if total is None else total + term
-        o_ref[...] = total.astype(o_ref.dtype)
-
-
-def sum_kernel(first_ref, *refs):
-    total = first_ref[...]
-    for ref in refs[:-1]:
-        total = total + ref[...].astype(F32)
-    refs[-1][...] = total.astype(refs[-1].dtype)
+        for part in range(len(g_refs) // pairs):
+            total = None
+            for t_ref, g_ref in zip(t_refs, g_refs[part * pairs :]):
+                term = dot(t_ref[:, lanes(target, rows)], g_ref[...], (0, 0))
+                total = term if total is None else total + term
+            o_ref[pl.ds(place * rows, rows), pl.ds(part * width, width)] = total.astype(
+                o_ref.dtype
+            )
+
+
+def sum_kernel(starts, *refs):
+    o_ref = refs[-1]
+    rows, width = o_ref.shape
+    total = None
+    for (row, col), ref in zip(starts, refs[:-1]):
+        term = ref[pl.ds(row, rows), pl.ds(col, width)].astype(F32)
+        total = term if total is None else total + term
+    o_ref[...] = total.astype(o_ref.dtype)
+
+
+def share_kernel(row, keep_ref, got_ref, near_ref, *refs):
+    o_ref = refs[-1]
+    rows = o_ref.shape[0]
+    width = refs[0].shape[1]
+    for part, cross_ref in enumerate(refs[:-1]):
+        cols = pl.ds(part * width, width)
+        total = keep_ref[pl.ds(row, rows), cols] + got_ref[pl.ds(rows, rows), cols].astype(F32)
+        total = total + near_ref[:, cols].astype(F32) + cross_ref[...].astype(F32)
+        o_ref[:, cols] = total.astype(o_ref.dtype)
 
 
 def join_kernel(*refs):
@@ -228,6 +260,9 @@
     width = refs[0].shape[1]
     for step, ref in enumerate(refs[:-1]):
         refs[-1][:, lanes(jnp.bitwise_xor(d, step), width)] = ref[...].astype(F32)
+
+
+HALVED = ("qg",)
 
 
 def body(tokens, query_weight, key_rows, value_rows, out_grad):
@@ -249,7 +284,7 @@
     def swap(value):
         return lax.all_to_all(value, "seq", 0, 0, tiled=True)
 
-    def carried(blocks, backward):
+    def carried(name, blocks, backward):
         if not split:
             scan = functools.partial(scan_kernel, seqs, backward)
             got = swap(blocks[0])
@@ -259,13 +294,15 @@
         got = flip_seq(send)
         pair = call(pair_kernel, [part], keep, got)[0]
         pair = flip_seq(pair, 2)
-        quad = call(quad_kernel, [part], keep, got, pair)[0]
+        thin = out((part.shape[0] // 2, DH), BF16) if name in HALVED else part
+        quad = call(quad_kernel, [thin], keep, got, pair)[0]
         low, high = range(4), range(4, 8)
         quad = lax.ppermute(
             quad, "seq", list(zip(high, low) if backward else zip(low, high))
         )
+        quads = [quad, flip_seq(quad, 2)] if name in HALVED else [quad]
         mine, theirs = call(
-            functools.partial(carry_kernel, backward), [part, part], keep, got, pair, quad
+            functools.partial(carry_kernel, backward), [part, part], keep, got, pair, *quads
         )
         return [mine, flip_seq(theirs)]
 
@@ -281,7 +318,7 @@
         group += [xor_dp(toks, step) for step in range(3, dps)]
 
     block_kv = call(functools.partial(kv_kernel, heads), halves, keys, values)
-    prefix = carried(block_kv, False)
+    prefix = carried("kv", block_kv, False)
 
     if split:
         d = lax.axis_index("dp")
@@ -316,41 +353,62 @@
         ).astype(BF16)
         pair = (query_rows[:, : width // 2], query_rows[:, width // 2 :])
 
-    grad_parts = call(
-        functools.partial(query_grad_kernel, factor, heads, states),
-        [out((rows, width // dps), BF16)] * dps,
-        keys,
-        values,
-        grads,
-        *prefix,
-        scratch=scratch,
-    )
-    grad_group = [grad_parts[0]] + [xor_dp(grad_parts[step], step) for step in range(1, dps)]
+    parts = 2 if split else 1
+    grad_groups = []
+    for part in range(parts):
+        sent = call(
+            functools.partial(query_grad_kernel, factor, heads, states, part, parts),
+            [out((rows, width // dps // parts), BF16)] * dps,
+            keys,
+            values,
+            grads,
+            *prefix,
+            scratch=scratch,
+        )
+        grad_groups.append([sent[0]] + [xor_dp(sent[step], step) for step in range(1, dps)])
 
     if split:
-        block = (model // seqs, width // dps)
-        weights = (*group, *grad_group)
-
-        def formed(other, steps, dtype):
+        block, half = model // seqs, width // dps // 2
+        thin, wide = (block, half), (block, 2 * half)
+
+        def formed(other, steps, dtype, *which):
             kernel = functools.partial(weight_kernel, seqs, dps, other, steps)
-            return dict(zip(steps, call(kernel, [out(block, dtype)] * len(steps), *weights)))
-
-        def added(dtype, *terms):
-            return call(sum_kernel, [out(block, dtype)], *terms)[0]
-
-        order = (3, 2, 1, 0)
-        sends = {**formed(1, order[:1], BF16), **formed(1, order[1:], BF16)}
-        got = {step: flip_seq(sends[step]) for step in order}
-        keep = formed(0, order, F32)
-        near = flip_seq(added(BF16, keep[3], got[3]), 2)
-        cross = flip_seq(added(BF16, keep[2], got[2], near), 4)
-        near = flip_seq(added(BF16, keep[1], got[1]), 2)
-        share = added(BF16, keep[0], got[0], near, cross)
+            shape = (len(steps) * block, len(which) * half)
+            terms = sum((grad_groups[part] for part in which), [])
+            return call(kernel, [out(shape, dtype)], *group, *terms)[0]
+
+        def added(shape, starts, *terms):
+            return call(functools.partial(sum_kernel, starts), [out(shape, BF16)], *terms)[0]
+
+        got = {
+            (step, part): flip_seq(formed(1, (step,), BF16, part))
+            for part in (0, 1)
+            for step in (3, 2)
+        }
+        rest = flip_seq(formed(1, (1, 0), BF16, 0, 1))
+        keep = formed(0, (3, 2, 1, 0), F32, 0, 1)
+        zero, crosses = (0, 0), []
+        for part in (0, 1):
+            near = added(thin, ((0, part * half), zero), keep, got[3, part])
+            near = flip_seq(near, 2)
+            starts = ((block, part * half), zero, zero)
+            far = added(thin, starts, keep, got[2, part], near)
+            crosses.append(flip_seq(far, 4))
+        near = added(wide, ((2 * block, 0), zero), keep, rest)
+        near = flip_seq(near, 2)
+        share = call(
+            functools.partial(share_kernel, 3 * block),
+            [out(wide, BF16)],
+            keep,
+            rest,
+            near,
+            *crosses,
+        )[0]
     else:
         share = lax.psum_scatter(
             lax.dot_general(
                 jnp.concatenate(group),
-                jnp.concatenate(grad_group),
+                jnp.concatenate(grad_groups[0]),
                 (((0,), (0,)), ((), ())),
                 preferred_element_type=F32,
             ),
@@ -372,7 +430,7 @@
         grads,
         scratch=[out((heads * DH, DH), F32)] if split else [],
     )
-    suffix = carried(block_qg, True)
+    suffix = carried("qg", block_qg, True)
     attended = call(
         functools.partial(attended_kernel, factor, heads, states, seqs, split, len(pair)),
         [out((rows, width), BF16)],

time: 165 us -> 170 us (1.030)
  waiting for transfers between devices: 85.3 us -> 90.1 us
    ppermute x20 -> x24, waiting for transfers between devices: 59.1 us -> 68.1 us  [flip_seq(): return lax.ppermute(value, 'seq', [(i, i ^ bits) for i in range(seqs)])]
    ppermute x13 -> x16, waiting for transfers between devices: 19.3 us -> 15.6 us  [xor_dp(): return lax.ppermute(value, 'dp', [(i, i ^ step) for i in range(dps)])]
    ppermute x13 -> x16, starting transfers between devices: 7.31 us -> 8.29 us  [xor_dp(): return lax.ppermute(value, 'dp', [(i, i ^ step) for i in range(dps)])]
    ppermute x20 -> x24, starting transfers between devices: 39 us -> 38.4 us  [flip_seq(): return lax.ppermute(value, 'seq', [(i, i ^ bits) for i in range(seqs)])]
    pallas_call x22 -> x28, Pallas kernels: 21.7 us -> 21.2 us  [call(): pl.pallas_call(kernel, out_shape=tuple(outs), in_specs=[pl.BlockSpec(memo...]
  transfers between devices with their start and end apart: 35 -> 42, of which waited for: 17 -> 17; matrix products, arithmetic and copies ran while one was open for 0% -> 0% of each run, Pallas kernels for 12% -> 12%
where the time goes in v5:
time: 170 us
  waiting for transfers between devices  90.1 us (53%)
  starting transfers between devices  53.7 us (32%)
  Pallas kernels  21.2 us (12%)
  local copies, waits for them, and re-layouts  3.45 us (2%)
    ppermute x24, waiting for transfers between devices, flip_seq(): return lax.ppermute(value, 'seq', [(i, i ^ bits) for i in range(seqs)])  68.1 us
    ppermute x24, starting transfers between devices, flip_seq(): return lax.ppermute(value, 'seq', [(i, i ^ bits) for i in range(seqs)])  38.4 us
    pallas_call x28, Pallas kernels, call(): pl.pallas_call(kernel, out_shape=tuple(outs), in_specs=[pl.BlockSpec(memo...  21.2 us
    ppermute x16, waiting for transfers between devices, xor_dp(): return lax.ppermute(value, 'dp', [(i, i ^ step) for i in range(dps)])  15.6 us
    ppermute x16, starting transfers between devices, xor_dp(): return lax.ppermute(value, 'dp', [(i, i ^ step) for i in range(dps)])  8.29 us
    ppermute x2, starting transfers between devices, carried(): lax.ppermute(quad, 'seq', list(zip(high, low) if backward else zip(low, h...  6.99 us
    ppermute x2, waiting for transfers between devices, carried(): lax.ppermute(quad, 'seq', list(zip(high, low) if backward else zip(low, h...  6.48 us
  transfers between devices with their start and end apart: 42, of which 17 were waited for; matrix products, arithmetic and copies ran while one was open for 0% of the time, Pallas kernels for 12%

profile of v5, /device:TPU:0, one launch (start us, length us, event | category | flops | bytes accessed | tf_op | source)
XLA Modules:
  0.0 169.8 jit_solution(10791801287671195231)
XLA Ops:
  1.6 4.1 %collective-permute-start.5 = (bf16[1024,128]{1,0:T(8,128)(2,1)S(1)}, bf16[1024,128]{1,0:T(8,128)(2,1)S(1)}, u32[]{:S(2)}, u32[]{:S(2)}) collective-permute-start(bf16[1024,128]{1,0:T(8,128)(2,1)S(1)} %dynamic_slice.3), channel_id=1, source_target_pairs={{0,16},{4,20},{8,24},{12,28},{16,0},{20,4},{24,8},{28,12},{1,17},{... | collective-permute-start | bytes 786440 | tf_op jit(solution)/shard_map/ppermute | solution.py:282
  5.8 1.6 collective-permute-start.2
  8.9 8.9 %collective-permute-done.5 = bf16[1024,128]{1,0:T(8,128)(2,1)S(1)} collective-permute-done((bf16[1024,128]{1,0:T(8,128)(2,1)S(1)}, bf16[1024,128]{1,0:T(8,128)(2,1)S(1)}, u32[]{:S(2)}, u32[]{:S(2)}) %collective-permute-start.5) | collective-permute-done | bytes 262176 | tf_op jit(solution)/shard_map/ppermute | solution.py:282
  18.4 1.5 collective-permute-start.3
  25.4 1.6 collective-permute-start.6
  28.1 11.5 %collective-permute-done.6 = bf16[1024,128]{1,0:T(8,128)(2,1)S(1)} collective-permute-done((bf16[1024,128]{1,0:T(8,128)(2,1)S(1)}, bf16[1024,128]{1,0:T(8,128)(2,1)S(1)}, u32[]{:S(2)}, u32[]{:S(2)}) %collective-permute-start.6) | collective-permute-done | bytes 262176 | tf_op jit(solution)/shard_map/ppermute | solution.py:282
  39.6 5.1 %collective-permute-done.8 = bf16[1024,128]{1,0:T(8,128)(2,1)S(1)} collective-permute-done((bf16[1024,128]{1,0:T(8,128)(2,1)S(1)}, bf16[1024,128]{1,0:T(8,128)(2,1)S(1)}, u32[]{:S(2)}, u32[]{:S(2)}) %collective-permute-start.8) | collective-permute-done | bytes 262176 | tf_op jit(solution)/shard_map/ppermute | solution.py:282
  46.8 7.0 %collective-permute-done.13.pair_ref = bf16[1024,128]{1,0:T(8,128)(2,1)S(1)} collective-permute-done((bf16[1024,128]{1,0:T(8,128)(2,1)S(1)}, bf16[1024,128]{1,0:T(8,128)(2,1)S(1)}, u32[]{:S(2)}, u32[]{:S(2)}) %collective-permute-start.13) | collective-permute-done | bytes 262176 | tf_op jit(solution)/shard_map/ppermute | solution.py:282
  53.9 5.5 %collective-permute-start.14 = (bf16[1024,128]{1,0:T(8,128)(2,1)S(1)}, bf16[1024,128]{1,0:T(8,128)(2,1)S(1)}, u32[]{:S(2)}, u32[]{:S(2)}) collective-permute-start(bf16[1024,128]{1,0:T(8,128)(2,1)S(1)} %shard_map.88), channel_id=1, source_target_pairs={{0,16},{4,20},{8,24},{12,28},{1,17},{5,21},{9,25},{13,29},{2,18},{... | collective-permute-start | bytes 786440 | tf_op jit(solution)/shard_map/ppermute | solution.py:300
  59.4 5.2 %collective-permute-done.14.refs_0_ = bf16[1024,128]{1,0:T(8,128)(2,1)S(1)} collective-permute-done((bf16[1024,128]{1,0:T(8,128)(2,1)S(1)}, bf16[1024,128]{1,0:T(8,128)(2,1)S(1)}, u32[]{:S(2)}, u32[]{:S(2)}) %collective-permute-start.14) | collective-permute-done | bytes 262176 | tf_op jit(solution)/shard_map/ppermute | solution.py:300
  65.4 6.5 %collective-permute-done.15.refs_7_.refs_1_ = bf16[1024,128]{1,0:T(8,128)(2,1)S(1)} collective-permute-done((bf16[1024,128]{1,0:T(8,128)(2,1)S(1)}, bf16[1024,128]{1,0:T(8,128)(2,1)S(1)}, u32[]{:S(2)}, u32[]{:S(2)}) %collective-permute-start.15) | collective-permute-done | bytes 262176 | tf_op jit(solution)/shard_map/ppermute | solution.py:282
  76.1 3.4 %collective-permute-done.27.refs_10_.refs_6_ = bf16[256,256]{1,0:T(8,128)(2,1)S(1)} collective-permute-done((bf16[256,256]{1,0:T(8,128)(2,1)S(1)}, bf16[256,256]{1,0:T(8,128)(2,1)S(1)}, u32[]{:S(2)}, u32[]{:S(2)}) %collective-permute-start.27) | collective-permute-done | bytes 131104 | tf_op jit(solution)/shard_map/ppermute | solution.py:279
  79.7 1.7 %collective-permute-start.25 = (bf16[256,256]{1,0:T(8,128)(2,1)S(1)}, bf16[256,256]{1,0:T(8,128)(2,1)S(1)}, u32[]{:S(2)}, u32[]{:S(2)}) collective-permute-start(bf16[256,256]{1,0:T(8,128)(2,1)S(1)} %get-tuple-element.39), channel_id=1, source_target_pairs={{0,3},{1,2},{2,1},{3,0},{4,7},{5,6},{6,5},{7,4},{8,11},{9,10},{10,... | collective-permute-start | bytes 393224 | tf_op jit(solution)/shard_map/ppermute | solution.py:279
  84.3 1.7 collective-permute-start.11
  86.0 1.8 %collective-permute-done.25.refs_7_ = bf16[256,256]{1,0:T(8,128)(2,1)S(1)} collective-permute-done((bf16[256,256]{1,0:T(8,128)(2,1)S(1)}, bf16[256,256]{1,0:T(8,128)(2,1)S(1)}, u32[]{:S(2)}, u32[]{:S(2)}) %collective-permute-start.25) | collective-permute-done | bytes 131104 | tf_op jit(solution)/shard_map/ppermute | solution.py:279
  89.2 5.2 %collective-permute-done.10.refs_2_ = bf16[256,512]{1,0:T(8,128)(2,1)S(1)} collective-permute-done((bf16[256,512]{1,0:T(8,128)(2,1)S(1)}, bf16[256,512]{1,0:T(8,128)(2,1)S(1)}, u32[]{:S(2)}, u32[]{:S(2)}) %collective-permute-start.10) | collective-permute-done | bytes 262176 | tf_op jit(solution)/shard_map/ppermute | solution.py:279
  94.3 5.2 %collective-permute-done.11.refs_3_ = bf16[256,512]{1,0:T(8,128)(2,1)S(1)} collective-permute-done((bf16[256,512]{1,0:T(8,128)(2,1)S(1)}, bf16[256,512]{1,0:T(8,128)(2,1)S(1)}, u32[]{:S(2)}, u32[]{:S(2)}) %collective-permute-start.11) | collective-permute-done | bytes 262176 | tf_op jit(solution)/shard_map/ppermute | solution.py:279
  101.0 1.6 collective-permute-start.36
  103.9 1.6 collective-permute-start.35
  107.3 4.9 %collective-permute-done.36.refs_1_ = bf16[256,256]{1,0:T(8,128)(2,1)S(1)} collective-permute-done((bf16[256,256]{1,0:T(8,128)(2,1)S(1)}, bf16[256,256]{1,0:T(8,128)(2,1)S(1)}, u32[]{:S(2)}, u32[]{:S(2)}) %collective-permute-start.36) | collective-permute-done | bytes 131104 | tf_op jit(solution)/shard_map/ppermute | solution.py:282
  112.2 6.5 %collective-permute-start.37 = (bf16[256,256]{1,0:T(8,128)(2,1)S(1)}, bf16[256,256]{1,0:T(8,128)(2,1)S(1)}, u32[]{:S(2)}, u32[]{:S(2)}) collective-permute-start(bf16[256,256]{1,0:T(8,128)(2,1)S(1)} %shard_map.108), channel_id=1, source_target_pairs={{0,8},{4,12},{8,0},{12,4},{16,24},{20,28},{24,16},{28,20},{1,9},{5... | collective-permute-start | bytes 393224 | tf_op jit(solution)/shard_map/ppermute | solution.py:282
  119.4 2.6 %collective-permute-start.33 = (bf16[256,256]{1,0:T(8,128)(2,1)S(1)}, bf16[256,256]{1,0:T(8,128)(2,1)S(1)}, u32[]{:S(2)}, u32[]{:S(2)}) collective-permute-start(bf16[256,256]{1,0:T(8,128)(2,1)S(1)} %shard_map.104), channel_id=1, source_target_pairs={{0,8},{4,12},{8,0},{12,4},{16,24},{20,28},{24,16},{28,20},{1,9},{5... | collective-permute-start | bytes 393224 | tf_op jit(solution)/shard_map/ppermute | solution.py:282
  122.0 2.1 %collective-permute-start.30 = (bf16[256,512]{1,0:T(8,128)(2,1)S(1)}, bf16[256,512]{1,0:T(8,128)(2,1)S(1)}, u32[]{:S(2)}, u32[]{:S(2)}) collective-permute-start(bf16[256,512]{1,0:T(8,128)(2,1)S(1)} %shard_map.101), channel_id=1, source_target_pairs={{0,8},{4,12},{8,0},{12,4},{16,24},{20,28},{24,16},{28,20},{1,9},{5... | collective-permute-start | bytes 786440 | tf_op jit(solution)/shard_map/ppermute | solution.py:282
  124.2 3.4 %collective-permute-start.38 = (bf16[256,256]{1,0:T(8,128)(2,1)S(1)}, bf16[256,256]{1,0:T(8,128)(2,1)S(1)}, u32[]{:S(2)}, u32[]{:S(2)}) collective-permute-start(bf16[256,256]{1,0:T(8,128)(2,1)S(1)} %shard_map.109), channel_id=1, source_target_pairs={{0,16},{4,20},{8,24},{12,28},{16,0},{20,4},{24,8},{28,12},{1,17},{... | collective-permute-start | bytes 393224 | tf_op jit(solution)/shard_map/ppermute | solution.py:282
  127.7 6.5 %collective-permute-done.33.refs_2_ = bf16[256,256]{1,0:T(8,128)(2,1)S(1)} collective-permute-done((bf16[256,256]{1,0:T(8,128)(2,1)S(1)}, bf16[256,256]{1,0:T(8,128)(2,1)S(1)}, u32[]{:S(2)}, u32[]{:S(2)}) %collective-permute-start.33) | collective-permute-done | bytes 131104 | tf_op jit(solution)/shard_map/ppermute | solution.py:282
  134.2 3.1 %collective-permute-start.34 = (bf16[256,256]{1,0:T(8,128)(2,1)S(1)}, bf16[256,256]{1,0:T(8,128)(2,1)S(1)}, u32[]{:S(2)}, u32[]{:S(2)}) collective-permute-start(bf16[256,256]{1,0:T(8,128)(2,1)S(1)} %shard_map.105), channel_id=1, source_target_pairs={{0,16},{4,20},{8,24},{12,28},{16,0},{20,4},{24,8},{28,12},{1,17},{... | collective-permute-start | bytes 393224 | tf_op jit(solution)/shard_map/ppermute | solution.py:282
  139.1 10.1 %collective-permute-done.34.refs_0_ = bf16[256,256]{1,0:T(8,128)(2,1)S(1)} collective-permute-done((bf16[256,256]{1,0:T(8,128)(2,1)S(1)}, bf16[256,256]{1,0:T(8,128)(2,1)S(1)}, u32[]{:S(2)}, u32[]{:S(2)}) %collective-permute-start.34) | collective-permute-done | bytes 131104 | tf_op jit(solution)/shard_map/ppermute | solution.py:282
  150.6 5.0 %collective-permute-done.19.refs_1_ = bf16[512,128]{1,0:T(8,128)(2,1)S(1)} collective-permute-done((bf16[512,128]{1,0:T(8,128)(2,1)S(1)}, bf16[512,128]{1,0:T(8,128)(2,1)S(1)}, u32[]{:S(2)}, u32[]{:S(2)}) %collective-permute-start.19) | collective-permute-done | bytes 131104 | tf_op jit(solution)/shard_map/ppermute | solution.py:282
  156.8 3.0 %shard_map.90 = bf16[256,2048]{1,0:T(8,128)(2,1)} custom-call(bf16[256,512]{1,0:T(8,128)(2,1)S(1)} %get-tuple-element.24.refs_0_, bf16[256,512]{1,0:T(8,128)(2,1)S(1)} %get-tuple-element.25.refs_1_, bf16[256,512]{1,0:T(8,128)(2,1)S(1)} %collective-permute-done.10.refs_2_, bf16[256,512]{1,0:T(8,128)(2,1)S(1)} %collective-permute-done.11.refs_3_, ...), custom_call_target="tpu_custom_call" | custom-call | bytes 4718592 | tf_op jit(solution)/shard_map/pallas_call | solution.py:28
  159.8 2.4 %collective-permute-done.20.refs_7_ = bf16[1024,128]{1,0:T(8,128)(2,1)S(1)} collective-permute-done((bf16[1024,128]{1,0:T(8,128)(2,1)S(1)}, bf16[1024,128]{1,0:T(8,128)(2,1)S(1)}, u32[]{:S(2)}, u32[]{:S(2)}) %collective-permute-start.20) | collective-permute-done | bytes 262176 | tf_op jit(solution)/shard_map/ppermute | solution.py:282
  162.2 3.0 %shard_map.96 = bf16[256,2048]{1,0:T(8,128)(2,1)} custom-call(bf16[256,512]{1,0:T(8,128)(2,1)S(1)} %get-tuple-element.24.refs_0_, bf16[256,512]{1,0:T(8,128)(2,1)S(1)} %get-tuple-element.25.refs_1_, bf16[256,512]{1,0:T(8,128)(2,1)S(1)} %collective-permute-done.10.refs_2_, bf16[256,512]{1,0:T(8,128)(2,1)S(1)} %collective-permute-done.11.refs_3_, ...), custom_call_target="tpu_custom_call" | custom-call | bytes 4718592 | tf_op jit(solution)/shard_map/pallas_call | solution.py:28
  165.2 3.1 %shard_map.95 = bf16[256,2048]{1,0:T(8,128)(2,1)} custom-call(bf16[256,512]{1,0:T(8,128)(2,1)S(1)} %get-tuple-element.24.refs_0_, bf16[256,512]{1,0:T(8,128)(2,1)S(1)} %get-tuple-element.25.refs_1_, bf16[256,512]{1,0:T(8,128)(2,1)S(1)} %collective-permute-done.10.refs_2_, bf16[256,512]{1,0:T(8,128)(2,1)S(1)} %collective-permute-done.11.refs_3_, ...), custom_call_target="tpu_custom_call" | custom-call | bytes 4718592 | tf_op jit(solution)/shard_map/pallas_call | solution.py:28
  (99 shorter events, 32.6 us)
Async XLA Ops:
  1.6 16.2 %collective-permute-start.5 = (bf16[1024,128]{1,0:T(8,128)(2,1)S(1)}, bf16[1024,128]{1,0:T(8,128)(2,1)S(1)}, u32[]{:S(2)}, u32[]{:S(2)}) collective-permute-start(bf16[1024,128]{1,0:T(8,128)(2,1)S(1)} %dynamic_slice.3), channel_id=1, source_target_pairs={{0,16},{4,20},{8,24},{12,28},{16,0},{20,4},{24,8},{28,12},{1,17},{... | collective-permute-start | bytes 786440 | tf_op jit(solution)/shard_map/ppermute | solution.py:282
  5.8 12.6 %collective-permute-start.2 = (bf16[1024,128]{1,0:T(8,128)(2,1)S(1)}, bf16[1024,128]{1,0:T(8,128)(2,1)S(1)}, u32[]{:S(2)}, u32[]{:S(2)}) collective-permute-start(bf16[1024,128]{1,0:T(8,128)(2,1)S(1)} %dynamic_slice.3), channel_id=1, source_target_pairs={{0,8},{4,12},{8,0},{12,4},{16,24},{20,28},{24,16},{28,20},{1,9},{5... | collective-permute-start | bytes 786440 | tf_op jit(solution)/shard_map/ppermute | solution.py:282
  7.3 17.4 %collective-permute-start.1 = (bf16[1024,128]{1,0:T(8,128)(2,1)S(1)}, bf16[1024,128]{1,0:T(8,128)(2,1)S(1)}, u32[]{:S(2)}, u32[]{:S(2)}) collective-permute-start(bf16[1024,128]{1,0:T(8,128)(2,1)S(1)} %dynamic_slice.3), channel_id=1, source_target_pairs={{0,4},{4,0},{8,12},{12,8},{16,20},{20,16},{24,28},{28,24},{1,5},{5... | collective-permute-start | bytes 786440 | tf_op jit(solution)/shard_map/ppermute | solution.py:282
  18.4 8.5 %collective-permute-start.3 = (bf16[1024,128]{1,0:T(8,128)(2,1)S(1)}, bf16[1024,128]{1,0:T(8,128)(2,1)S(1)}, u32[]{:S(2)}, u32[]{:S(2)}) collective-permute-start(bf16[1024,128]{1,0:T(8,128)(2,1)S(1)} %collective-permute-done.2), channel_id=1, source_target_pairs={{0,4},{4,0},{8,12},{12,8},{16,20},{20,16},{24,28},{28,24},{1,5},{5... | collective-permute-start | bytes 786440 | tf_op jit(solution)/shard_map/ppermute | solution.py:282
  19.9 26.7 %collective-permute-start = (bf16[256,2048]{1,0:T(8,128)(2,1)}, bf16[256,2048]{1,0:T(8,128)(2,1)S(1)}, u32[]{:S(2)}, u32[]{:S(2)}) collective-permute-start(bf16[256,2048]{1,0:T(8,128)(2,1)} %bitcast.15), channel_id=1, source_target_pairs={{0,2},{1,3},{2,0},{3,1},{4,6},{5,7},{6,4},{7,5},{8,10},{9,11},{10,... | collective-permute-start | bytes 3145736 | tf_op jit(solution)/shard_map/ppermute | solution.py:279
  21.4 51.7 %collective-permute-start.21 = (bf16[256,2048]{1,0:T(8,128)(2,1)}, bf16[256,2048]{1,0:T(8,128)(2,1)S(1)}, u32[]{:S(2)}, u32[]{:S(2)}) collective-permute-start(bf16[256,2048]{1,0:T(8,128)(2,1)} %bitcast.16), channel_id=1, source_target_pairs={{0,1},{1,0},{2,3},{3,2},{4,5},{5,4},{6,7},{7,6},{8,9},{9,8},{10,11... | collective-permute-start | bytes 3145736 | tf_op jit(solution)/shard_map/ppermute | solution.py:279
  24.7 20.3 %collective-permute-start.12 = (bf16[1024,128]{1,0:T(8,128)(2,1)S(1)}, bf16[1024,128]{1,0:T(8,128)(2,1)S(1)}, u32[]{:S(2)}, u32[]{:S(2)}) collective-permute-start(bf16[1024,128]{1,0:T(8,128)(2,1)S(1)} %get-tuple-element.29), channel_id=1, source_target_pairs={{0,4},{4,0},{8,12},{12,8},{16,20},{20,16},{24,28},{28,24},{1,5},{5... | collective-permute-start | bytes 786440 | tf_op jit(solution)/shard_map/ppermute | solution.py:282
  25.4 14.2 %collective-permute-start.6 = (bf16[1024,128]{1,0:T(8,128)(2,1)S(1)}, bf16[1024,128]{1,0:T(8,128)(2,1)S(1)}, u32[]{:S(2)}, u32[]{:S(2)}) collective-permute-start(bf16[1024,128]{1,0:T(8,128)(2,1)S(1)} %collective-permute-done.5), channel_id=1, source_target_pairs={{0,4},{4,0},{8,12},{12,8},{16,20},{20,16},{24,28},{28,24},{1,5},{5... | collective-permute-start | bytes 786440 | tf_op jit(solution)/shard_map/ppermute | solution.py:282
  26.9 17.8 %collective-permute-start.8 = (bf16[1024,128]{1,0:T(8,128)(2,1)S(1)}, bf16[1024,128]{1,0:T(8,128)(2,1)S(1)}, u32[]{:S(2)}, u32[]{:S(2)}) collective-permute-start(bf16[1024,128]{1,0:T(8,128)(2,1)S(1)} %collective-permute-done.7), channel_id=1, source_target_pairs={{0,4},{4,0},{8,12},{12,8},{16,20},{20,16},{24,28},{28,24},{1,5},{5... | collective-permute-start | bytes 786440 | tf_op jit(solution)/shard_map/ppermute | solution.py:282
  39.6 40.0 %collective-permute-start.4 = (bf16[2,1024,256]{2,1,0:T(8,128)(2,1)S(1)}, bf16[2,1024,256]{2,1,0:T(8,128)(2,1)S(1)}, u32[]{:S(2)}, u32[]{:S(2)}) collective-permute-start(bf16[2,1024,256]{2,1,0:T(8,128)(2,1)S(1)} %pad_maximum_fusion.near_ref), channel_id=1, source_target_pairs={{0,1},{1,0},{2,3},{3,2},{4,5},{5,4},{6,7},{7,6},{8,9},{9,8},{10,11... | collective-permute-start | bytes 3145736 | tf_op jit(solution)/shard_map/ppermute | solution.py:279
  44.9 34.8 %collective-permute-start.9 = (bf16[2,1024,256]{2,1,0:T(8,128)(2,1)S(1)}, bf16[2,1024,256]{2,1,0:T(8,128)(2,1)S(1)}, u32[]{:S(2)}, u32[]{:S(2)}) collective-permute-start(bf16[2,1024,256]{2,1,0:T(8,128)(2,1)S(1)} %pad_maximum_fusion.1.near_ref), channel_id=1, source_target_pairs={{0,1},{1,0},{2,3},{3,2},{4,5},{5,4},{6,7},{7,6},{8,9},{9,8},{10,11... | collective-permute-start | bytes 3145736 | tf_op jit(solution)/shard_map/ppermute | solution.py:279
  45.1 8.8 %collective-permute-start.13 = (bf16[1024,128]{1,0:T(8,128)(2,1)S(1)}, bf16[1024,128]{1,0:T(8,128)(2,1)S(1)}, u32[]{:S(2)}, u32[]{:S(2)}) collective-permute-start(bf16[1024,128]{1,0:T(8,128)(2,1)S(1)} %shard_map.87), channel_id=1, source_target_pairs={{0,8},{4,12},{8,0},{12,4},{16,24},{20,28},{24,16},{28,20},{1,9},{5... | collective-permute-start | bytes 786440 | tf_op jit(solution)/shard_map/ppermute | solution.py:282
  46.6 41.2 %collective-permute-start.22 = (bf16[256,2048]{1,0:T(8,128)(2,1)S(1)}, bf16[256,2048]{1,0:T(8,128)(2,1)S(1)}, u32[]{:S(2)}, u32[]{:S(2)}) collective-permute-start(bf16[256,2048]{1,0:T(8,128)(2,1)S(1)} %collective-permute-done.theirs_ref.refs_2_), channel_id=1, source_target_pairs={{0,1},{1,0},{2,3},{3,2},{4,5},{5,4},{6,7},{7,6},{8,9},{9,8},{10,11... | collective-permute-start | bytes 3145736 | tf_op jit(solution)/shard_map/ppermute | solution.py:279
  53.9 10.7 %collective-permute-start.14 = (bf16[1024,128]{1,0:T(8,128)(2,1)S(1)}, bf16[1024,128]{1,0:T(8,128)(2,1)S(1)}, u32[]{:S(2)}, u32[]{:S(2)}) collective-permute-start(bf16[1024,128]{1,0:T(8,128)(2,1)S(1)} %shard_map.88), channel_id=1, source_target_pairs={{0,16},{4,20},{8,24},{12,28},{1,17},{5,21},{9,25},{13,29},{2,18},{... | collective-permute-start | bytes 786440 | tf_op jit(solution)/shard_map/ppermute | solution.py:300
  74.8 9.1 %collective-permute-start.28 = (bf16[256,256]{1,0:T(8,128)(2,1)S(1)}, bf16[256,256]{1,0:T(8,128)(2,1)S(1)}, u32[]{:S(2)}, u32[]{:S(2)}) collective-permute-start(bf16[256,256]{1,0:T(8,128)(2,1)S(1)} %get-tuple-element.43), channel_id=1, source_target_pairs={{0,3},{1,2},{2,1},{3,0},{4,7},{5,6},{6,5},{7,4},{8,11},{9,10},{10,... | collective-permute-start | bytes 393224 | tf_op jit(solution)/shard_map/ppermute | solution.py:279
  83.9 10.4 %collective-permute-start.10 = (bf16[256,512]{1,0:T(8,128)(2,1)S(1)}, bf16[256,512]{1,0:T(8,128)(2,1)S(1)}, u32[]{:S(2)}, u32[]{:S(2)}) collective-permute-start(bf16[256,512]{1,0:T(8,128)(2,1)S(1)} %get-tuple-element.26), channel_id=1, source_target_pairs={{0,2},{1,3},{2,0},{3,1},{4,6},{5,7},{6,4},{7,5},{8,10},{9,11},{10,... | collective-permute-start | bytes 786440 | tf_op jit(solution)/shard_map/ppermute | solution.py:279
  84.3 15.2 %collective-permute-start.11 = (bf16[256,512]{1,0:T(8,128)(2,1)S(1)}, bf16[256,512]{1,0:T(8,128)(2,1)S(1)}, u32[]{:S(2)}, u32[]{:S(2)}) collective-permute-start(bf16[256,512]{1,0:T(8,128)(2,1)S(1)} %get-tuple-element.27), channel_id=1, source_target_pairs={{0,2},{1,3},{2,0},{3,1},{4,6},{5,7},{6,4},{7,5},{8,10},{9,11},{10,... | collective-permute-start | bytes 786440 | tf_op jit(solution)/shard_map/ppermute | solution.py:279
  88.6 30.8 %collective-permute-start.29 = (bf16[512,512]{1,0:T(8,128)(2,1)S(1)}, bf16[512,512]{1,0:T(8,128)(2,1)S(1)}, u32[]{:S(2)}, u32[]{:S(2)}) collective-permute-start(bf16[512,512]{1,0:T(8,128)(2,1)S(1)} %shard_map.100), channel_id=1, source_target_pairs={{0,4},{4,0},{8,12},{12,8},{16,20},{20,16},{24,28},{28,24},{1,5},{5... | collective-permute-start | bytes 1572872 | tf_op jit(solution)/shard_map/ppermute | solution.py:282
  100.1 18.6 %collective-permute-start.16 = (bf16[1024,128]{1,0:T(8,128)(2,1)S(1)}, bf16[1024,128]{1,0:T(8,128)(2,1)S(1)}, u32[]{:S(2)}, u32[]{:S(2)}) collective-permute-start(bf16[1024,128]{1,0:T(8,128)(2,1)S(1)} %get-tuple-element.33), channel_id=1, source_target_pairs={{0,4},{4,0},{8,12},{12,8},{16,20},{20,16},{24,28},{28,24},{1,5},{5... | collective-permute-start | bytes 786440 | tf_op jit(solution)/shard_map/ppermute | solution.py:282
  101.0 11.1 %collective-permute-start.36 = (bf16[256,256]{1,0:T(8,128)(2,1)S(1)}, bf16[256,256]{1,0:T(8,128)(2,1)S(1)}, u32[]{:S(2)}, u32[]{:S(2)}) collective-permute-start(bf16[256,256]{1,0:T(8,128)(2,1)S(1)} %shard_map.107), channel_id=1, source_target_pairs={{0,4},{4,0},{8,12},{12,8},{16,20},{20,16},{24,28},{28,24},{1,5},{5... | collective-permute-start | bytes 393224 | tf_op jit(solution)/shard_map/ppermute | solution.py:282
  103.0 15.8 %collective-permute-start.32 = (bf16[256,256]{1,0:T(8,128)(2,1)S(1)}, bf16[256,256]{1,0:T(8,128)(2,1)S(1)}, u32[]{:S(2)}, u32[]{:S(2)}) collective-permute-start(bf16[256,256]{1,0:T(8,128)(2,1)S(1)} %shard_map.103), channel_id=1, source_target_pairs={{0,4},{4,0},{8,12},{12,8},{16,20},{20,16},{24,28},{28,24},{1,5},{5... | collective-permute-start | bytes 393224 | tf_op jit(solution)/shard_map/ppermute | solution.py:282
  103.9 18.1 %collective-permute-start.35 = (bf16[256,256]{1,0:T(8,128)(2,1)S(1)}, bf16[256,256]{1,0:T(8,128)(2,1)S(1)}, u32[]{:S(2)}, u32[]{:S(2)}) collective-permute-start(bf16[256,256]{1,0:T(8,128)(2,1)S(1)} %shard_map.106), channel_id=1, source_target_pairs={{0,4},{4,0},{8,12},{12,8},{16,20},{20,16},{24,28},{28,24},{1,5},{5... | collective-permute-start | bytes 393224 | tf_op jit(solution)/shard_map/ppermute | solution.py:282
  112.2 12.0 %collective-permute-start.37 = (bf16[256,256]{1,0:T(8,128)(2,1)S(1)}, bf16[256,256]{1,0:T(8,128)(2,1)S(1)}, u32[]{:S(2)}, u32[]{:S(2)}) collective-permute-start(bf16[256,256]{1,0:T(8,128)(2,1)S(1)} %shard_map.108), channel_id=1, source_target_pairs={{0,8},{4,12},{8,0},{12,4},{16,24},{20,28},{24,16},{28,20},{1,9},{5... | collective-permute-start | bytes 393224 | tf_op jit(solution)/shard_map/ppermute | solution.py:282
  118.7 18.6 %collective-permute-start.17 = (bf16[1024,128]{1,0:T(8,128)(2,1)S(1)}, bf16[1024,128]{1,0:T(8,128)(2,1)S(1)}, u32[]{:S(2)}, u32[]{:S(2)}) collective-permute-start(bf16[1024,128]{1,0:T(8,128)(2,1)S(1)} %shard_map.92), channel_id=1, source_target_pairs={{0,8},{4,12},{8,0},{12,4},{16,24},{20,28},{24,16},{28,20},{1,9},{5... | collective-permute-start | bytes 786440 | tf_op jit(solution)/shard_map/ppermute | solution.py:282
  118.8 8.9 %collective-permute-start.31 = (bf16[256,256]{1,0:T(8,128)(2,1)S(1)}, bf16[256,256]{1,0:T(8,128)(2,1)S(1)}, u32[]{:S(2)}, u32[]{:S(2)}) collective-permute-start(bf16[256,256]{1,0:T(8,128)(2,1)S(1)} %shard_map.102), channel_id=1, source_target_pairs={{0,4},{4,0},{8,12},{12,8},{16,20},{20,16},{24,28},{28,24},{1,5},{5... | collective-permute-start | bytes 393224 | tf_op jit(solution)/shard_map/ppermute | solution.py:282
  119.4 14.8 %collective-permute-start.33 = (bf16[256,256]{1,0:T(8,128)(2,1)S(1)}, bf16[256,256]{1,0:T(8,128)(2,1)S(1)}, u32[]{:S(2)}, u32[]{:S(2)}) collective-permute-start(bf16[256,256]{1,0:T(8,128)(2,1)S(1)} %shard_map.104), channel_id=1, source_target_pairs={{0,8},{4,12},{8,0},{12,4},{16,24},{20,28},{24,16},{28,20},{1,9},{5... | collective-permute-start | bytes 393224 | tf_op jit(solution)/shard_map/ppermute | solution.py:282
  122.0 27.1 %collective-permute-start.30 = (bf16[256,512]{1,0:T(8,128)(2,1)S(1)}, bf16[256,512]{1,0:T(8,128)(2,1)S(1)}, u32[]{:S(2)}, u32[]{:S(2)}) collective-permute-start(bf16[256,512]{1,0:T(8,128)(2,1)S(1)} %shard_map.101), channel_id=1, source_target_pairs={{0,8},{4,12},{8,0},{12,4},{16,24},{20,28},{24,16},{28,20},{1,9},{5... | collective-permute-start | bytes 786440 | tf_op jit(solution)/shard_map/ppermute | solution.py:282
  124.2 14.8 %collective-permute-start.38 = (bf16[256,256]{1,0:T(8,128)(2,1)S(1)}, bf16[256,256]{1,0:T(8,128)(2,1)S(1)}, u32[]{:S(2)}, u32[]{:S(2)}) collective-permute-start(bf16[256,256]{1,0:T(8,128)(2,1)S(1)} %shard_map.109), channel_id=1, source_target_pairs={{0,16},{4,20},{8,24},{12,28},{16,0},{20,4},{24,8},{28,12},{1,17},{... | collective-permute-start | bytes 393224 | tf_op jit(solution)/shard_map/ppermute | solution.py:282
  134.2 14.9 %collective-permute-start.34 = (bf16[256,256]{1,0:T(8,128)(2,1)S(1)}, bf16[256,256]{1,0:T(8,128)(2,1)S(1)}, u32[]{:S(2)}, u32[]{:S(2)}) collective-permute-start(bf16[256,256]{1,0:T(8,128)(2,1)S(1)} %shard_map.105), channel_id=1, source_target_pairs={{0,16},{4,20},{8,24},{12,28},{16,0},{20,4},{24,8},{28,12},{1,17},{... | collective-permute-start | bytes 393224 | tf_op jit(solution)/shard_map/ppermute | solution.py:282
  137.3 13.3 %collective-permute-start.18 = (bf16[512,128]{1,0:T(8,128)(2,1)S(1)}, bf16[512,128]{1,0:T(8,128)(2,1)S(1)}, u32[]{:S(2)}, u32[]{:S(2)}) collective-permute-start(bf16[512,128]{1,0:T(8,128)(2,1)S(1)} %shard_map.93), channel_id=1, source_target_pairs={{16,0},{20,4},{24,8},{28,12},{17,1},{21,5},{25,9},{29,13},{18,2},{... | collective-permute-start | bytes 393224 | tf_op jit(solution)/shard_map/ppermute | solution.py:300
  156.3 12.0 %collective-permute-start.39 = (bf16[256,512]{1,0:T(8,128)(2,1)S(1)}, bf16[256,512]{1,0:T(8,128)(2,1)S(1)}, u32[]{:S(2)}, u32[]{:S(2)}) collective-permute-start(bf16[256,512]{1,0:T(8,128)(2,1)S(1)} %shard_map.110.refs_0_), channel_id=1, source_target_pairs={{0,1},{1,0},{2,3},{3,2},{4,5},{5,4},{6,7},{7,6},{8,9},{9,8},{10,11... | collective-permute-start | bytes 786440 | tf_op jit(solution)/shard_map/ppermute | solution.py:279
  156.3 12.0 %collective-permute-start.41 = (bf16[256,512]{1,0:T(8,128)(2,1)S(1)}, bf16[256,512]{1,0:T(8,128)(2,1)S(1)}, u32[]{:S(2)}, u32[]{:S(2)}) collective-permute-start(bf16[256,512]{1,0:T(8,128)(2,1)S(1)} %collective-permute-done.40.refs_2_), channel_id=1, source_target_pairs={{0,1},{1,0},{2,3},{3,2},{4,5},{5,4},{6,7},{7,6},{8,9},{9,8},{10,11... | collective-permute-start | bytes 786440 | tf_op jit(solution)/shard_map/ppermute | solution.py:279
  (16 other events, 152.5 us)
